TPU v7x, 32 devices: a whole 2x2x4 slice. The times are simulated.
32 devices in a mesh: grp: 2 (over y), elem: 4 (over z), src: 2 (over x), sub: 2 (over core).
Axes of the slice: x: 2, y: 2, z: 4, core: 2. Of those that a mesh axis runs over, the one named last changes fastest.
Arguments:
- trace_rhs: bfloat16 [6144, 2048], P(('grp', 'elem', 'sub'), 'src'), parts along dimension 0, may hold values from -6 to 6
- face_scale: float32 [6144], P(('grp', 'elem', 'sub')), parts along dimension 0, may hold values from 0.5 to 2
- stiff_scale: float32 [2048], P(('grp', 'elem', 'sub')), parts along dimension 0, may hold values from 0.25 to 1
- mass_scale: float32 [2048], P(('grp', 'elem', 'sub')), parts along dimension 0, may hold values from 0.1 to 0.5
- elem_faces: int32 [2048, 6], P(('grp', 'elem', 'sub')), parts along dimension 0, may hold values from 0 to 479, as said below
- halo_faces: int32 [16, 3, 32], P(('grp', 'elem', 'sub')), parts along dimension 0, may hold values from 0 to 383
- elem_count: int32 [16], P(('grp', 'elem', 'sub')), parts along dimension 0, may hold values from 16 to 128, as said below
- jacobi_block: bfloat16 [64, 64], replicated, may hold values from -0.75 to 0.75
- stiffness: bfloat16 [384, 384], replicated, may hold values from -0.3125 to 0.3125
- mass: bfloat16 [384, 384], replicated, may hold values from -0.3125 to 0.3125
- lifting: bfloat16 [384, 512], replicated, may hold values from -0.3125 to 0.3125
Outputs:
- applied: bfloat16 [6144, 2048], P(('grp', 'elem', 'sub'), 'src'), parts along dimension 0
- interior: bfloat16 [2048, 16384], P(('grp', 'elem', 'sub'), 'src'), parts along dimension 0
There are 2 independent parts, one for each index of `grp`. A program takes and returns all parts, laid end to end along the dimension named above; an argument that names none is the same for every part. Nothing has to cross between parts.
Inputs may be any that keep to these rules, and one draw needn't show every extreme that they name: `elem_faces`: each element's six entries index owned faces of its own partition or halo slots toward neighbours that exist (partitions 0 to 7). `elem_count`: A multiple of 16; some partition is full in every draw.
All inputs are finite; a program needn't handle non-finite values.
Results may differ from a plain program's by a relative error of at most 0.0065.
Values may be sent and summed in bfloat16 or wider, within the bound.
No kernel may reach another device: no remote copies, remote signals or barrier semaphores. Data moves between devices by JAX's collectives and lax.ppermute only.
A program may use at most 64 MiB of HBM per device.

v0:
```python
import jax
import jax.numpy as jnp
from jax import lax
from jax.sharding import PartitionSpec as P


def with_halo(cells, sides, width):
    for axis, dim in sides:
        count = lax.axis_size(axis)
        ends = count - 1
        head = lax.slice_in_dim(cells, 0, width, axis=dim)
        tail = lax.slice_in_dim(cells, cells.shape[dim] - width, cells.shape[dim], axis=dim)
        cells = jnp.concatenate(
            [
                lax.ppermute(tail, axis, [(i, (i + 1) % count) for i in range(ends)]),
                cells,
                lax.ppermute(head, axis, [((i + 1) % count, i) for i in range(ends)]),
            ],
            axis=dim,
        )
    return cells


def shifted(array, axis, by):
    size = lax.axis_size(axis)
    return lax.ppermute(array, axis, [(i, (i + by) % size) for i in range(size)])


def precondition(traces, face_scale, jacobi_block):
    face_dofs = jacobi_block.shape[0]
    row_count = traces.shape[0]
    flattened = traces.reshape(-1, face_dofs)
    product = jnp.dot(flattened, jacobi_block, preferred_element_type=jnp.float32).reshape(
        row_count, -1
    )
    return (product * face_scale[:, None]).astype(jnp.bfloat16)


def neighbour_links():
    elem_size = lax.axis_size("elem")
    elem_pos = lax.axis_index("elem")
    opposite = (elem_pos + elem_size // 2) % elem_size
    targets = jnp.stack([elem_pos - 1, elem_pos + 1, opposite])
    present = jnp.stack([elem_pos > 0, elem_pos < elem_size - 1, elem_pos >= 0])
    return (targets, present, elem_size)


def spread_dense(outgoing, links):
    targets, present, slot_total = links
    placed = jnp.where(present, targets, slot_total)
    empty = jnp.zeros((slot_total,) + outgoing.shape[1:], outgoing.dtype)
    return empty.at[placed].set(outgoing, mode="drop")


def pick_dense(received, links):
    targets, present, slot_total = links
    rows = received[jnp.clip(targets, 0, slot_total - 1)]
    keep = present.reshape((3,) + (1,) * (rows.ndim - 1))
    return jnp.where(keep, rows, jnp.zeros_like(rows))


def forward_rows(outgoing):
    slot_count = outgoing.shape[1]
    sides = outgoing[:2].reshape(2 * slot_count, outgoing.shape[2])
    widened = with_halo(sides, (("elem", 0),), slot_count)
    opposite_rows = shifted(outgoing[2], "elem", lax.axis_size("elem") // 2)
    result = jnp.stack([widened[:slot_count], widened[3 * slot_count :], opposite_rows])
    return result


def return_sums(outgoing):
    slot_count = outgoing.shape[1]
    sides = outgoing[:2].reshape(2 * slot_count, outgoing.shape[2])
    widened = with_halo(sides, (("elem", 0),), slot_count)
    opposite_rows = shifted(outgoing[2], "elem", lax.axis_size("elem") // 2)
    result = jnp.stack([widened[:slot_count], widened[3 * slot_count :], opposite_rows])
    return result


def element_terms(
    extended, block_ids, stiff_part, mass_part, stiffness, mass, lifting, with_interior
):
    face_dofs = stiffness.shape[0] // 6
    elem_rows = block_ids.shape[0]
    row_width = extended.shape[1]
    src_count = row_width // face_dofs
    gathered = extended[block_ids.reshape(-1)].reshape(elem_rows, 6, src_count, face_dofs)
    stiff_term = jnp.einsum(
        "efsd,fdk->esk",
        gathered,
        stiffness.reshape(6, face_dofs, -1),
        preferred_element_type=jnp.float32,
    )
    mass_term = jnp.einsum(
        "efsd,fdk->esk",
        gathered,
        mass.reshape(6, face_dofs, -1),
        preferred_element_type=jnp.float32,
    )
    terms = stiff_part[:, None, None] * stiff_term - mass_part[:, None, None] * mass_term
    terms = (
        terms.reshape(elem_rows, src_count, 6, face_dofs)
        .transpose(0, 2, 1, 3)
        .reshape(elem_rows * 6, row_width)
    )
    interior_part = None
    if with_interior:
        interior_part = jnp.einsum(
            "efsd,fdi->esi",
            gathered,
            lifting.reshape(6, face_dofs, -1),
            preferred_element_type=jnp.float32,
        )
    return (terms, interior_part)


def apply_operator(
    traces,
    wanted,
    elem_faces,
    live_count,
    stiff_scale,
    mass_scale,
    stiffness,
    mass,
    lifting,
    with_interior,
):
    faces_here, row_width = traces.shape
    side_count, slot_count = wanted.shape
    face_dofs = stiffness.shape[0] // 6
    src_count = row_width // face_dofs
    interior_width = lifting.shape[1]
    elem_total = elem_faces.shape[0]
    outgoing = traces[wanted.reshape(-1)].reshape(side_count, slot_count, row_width)
    arrived = forward_rows(outgoing)
    extended = jnp.concatenate(
        [traces, arrived.reshape(side_count * slot_count, row_width)], axis=0
    )
    summed = jnp.zeros((faces_here + side_count * slot_count, row_width), jnp.float32)
    interior = jnp.zeros((elem_total, src_count * interior_width), jnp.bfloat16)
    alive_mask = (jnp.arange(elem_total) < live_count).astype(jnp.float32)
    terms, interior_part = element_terms(
        extended,
        elem_faces,
        stiff_scale * alive_mask,
        mass_scale * alive_mask,
        stiffness,
        mass,
        lifting,
        with_interior,
    )
    summed = summed.at[elem_faces.reshape(-1)].add(terms)
    if with_interior:
        interior = (
            (interior_part * alive_mask[:, None, None])
            .astype(jnp.bfloat16)
            .reshape(elem_total, src_count * interior_width)
        )
    returned = return_sums(summed[faces_here:].reshape(side_count, slot_count, row_width))
    owned = (
        summed[:faces_here]
        .at[wanted.reshape(-1)]
        .add(returned.reshape(side_count * slot_count, row_width))
    )
    return (owned, interior)


def per_device(
    trace_rhs,
    face_scale,
    stiff_scale,
    mass_scale,
    elem_faces,
    halo_faces,
    elem_count,
    jacobi_block,
    stiffness,
    mass,
    lifting,
):
    links = neighbour_links()
    requested = halo_faces.reshape(halo_faces.shape[1], halo_faces.shape[2])
    arrived_lists = lax.all_to_all(
        spread_dense(requested, links), "elem", split_axis=0, concat_axis=0, tiled=True
    )
    wanted = pick_dense(arrived_lists, links)
    live_count = elem_count[0]
    first = precondition(trace_rhs, face_scale, jacobi_block)
    summed, unused = apply_operator(
        first,
        wanted,
        elem_faces,
        live_count,
        stiff_scale,
        mass_scale,
        stiffness,
        mass,
        lifting,
        False,
    )
    second = precondition(summed.astype(jnp.bfloat16), face_scale, jacobi_block)
    applied, interior = apply_operator(
        second,
        wanted,
        elem_faces,
        live_count,
        stiff_scale,
        mass_scale,
        stiffness,
        mass,
        lifting,
        True,
    )
    return (applied.astype(jnp.bfloat16), interior)


def solution(mesh):
    in_specs = (
        P(("grp", "elem", "sub"), "src"),
        P(("grp", "elem", "sub")),
        P(("grp", "elem", "sub")),
        P(("grp", "elem", "sub")),
        P(("grp", "elem", "sub"), None),
        P(("grp", "elem", "sub"), None, None),
        P(("grp", "elem", "sub")),
        P(),
        P(),
        P(),
        P(),
    )
    out_specs = (P(("grp", "elem", "sub"), "src"), P(("grp", "elem", "sub"), "src"))
    return jax.shard_map(
        per_device, mesh=mesh, in_specs=in_specs, out_specs=out_specs, check_vma=False
    )
```

profile of v0, /device:TPU:0, one launch (start us, length us, event | category | flops | bytes accessed | tf_op | source)
XLA Modules:
  0.0 174.7 jit_solution(8501302903585435865)
XLA Ops:
  2.1 6.3 %all-to-all-start = ((s32[4,1,32]{2,1,0:T(1,128)}), s32[4,1,32]{2,1,0:T(1,128)S(1)}, u32[]{:S(2)}, u32[]{:S(2)}) async-start(s32[4,1,32]{2,1,0:T(1,128)} %bitcast.12), calls=%async_computation | async-start | bytes 4096 | tf_op jit(solution)/shard_map/all_to_all | solution.py:184
  8.4 3.2 %reshape.322 = bf16[6144,64]{1,0:T(8,128)(2,1)} reshape(bf16[384,1024]{1,0:T(8,128)(2,1)} %param.11) | data formatting | bytes 1572864 | tf_op jit(solution)/shard_map/reshape | solution.py:32
  20.2 3.9 %collective-permute-start = (bf16[32,1024]{1,0:T(8,128)(2,1)S(1)}, bf16[32,1024]{1,0:T(8,128)(2,1)S(1)}, u32[]{:S(2)}, u32[]{:S(2)}) collective-permute-start(bf16[32,1024]{1,0:T(8,128)(2,1)S(1)} %get-tuple-element.17), channel_id=1, source_target_pairs={{0,4},{4,8},{8,12},{1,5},{5,9},{9,13},{2,6},{6,10},{10,14},{3,7},{... | collective-permute-start | bytes 196616 | tf_op jit(solution)/shard_map/ppermute | solution.py:15
  25.6 3.6 %collective-permute-start.2 = (bf16[32,1024]{1,0:T(8,128)(2,1)S(1)}, bf16[32,1024]{1,0:T(8,128)(2,1)S(1)}, u32[]{:S(2)}, u32[]{:S(2)}) collective-permute-start(bf16[32,1024]{1,0:T(8,128)(2,1)S(1)} %get-tuple-element.19), channel_id=1, source_target_pairs={{0,8},{4,12},{8,0},{12,4},{1,9},{5,13},{9,1},{13,5},{2,10},{6,14},... | collective-permute-start | bytes 196616 | tf_op jit(solution)/shard_map/ppermute | solution.py:26
  35.2 3.3 %reshape.326 = bf16[128,6,16,64]{3,2,1,0:T(8,128)(2,1)} reshape(bf16[768,1024]{1,0:T(8,128)(2,1)S(1)} %gather_fusion.2) | data formatting | bytes 3145728 | tf_op jit(solution)/shard_map/reshape | solution.py:87
  38.5 4.5 %copy.37 = bf16[128,6,16,64]{0,3,1,2:T(8,128)(2,1)S(1)} copy(bf16[128,6,16,64]{3,2,1,0:T(8,128)(2,1)} %reshape.326) | data formatting | bytes 3145728 | tf_op jit(solution)/shard_map/reshape | solution.py:87
  44.3 2.9 %fusion.2 = f32[128,16,384]{2,0,1:T(8,128)} fusion(f32[128,16,384,1]{2,0,3,1:T(8,128)S(1)} %fusion.23, bf16[128,6,16,64]{0,3,1,2:T(8,128)(2,1)S(1)} %copy.37, bf16[6,64,384,1]{2,1,0,3:T(8,128)(2,1)S(1)} %bitcast.108, f32[128]{0:T(128)S(1)} %get-tuple-element.20, f32[128]{0:T(128)S(1)} %get-tuple-element.21), kind=kOutput, calls=%fused_computation.16 | convolution fusion | flops 606339072 | bytes 8160256 | tf_op jit(solution)/shard_map/efsd,fdk->esk/dot_general | solution.py:94
  49.5 6.2 %copy.40 = f32[128,6,16,64]{3,2,1,0:T(8,128)} copy(f32[128,6,16,64]{0,3,1,2:T(8,128)S(1)} %bitcast.101) | data formatting | bytes 6291456 | tf_op jit(solution)/shard_map/transpose | solution.py:103
  55.7 6.3 %reshape.393 = f32[768,1024]{1,0:T(8,128)} reshape(f32[128,6,16,64]{3,2,1,0:T(8,128)} %copy.40) | data formatting | bytes 6291456 | tf_op jit(solution)/shard_map/reshape | solution.py:104
  62.0 10.8 %scatter_custom_fusion.1 = f32[480,1024]{1,0:T(8,128)S(1)} fusion(s32[768]{0:T(1024)S(1)} %fusion.7, f32[768,1024]{1,0:T(8,128)} %reshape.393, f32[]{:T(128)} %constant.12.clone.1), kind=kCustom, calls=%fused_computation.24 | custom fusion | flops 786432 | bytes 1966592 | tf_op jit(solution)/shard_map/scatter-add | solution.py:153
  72.9 3.2 %collective-permute-start.3 = (f32[32,1024]{1,0:T(8,128)S(1)}, f32[32,1024]{1,0:T(8,128)S(1)}, u32[]{:S(2)}, u32[]{:S(2)}) collective-permute-start(f32[32,1024]{1,0:T(8,128)S(1)} %get-tuple-element.11), channel_id=1, source_target_pairs={{0,4},{4,8},{8,12},{1,5},{5,9},{9,13},{2,6},{6,10},{10,14},{3,7},{... | collective-permute-start | bytes 393224 | tf_op jit(solution)/shard_map/ppermute | solution.py:15
  77.6 3.7 %collective-permute-start.5 = (f32[32,1024]{1,0:T(8,128)S(1)}, f32[32,1024]{1,0:T(8,128)S(1)}, u32[]{:S(2)}, u32[]{:S(2)}) collective-permute-start(f32[32,1024]{1,0:T(8,128)S(1)} %get-tuple-element.12), channel_id=1, source_target_pairs={{0,8},{4,12},{8,0},{12,4},{1,9},{5,13},{9,1},{13,5},{2,10},{6,14},... | collective-permute-start | bytes 393224 | tf_op jit(solution)/shard_map/ppermute | solution.py:26
  83.2 4.6 %collective-permute-done.5 = f32[32,1024]{1,0:T(8,128)S(1)} collective-permute-done((f32[32,1024]{1,0:T(8,128)S(1)}, f32[32,1024]{1,0:T(8,128)S(1)}, u32[]{:S(2)}, u32[]{:S(2)}) %collective-permute-start.5) | collective-permute-done | bytes 131104 | tf_op jit(solution)/shard_map/ppermute | solution.py:26
  101.0 3.3 %collective-permute-start.8 = (bf16[32,1024]{1,0:T(8,128)(2,1)S(1)}, bf16[32,1024]{1,0:T(8,128)(2,1)S(1)}, u32[]{:S(2)}, u32[]{:S(2)}) collective-permute-start(bf16[32,1024]{1,0:T(8,128)(2,1)S(1)} %get-tuple-element.16), channel_id=1, source_target_pairs={{0,8},{4,12},{8,0},{12,4},{1,9},{5,13},{9,1},{13,5},{2,10},{6,14},... | collective-permute-start | bytes 196616 | tf_op jit(solution)/shard_map/ppermute | solution.py:26
  110.0 3.3 %reshape.335 = bf16[128,6,16,64]{3,2,1,0:T(8,128)(2,1)} reshape(bf16[768,1024]{1,0:T(8,128)(2,1)S(1)} %gather_fusion.4) | data formatting | bytes 3145728 | tf_op jit(solution)/shard_map/reshape | solution.py:87
  113.4 4.5 %copy.42 = bf16[128,6,16,64]{0,3,1,2:T(8,128)(2,1)S(1)} copy(bf16[128,6,16,64]{3,2,1,0:T(8,128)(2,1)} %reshape.335) | data formatting | bytes 3145728 | tf_op jit(solution)/shard_map/reshape | solution.py:87
  119.1 2.9 %fusion.1 = f32[128,16,384]{2,0,1:T(8,128)} fusion(f32[128,16,384,1]{2,0,3,1:T(8,128)S(1)} %fusion.25, bf16[128,6,16,64]{0,3,1,2:T(8,128)(2,1)S(1)} %copy.42, bf16[6,64,384,1]{2,1,0,3:T(8,128)(2,1)S(1)} %bitcast.109, f32[128]{0:T(128)S(1)} %copy-done.15, f32[128]{0:T(128)S(1)} %copy-done.17), kind=kOutput, calls=%fused_computation.13 | convolution fusion | flops 606339072 | bytes 8160256 | tf_op jit(solution)/shard_map/efsd,fdk->esk/dot_general | solution.py:94
  122.0 3.6 %copy.44 = f32[128,16,384]{0,2,1:T(8,128)} copy(f32[128,16,384]{2,0,1:T(8,128)} %fusion.1) | data formatting | bytes 6291456 | tf_op jit(solution)/shard_map/sub | solution.py:100
  125.6 7.7 %copy.45 = f32[128,6,16,64]{3,2,1,0:T(8,128)} copy(f32[128,6,16,64]{0,3,1,2:T(8,128)} %bitcast.102) | data formatting | bytes 6291456 | tf_op jit(solution)/shard_map/transpose | solution.py:103
  133.3 6.3 %reshape.409 = f32[768,1024]{1,0:T(8,128)} reshape(f32[128,6,16,64]{3,2,1,0:T(8,128)} %copy.45) | data formatting | bytes 6291456 | tf_op jit(solution)/shard_map/reshape | solution.py:104
  139.6 11.7 %scatter_custom_fusion.3 = f32[480,1024]{1,0:T(8,128)} fusion(s32[768]{0:T(1024)} %copy-done.10, f32[768,1024]{1,0:T(8,128)} %reshape.409, f32[]{:T(128)} %constant.12.clone.1), kind=kCustom, calls=%fused_computation.22 | custom fusion | flops 786432 | bytes 1966592 | tf_op jit(solution)/shard_map/scatter-add | solution.py:153
  152.3 3.9 %collective-permute-start.9 = (f32[32,1024]{1,0:T(8,128)S(1)}, f32[32,1024]{1,0:T(8,128)S(1)}, u32[]{:S(2)}, u32[]{:S(2)}) collective-permute-start(f32[32,1024]{1,0:T(8,128)S(1)} %get-tuple-element.8), channel_id=1, source_target_pairs={{0,4},{4,8},{8,12},{1,5},{5,9},{9,13},{2,6},{6,10},{10,14},{3,7},{... | collective-permute-start | bytes 393224 | tf_op jit(solution)/shard_map/ppermute | solution.py:15
  157.8 3.2 %collective-permute-start.11 = (f32[32,1024]{1,0:T(8,128)S(1)}, f32[32,1024]{1,0:T(8,128)S(1)}, u32[]{:S(2)}, u32[]{:S(2)}) collective-permute-start(f32[32,1024]{1,0:T(8,128)S(1)} %get-tuple-element.9), channel_id=1, source_target_pairs={{0,8},{4,12},{8,0},{12,4},{1,9},{5,13},{9,1},{13,5},{2,10},{6,14},... | collective-permute-start | bytes 393224 | tf_op jit(solution)/shard_map/ppermute | solution.py:26
  167.5 4.2 %copy.48 = bf16[128,8192]{1,0:T(8,128)(2,1)} copy(bf16[128,8192]{0,1:T(8,128)(2,1)} %bitcast.103) | data formatting | bytes 4194304
  (112 shorter events, 55.8 us)
Async XLA Ops:
  0.6 160.3 %copy-start = (bf16[384,512]{1,0:T(8,128)(2,1)S(1)}, bf16[384,512]{1,0:T(8,128)(2,1)}, u32[]{:S(2)}) copy-start(bf16[384,512]{1,0:T(8,128)(2,1)} %param.21) | copy-start | bytes 1179652
  2.1 16.0 %all-to-all-start = ((s32[4,1,32]{2,1,0:T(1,128)}), s32[4,1,32]{2,1,0:T(1,128)S(1)}, u32[]{:S(2)}, u32[]{:S(2)}) async-start(s32[4,1,32]{2,1,0:T(1,128)} %bitcast.12), calls=%async_computation | async-start | bytes 4096 | tf_op jit(solution)/shard_map/all_to_all | solution.py:184
  15.7 46.3 %copy-start.10 = (s32[768]{0:T(1024)}, s32[768]{0:T(1024)S(1)}, u32[]{:S(2)}) copy-start(s32[768]{0:T(1024)S(1)} %fusion.7) | copy-start | bytes 9220
  18.0 26.2 %copy-start.14 = (f32[128]{0:T(128)}, f32[128]{0:T(128)S(1)}, u32[]{:S(2)}) copy-start(f32[128]{0:T(128)S(1)} %get-tuple-element.20) | copy-start | bytes 1540
  18.0 26.2 %copy-start.16 = (f32[128]{0:T(128)}, f32[128]{0:T(128)S(1)}, u32[]{:S(2)}) copy-start(f32[128]{0:T(128)S(1)} %get-tuple-element.21) | copy-start | bytes 1540
  18.8 69.0 %copy-start.18 = (s32[96]{0:T(128)}, s32[96]{0:T(128)S(1)}, u32[]{:S(2)}) copy-start(s32[96]{0:T(128)S(1)} %fusion.14) | copy-start | bytes 1156
  20.2 9.0 %collective-permute-start = (bf16[32,1024]{1,0:T(8,128)(2,1)S(1)}, bf16[32,1024]{1,0:T(8,128)(2,1)S(1)}, u32[]{:S(2)}, u32[]{:S(2)}) collective-permute-start(bf16[32,1024]{1,0:T(8,128)(2,1)S(1)} %get-tuple-element.17), channel_id=1, source_target_pairs={{0,4},{4,8},{8,12},{1,5},{5,9},{9,13},{2,6},{6,10},{10,14},{3,7},{... | collective-permute-start | bytes 196616 | tf_op jit(solution)/shard_map/ppermute | solution.py:15
  24.2 6.5 %collective-permute-start.1 = (bf16[32,1024]{1,0:T(8,128)(2,1)S(1)}, bf16[32,1024]{1,0:T(8,128)(2,1)S(1)}, u32[]{:S(2)}, u32[]{:S(2)}) collective-permute-start(bf16[32,1024]{1,0:T(8,128)(2,1)S(1)} %get-tuple-element.18), channel_id=1, source_target_pairs={{4,0},{8,4},{12,8},{5,1},{9,5},{13,9},{6,2},{10,6},{14,10},{7,3},{... | collective-permute-start | bytes 196616 | tf_op jit(solution)/shard_map/ppermute | solution.py:17
  25.6 6.6 %collective-permute-start.2 = (bf16[32,1024]{1,0:T(8,128)(2,1)S(1)}, bf16[32,1024]{1,0:T(8,128)(2,1)S(1)}, u32[]{:S(2)}, u32[]{:S(2)}) collective-permute-start(bf16[32,1024]{1,0:T(8,128)(2,1)S(1)} %get-tuple-element.19), channel_id=1, source_target_pairs={{0,8},{4,12},{8,0},{12,4},{1,9},{5,13},{9,1},{13,5},{2,10},{6,14},... | collective-permute-start | bytes 196616 | tf_op jit(solution)/shard_map/ppermute | solution.py:26
  29.3 5.9 %copy-start.8 = (s32[1024]{0:T(1024)}, s32[1024]{0:T(1024)S(1)}, u32[]{:S(2)}) copy-start(s32[1024]{0:T(1024)S(1)} %pad_clamp_fusion) | copy-start | bytes 12292
  38.5 4.5 %copy-start.3 = (bf16[384,384]{1,0:T(8,128)(2,1)S(1)}, bf16[384,384]{1,0:T(8,128)(2,1)}, u32[]{:S(2)}) copy-start(bf16[384,384]{1,0:T(8,128)(2,1)} %param.19) | copy-start | bytes 884740
  72.8 4.7 %copy-start.2 = (f32[480,1024]{1,0:T(8,128)}, f32[480,1024]{1,0:T(8,128)S(1)}, u32[]{:S(2)}) copy-start(f32[480,1024]{1,0:T(8,128)S(1)} %scatter_custom_fusion.1) | copy-start | bytes 5898244
  72.9 10.0 %collective-permute-start.3 = (f32[32,1024]{1,0:T(8,128)S(1)}, f32[32,1024]{1,0:T(8,128)S(1)}, u32[]{:S(2)}, u32[]{:S(2)}) collective-permute-start(f32[32,1024]{1,0:T(8,128)S(1)} %get-tuple-element.11), channel_id=1, source_target_pairs={{0,4},{4,8},{8,12},{1,5},{5,9},{9,13},{2,6},{6,10},{10,14},{3,7},{... | collective-permute-start | bytes 393224 | tf_op jit(solution)/shard_map/ppermute | solution.py:15
  76.0 7.2 %collective-permute-start.4 = (f32[32,1024]{1,0:T(8,128)S(1)}, f32[32,1024]{1,0:T(8,128)S(1)}, u32[]{:S(2)}, u32[]{:S(2)}) collective-permute-start(f32[32,1024]{1,0:T(8,128)S(1)} %get-tuple-element.13), channel_id=1, source_target_pairs={{4,0},{8,4},{12,8},{5,1},{9,5},{13,9},{6,2},{10,6},{14,10},{7,3},{... | collective-permute-start | bytes 393224 | tf_op jit(solution)/shard_map/ppermute | solution.py:17
  77.6 10.2 %collective-permute-start.5 = (f32[32,1024]{1,0:T(8,128)S(1)}, f32[32,1024]{1,0:T(8,128)S(1)}, u32[]{:S(2)}, u32[]{:S(2)}) collective-permute-start(f32[32,1024]{1,0:T(8,128)S(1)} %get-tuple-element.12), channel_id=1, source_target_pairs={{0,8},{4,12},{8,0},{12,4},{1,9},{5,13},{9,1},{13,5},{2,10},{6,14},... | collective-permute-start | bytes 393224 | tf_op jit(solution)/shard_map/ppermute | solution.py:26
  97.1 10.1 %copy-start.9 = (s32[1024]{0:T(1024)S(1)}, s32[1024]{0:T(1024)}, u32[]{:S(2)}) copy-start(s32[1024]{0:T(1024)} %copy-done.8) | copy-start | bytes 12292
  98.1 6.2 %collective-permute-start.6 = (bf16[32,1024]{1,0:T(8,128)(2,1)S(1)}, bf16[32,1024]{1,0:T(8,128)(2,1)S(1)}, u32[]{:S(2)}, u32[]{:S(2)}) collective-permute-start(bf16[32,1024]{1,0:T(8,128)(2,1)S(1)} %get-tuple-element.14), channel_id=1, source_target_pairs={{0,4},{4,8},{8,12},{1,5},{5,9},{9,13},{2,6},{6,10},{10,14},{3,7},{... | collective-permute-start | bytes 196616 | tf_op jit(solution)/shard_map/ppermute | solution.py:15
  99.7 6.2 %collective-permute-start.7 = (bf16[32,1024]{1,0:T(8,128)(2,1)S(1)}, bf16[32,1024]{1,0:T(8,128)(2,1)S(1)}, u32[]{:S(2)}, u32[]{:S(2)}) collective-permute-start(bf16[32,1024]{1,0:T(8,128)(2,1)S(1)} %get-tuple-element.15), channel_id=1, source_target_pairs={{4,0},{8,4},{12,8},{5,1},{9,5},{13,9},{6,2},{10,6},{14,10},{7,3},{... | collective-permute-start | bytes 196616 | tf_op jit(solution)/shard_map/ppermute | solution.py:17
  101.0 6.1 %collective-permute-start.8 = (bf16[32,1024]{1,0:T(8,128)(2,1)S(1)}, bf16[32,1024]{1,0:T(8,128)(2,1)S(1)}, u32[]{:S(2)}, u32[]{:S(2)}) collective-permute-start(bf16[32,1024]{1,0:T(8,128)(2,1)S(1)} %get-tuple-element.16), channel_id=1, source_target_pairs={{0,8},{4,12},{8,0},{12,4},{1,9},{5,13},{9,1},{13,5},{2,10},{6,14},... | collective-permute-start | bytes 196616 | tf_op jit(solution)/shard_map/ppermute | solution.py:26
  113.4 4.5 %copy-start.4 = (bf16[384,384]{1,0:T(8,128)(2,1)S(1)}, bf16[384,384]{1,0:T(8,128)(2,1)}, u32[]{:S(2)}) copy-start(bf16[384,384]{1,0:T(8,128)(2,1)} %param.19) | copy-start | bytes 884740
  152.3 19.4 %collective-permute-start.9 = (f32[32,1024]{1,0:T(8,128)S(1)}, f32[32,1024]{1,0:T(8,128)S(1)}, u32[]{:S(2)}, u32[]{:S(2)}) collective-permute-start(f32[32,1024]{1,0:T(8,128)S(1)} %get-tuple-element.8), channel_id=1, source_target_pairs={{0,4},{4,8},{8,12},{1,5},{5,9},{9,13},{2,6},{6,10},{10,14},{3,7},{... | collective-permute-start | bytes 393224 | tf_op jit(solution)/shard_map/ppermute | solution.py:15
  156.2 15.5 %collective-permute-start.10 = (f32[32,1024]{1,0:T(8,128)S(1)}, f32[32,1024]{1,0:T(8,128)S(1)}, u32[]{:S(2)}, u32[]{:S(2)}) collective-permute-start(f32[32,1024]{1,0:T(8,128)S(1)} %get-tuple-element.10), channel_id=1, source_target_pairs={{4,0},{8,4},{12,8},{5,1},{9,5},{13,9},{6,2},{10,6},{14,10},{7,3},{... | collective-permute-start | bytes 393224 | tf_op jit(solution)/shard_map/ppermute | solution.py:17
  157.8 13.9 %collective-permute-start.11 = (f32[32,1024]{1,0:T(8,128)S(1)}, f32[32,1024]{1,0:T(8,128)S(1)}, u32[]{:S(2)}, u32[]{:S(2)}) collective-permute-start(f32[32,1024]{1,0:T(8,128)S(1)} %get-tuple-element.9), channel_id=1, source_target_pairs={{0,8},{4,12},{8,0},{12,4},{1,9},{5,13},{9,1},{13,5},{2,10},{6,14},... | collective-permute-start | bytes 393224 | tf_op jit(solution)/shard_map/ppermute | solution.py:26
  167.5 4.2 %copy-start.19 = (s32[96]{0:T(128)S(1)}, s32[96]{0:T(128)}, u32[]{:S(2)}) copy-start(s32[96]{0:T(128)} %copy-done.18) | copy-start | bytes 1156
  (13 other events, 24.7 us)
where the time goes:
time: 176 us; the launch traced here: 175 us
  local copies, waits for them, and re-layouts  77.8 us (44%)
  starting transfers between devices  38.6 us (22%)
  other arithmetic  31.1 us (18%)
  matrix products  14.6 us (8%)
  waiting for transfers between devices  10.8 us (6%)
  between operations  1.86 us (1%)
    scatter-add x2, other arithmetic, apply_operator(): summed = summed.at[elem_faces.reshape(-1)].add(terms)  22.4 us
    reshape x4, local copies, waits for them, and re-layouts, element_terms(): extended[block_ids.reshape(-1)].reshape(elem_rows, 6, src_count, face_dofs)  15.6 us
    transpose x2, local copies, waits for them, and re-layouts, element_terms(): terms = terms.reshape(elem_rows, src_count, 6, face_dofs).transpose(0, 2,...  13.9 us
    ppermute x4, starting transfers between devices, shifted(): lax.ppermute(array, axis, [(i, (i + by) % size) for i in range(size)])  13.8 us
    reshape x2, local copies, waits for them, and re-layouts, element_terms(): terms = terms.reshape(elem_rows, src_count, 6, face_dofs).transpose(0, 2,...  12.6 us
    ppermute x4, starting transfers between devices, with_halo(): lax.ppermute(tail, axis, [(i, (i + 1) % count) for i in range(ends)])  12.6 us
    ppermute x4, waiting for transfers between devices, shifted(): lax.ppermute(array, axis, [(i, (i + by) % size) for i in range(size)])  7.46 us
    unnamed x48, local copies, waits for them, and re-layouts  6.57 us
  transfers between devices with their start and end apart: 13, of which 6 were waited for; matrix products, arithmetic and copies ran while one was open for 11% of the time, Pallas kernels for 0%

commit v1 on v0

v1 whole, which is shorter than its diff:
```python
import functools

import jax
import jax.numpy as jnp
from jax import lax
from jax.experimental import pallas as pl
from jax.experimental.pallas import tpu as pltpu
from jax.sharding import PartitionSpec as P

F32 = jnp.float32
BF16 = jnp.bfloat16
I32 = jnp.int32
LANES = 128
VMEM = pltpu.VMEM
SMEM = pltpu.SMEM


def iota(shape, dim):
    return lax.broadcasted_iota(I32, shape, dim)


def one_hot(condition):
    return jnp.where(condition, 1.0, 0.0).astype(BF16)


def matmul(a, b):
    return jnp.dot(a, b, preferred_element_type=F32)


def column_tiles(row):
    count = row.shape[1] // LANES
    return [
        jnp.transpose(
            jnp.broadcast_to(row[:, t * LANES : (t + 1) * LANES].astype(F32), (LANES, LANES))
        )
        for t in range(count)
    ]


def block_diagonal(block, copies):
    rows, cols = block.shape
    wide = jnp.concatenate([block] * copies, axis=1)
    full = jnp.concatenate([wide] * copies, axis=0)
    shape = (rows * copies, cols * copies)
    keep = (iota(shape, 0) // rows) == (iota(shape, 1) // cols)
    return jnp.where(keep, full, jnp.zeros_like(full))


def precondition(traces_ref, scale_ref, jacobi_ref, z_ref):
    rows, width = traces_ref.shape
    block = block_diagonal(jacobi_ref[...].astype(F32), 4).astype(BF16)
    scales = column_tiles(scale_ref[...])
    step = block.shape[0]
    for start in range(0, width, step):
        product = matmul(traces_ref[:, start : start + step], block)
        for t, scale in enumerate(scales):
            part = product[t * LANES : (t + 1) * LANES, :]
            both = jnp.concatenate([scale, scale], axis=1)
            z_ref[t * LANES : (t + 1) * LANES, start : start + step] = (part * both).astype(BF16)


def wanted_row(wanted_refs):
    row = jnp.concatenate([ref[...] for ref in wanted_refs], axis=1)
    pad = jnp.full((1, LANES - row.shape[1]), -1, I32)
    return jnp.concatenate([row, pad], axis=1)


def send_rows(wanted, z_ref, out_refs):
    faces = z_ref.shape[0]
    (column,) = column_tiles(wanted)
    column = column.astype(I32)
    lane = iota((LANES, LANES), 1)
    picks = jnp.concatenate(
        [one_hot(column == lane + t * LANES) for t in range(faces // LANES)], axis=1
    )
    rows = matmul(picks, z_ref[...]).astype(BF16)
    slots = out_refs[0].shape[0]
    for c, out_ref in enumerate(out_refs):
        out_ref[...] = rows[c * slots : (c + 1) * slots, :]


def first_kernel(rhs_ref, scale_ref, jacobi_ref, wa_ref, wb_ref, wc_ref, z_ref, *out_refs):
    precondition(rhs_ref, scale_ref, jacobi_ref, z_ref)
    send_rows(wanted_row([wa_ref, wb_ref, wc_ref]), z_ref, out_refs)


def paired_weight(src_ref, dst_ref, offset, face_dofs):
    rows, cols = src_ref.shape
    low = iota((face_dofs, LANES), 1) < face_dofs
    zero = jnp.zeros((face_dofs, LANES), F32)
    for k in range(rows // face_dofs):
        top = k * 2 * face_dofs
        for t in range(cols // LANES):
            tile = src_ref[k * face_dofs : (k + 1) * face_dofs, t * LANES : (t + 1) * LANES]
            tile = tile.astype(F32)
            turned = pltpu.roll(tile, face_dofs, 1)
            at = offset + 2 * t * LANES
            pieces = (
                (0, 0, jnp.where(low, tile, zero)),
                (1, 0, jnp.where(low, zero, turned)),
                (0, 1, jnp.where(low, turned, zero)),
                (1, 1, jnp.where(low, zero, tile)),
            )
            for half, odd, piece in pieces:
                dst_ref[
                    top + half * face_dofs : top + (half + 1) * face_dofs,
                    at + odd * LANES : at + (odd + 1) * LANES,
                ] = piece.astype(BF16)


def column_ids(par, faces, slots, tile, axis):
    index = iota((LANES, LANES), axis) + tile * LANES
    shift = slots * (1 - par)
    first = (index >= faces) & (index < faces + slots)
    second = (index >= faces + slots) & (index < faces + 2 * slots)
    return index + jnp.where(first, shift, 0) - jnp.where(second, shift, 0)


def gather_elements(faces_col, z_ref, arrived_refs, par, ext_ref, x_ref):
    faces, width = z_ref.shape
    slots = arrived_refs[0].shape[0]
    ext_ref[:faces, :] = z_ref[...]
    for c, ref in enumerate(arrived_refs):
        ext_ref[faces + c * slots : faces + (c + 1) * slots, :] = ref[...]
    filled = faces + 3 * slots
    ext_ref[filled:, :] = jnp.zeros((ext_ref.shape[0] - filled, width), BF16)
    tiles = ext_ref.shape[0] // LANES
    ids = [column_ids(par, faces, slots, t, 1) for t in range(tiles)]
    for k in range(6):
        mine = jnp.broadcast_to(faces_col[:, k : k + 1], (LANES, LANES))
        picks = jnp.concatenate([one_hot(mine == i) for i in ids], axis=1)
        rows = matmul(picks, ext_ref[...]).astype(BF16)
        for p in range(width // LANES):
            x_ref[p * LANES : (p + 1) * LANES, k * LANES : (k + 1) * LANES] = rows[
                :, p * LANES : (p + 1) * LANES
            ]


def element_terms(x_ref, w_ref, stiff_scale, mass_scale, y_ref):
    half = w_ref.shape[1] // 2
    stiff = jnp.concatenate([stiff_scale] * 6, axis=1)
    mass = jnp.concatenate([mass_scale] * 6, axis=1)
    rows = 2 * LANES
    for start in range(0, x_ref.shape[0], rows):
        product = matmul(x_ref[start : start + rows, :], w_ref[...])
        for r in range(rows // LANES):
            p = start // LANES + r
            part = product[r * LANES : (r + 1) * LANES, :]
            term = (stiff * part[:, :half] - mass * part[:, half:]).astype(BF16)
            for k in range(6):
                y_ref[k * LANES : (k + 1) * LANES, p * LANES : (p + 1) * LANES] = term[
                    :, k * LANES : (k + 1) * LANES
                ]


def scatter_elements(faces_col, par, y_ref, own_ref, back_refs, tiles):
    faces = own_ref.shape[0]
    slots = back_refs[0].shape[0]
    lane = iota((LANES, LANES), 1)
    spread = jnp.zeros((LANES, LANES), F32)
    for k in range(6):
        spread = jnp.where(lane == k, faces_col[:, k : k + 1].astype(F32), spread)
    turned = jnp.transpose(spread).astype(I32)
    order = list(range(faces // LANES, tiles)) + list(range(faces // LANES))
    for t in order:
        ids = column_ids(par, faces, slots, t, 0)
        picks = jnp.concatenate(
            [one_hot(ids == jnp.broadcast_to(turned[k : k + 1, :], (LANES, LANES))) for k in range(6)],
            axis=1,
        )
        rows = matmul(picks, y_ref[...])
        if t < faces // LANES:
            own_ref[t * LANES : (t + 1) * LANES, :] = rows
        else:
            for c, ref in enumerate(back_refs):
                ref[...] = rows[c * slots : (c + 1) * slots, :].astype(BF16)


def operator_kernel(
    with_interior,
    count_ref,
    par_ref,
    z_ref,
    aa_ref,
    ab_ref,
    ac_ref,
    faces_ref,
    stiff_scale_ref,
    mass_scale_ref,
    w_ref,
    *rest,
):
    if with_interior:
        lift_ref, own_ref, ba_ref, bb_ref, bc_ref, interior_ref, ext_ref, x_ref, y_ref = rest
    else:
        own_ref, ba_ref, bb_ref, bc_ref, ext_ref, x_ref, y_ref = rest
    par = par_ref[0]
    faces_col = faces_ref[...]
    alive = iota(faces_col.shape, 0) < count_ref[0]
    faces_col = jnp.where(alive, faces_col, -1)
    gather_elements(faces_col, z_ref, [aa_ref, ab_ref, ac_ref], par, ext_ref, x_ref)
    (stiff_scale,) = column_tiles(stiff_scale_ref[...])
    (mass_scale,) = column_tiles(mass_scale_ref[...])
    element_terms(x_ref, w_ref, stiff_scale, mass_scale, y_ref)
    scatter_elements(
        faces_col, par, y_ref, own_ref, [ba_ref, bb_ref, bc_ref], ext_ref.shape[0] // LANES
    )
    if with_interior:
        wide = lift_ref.shape[1]
        rows = 2 * LANES
        for start in range(0, x_ref.shape[0], rows):
            product = matmul(x_ref[start : start + rows, :], lift_ref[...]).astype(BF16)
            for r in range(rows // LANES):
                p = start // LANES + r
                interior_ref[:, p * wide : (p + 1) * wide] = product[
                    r * LANES : (r + 1) * LANES, :
                ]


def collect(own_ref, back_refs, wanted, gathered_ref):
    slots, width = back_refs[0].shape
    for c, ref in enumerate(back_refs):
        gathered_ref[c * slots : (c + 1) * slots, :] = ref[...]
    gathered_ref[3 * slots :, :] = jnp.zeros((LANES - 3 * slots, width), BF16)
    faces = own_ref.shape[0]
    target = jnp.broadcast_to(wanted, (faces, LANES))
    picks = one_hot(target == iota((faces, LANES), 0))
    return (own_ref[...] + matmul(picks, gathered_ref[...])).astype(BF16)


def middle_kernel(
    own_ref, ba_ref, bb_ref, bc_ref, wa_ref, wb_ref, wc_ref, scale_ref, jacobi_ref, z_ref,
    oa_ref, ob_ref, oc_ref, gathered_ref, v_ref
):
    wanted = wanted_row([wa_ref, wb_ref, wc_ref])
    v_ref[...] = collect(own_ref, [ba_ref, bb_ref, bc_ref], wanted, gathered_ref)
    precondition(v_ref, scale_ref, jacobi_ref, z_ref)
    send_rows(wanted, z_ref, [oa_ref, ob_ref, oc_ref])


def last_kernel(own_ref, ba_ref, bb_ref, bc_ref, wa_ref, wb_ref, wc_ref, out_ref, gathered_ref):
    wanted = wanted_row([wa_ref, wb_ref, wc_ref])
    out_ref[...] = collect(own_ref, [ba_ref, bb_ref, bc_ref], wanted, gathered_ref)


def weights_kernel(face_dofs, stiff_ref, mass_ref, lift_ref, w_ref, lift_out_ref):
    paired_weight(stiff_ref, w_ref, 0, face_dofs)
    paired_weight(mass_ref, w_ref, w_ref.shape[1] // 2, face_dofs)
    rows, inside = lift_ref.shape
    zero = jnp.zeros((face_dofs, inside), BF16)
    for k in range(rows // face_dofs):
        part = lift_ref[k * face_dofs : (k + 1) * face_dofs, :]
        top = 2 * k * face_dofs
        lift_out_ref[top : top + face_dofs, :inside] = part
        lift_out_ref[top : top + face_dofs, inside:] = zero
        lift_out_ref[top + face_dofs : top + 2 * face_dofs, :inside] = zero
        lift_out_ref[top + face_dofs : top + 2 * face_dofs, inside:] = part


def call(kernel, operands, scalars, outs, scratch, flops, name):
    specs = [pl.BlockSpec(memory_space=SMEM)] * len(scalars) + [
        pl.BlockSpec(memory_space=VMEM)
    ] * len(operands)
    moved = sum(a.size * a.dtype.itemsize for a in operands)
    return pl.pallas_call(
        kernel,
        out_shape=[jax.ShapeDtypeStruct(s, d) for s, d in outs],
        in_specs=specs,
        out_specs=[pl.BlockSpec(memory_space=VMEM)] * len(outs),
        scratch_shapes=[VMEM(s, d) for s, d in scratch],
        compiler_params=pltpu.CompilerParams(vmem_limit_bytes=32 * 1024 * 1024),
        cost_estimate=pl.CostEstimate(flops=flops, bytes_accessed=moved, transcendentals=0),
        name=name,
    )(*scalars, *operands)


def pairings(size):
    def both(pairs):
        return [pair for a, b in pairs for pair in ((a, b), (b, a))]

    even = both([(i, i + 1) for i in range(0, size - 1, 2)])
    odd = both([(i, i + 1) for i in range(1, size - 1, 2)])
    opposite = [(i, (i + size // 2) % size) for i in range(size)]
    return (even, odd, opposite)


def exchange(arrays, size):
    return [lax.ppermute(a, "elem", p) for a, p in zip(arrays, pairings(size))]


def per_device(
    size,
    trace_rhs,
    face_scale,
    stiff_scale,
    mass_scale,
    elem_faces,
    halo_faces,
    elem_count,
    jacobi_block,
    stiffness,
    mass,
    lifting,
):
    faces, width = trace_rhs.shape
    slots = halo_faces.shape[2]
    elems = elem_faces.shape[0]
    face_dofs = jacobi_block.shape[0]
    eld, inside = lifting.shape
    pairs = width // LANES
    ext_rows = -(-(faces + 3 * slots) // LANES) * LANES
    par = lax.axis_index("elem") % 2
    even = par == 0
    lists = [
        jnp.where(even, halo_faces[:, 1, :], halo_faces[:, 0, :]),
        jnp.where(even, halo_faces[:, 0, :], halo_faces[:, 1, :]),
        halo_faces[:, 2, :],
    ]
    par = par.astype(I32).reshape(1)
    wanted = exchange(lists, size)
    scale = face_scale.reshape(1, faces)
    stiff_row = stiff_scale.reshape(1, elems)
    mass_row = mass_scale.reshape(1, elems)
    paired, lift = call(
        functools.partial(weights_kernel, face_dofs),
        [stiffness, mass, lifting],
        [],
        [((2 * eld, 4 * eld), BF16), ((2 * eld, 2 * inside), BF16)],
        [],
        10_000_000,
        "weights",
    )
    field = ((faces, width), BF16)
    rows = [((slots, width), BF16)] * 3
    first, *outgoing = call(
        first_kernel,
        [trace_rhs, scale, jacobi_block, *wanted],
        [],
        [field, *rows],
        [],
        2 * faces * width * 256,
        "first",
    )
    arrived = exchange(outgoing, size)
    scratch = [
        ((ext_rows, width), BF16),
        ((pairs * elems, 6 * LANES), BF16),
        ((6 * elems, width), BF16),
    ]
    own_shape = ((faces, width), F32)
    own, *back = call(
        functools.partial(operator_kernel, False),
        [first, *arrived, elem_faces, stiff_row, mass_row, paired],
        [elem_count, par],
        [own_shape, *rows],
        scratch,
        4 * pairs * elems * 768 * 768,
        "operator",
    )
    returned = exchange(back, size)
    second, *outgoing = call(
        middle_kernel,
        [own, *returned, *wanted, scale, jacobi_block],
        [],
        [field, *rows],
        [((LANES, width), BF16), ((faces, width), BF16)],
        2 * faces * width * 256,
        "middle",
    )
    arrived = exchange(outgoing, size)
    own, b0, b1, b2, interior = call(
        functools.partial(operator_kernel, True),
        [second, *arrived, elem_faces, stiff_row, mass_row, paired, lift],
        [elem_count, par],
        [own_shape, *rows, ((elems, width // face_dofs * inside), BF16)],
        scratch,
        4 * pairs * elems * 768 * 768,
        "operator_interior",
    )
    returned = exchange([b0, b1, b2], size)
    (applied,) = call(
        last_kernel,
        [own, *returned, *wanted],
        [],
        [field],
        [((LANES, width), BF16)],
        2 * faces * width * 128,
        "last",
    )
    return (applied, interior)


def solution(mesh):
    rows = P(("grp", "elem", "sub"))
    split = P(("grp", "elem", "sub"), "src")
    in_specs = (
        split,
        rows,
        rows,
        rows,
        P(("grp", "elem", "sub"), None),
        P(("grp", "elem", "sub"), None, None),
        rows,
        P(),
        P(),
        P(),
        P(),
    )
    return jax.shard_map(
        functools.partial(per_device, mesh.shape["elem"]),
        mesh=mesh,
        in_specs=in_specs,
        out_specs=(split, split),
        check_vma=False,
    )
```

time: 176 us -> 65 us (0.37)
  local copies, waits for them, and re-layouts: 77.8 us -> 6.26 us
  other arithmetic: 31.1 us -> 0.69 us
  Pallas kernels: 0 us -> 15.3 us
  matrix products: 14.6 us -> 0 us
  starting transfers between devices: 38.6 us -> 31.6 us
    reshape x11 -> x1, local copies, waits for them, and re-layouts: 37.1 us -> 0.68 us  [per_device(): scale = face_scale.reshape(1, faces)]
    scatter-add x4 -> x0, other arithmetic: 26.3 us -> none  [the longest x2 22.4 us: apply_operator(): summed = summed.at[elem_faces.reshape(-1)].add(terms)]
    pallas_call x0 -> x6, Pallas kernels: none -> 15.3 us  [call(): pl.pallas_call(kernel, out_shape=[jax.ShapeDtypeStruct(s, d) for s, d in...]
    dot_general x7 -> x0, matrix products: 14.6 us -> none  [the longest x2 5.76 us: element_terms(): jnp.einsum('efsd,fdk->esk', gathered, mass.reshape(6, face_dofs, -1), pre...]
    transpose x2 -> x0, local copies, waits for them, and re-layouts: 13.9 us -> none  [element_terms(): terms = terms.reshape(elem_rows, src_count, 6, face_dofs).transpose(0, 2,...]
    gather x5 -> x0, local copies, waits for them, and re-layouts: 7.87 us -> none  [the longest x2 5.62 us: element_terms(): extended[block_ids.reshape(-1)].reshape(elem_rows, 6, src_count, face_dofs)]
    all_to_all x1 -> x0, starting transfers between devices: 6.32 us -> none  [per_device(): lax.all_to_all(spread_dense(requested, links), 'elem', split_axis=0, conc...]
    sub x2 -> x0, local copies, waits for them, and re-layouts: 5.97 us -> none  [element_terms(): stiff_part[:, None, None] * stiff_term]
  transfers between devices with their start and end apart: 13 -> 15, of which waited for: 6 -> 4; matrix products, arithmetic and copies ran while one was open for 11% -> 2% of each run, Pallas kernels for 0% -> 1%
where the time goes in v1:
time: 65 us; the launch traced here: 64.5 us
  starting transfers between devices  31.6 us (49%)
  Pallas kernels  15.3 us (24%)
  waiting for transfers between devices  9.22 us (14%)
  local copies, waits for them, and re-layouts  6.26 us (10%)
  between operations  1.45 us (2%)
  other arithmetic  0.69 us (1%)
    ppermute x15, starting transfers between devices, exchange(): return [lax.ppermute(a, 'elem', p) for a, p in zip(arrays, pairings(size))]  31.6 us
    pallas_call x6, Pallas kernels, call(): pl.pallas_call(kernel, out_shape=[jax.ShapeDtypeStruct(s, d) for s, d in...  15.3 us
    ppermute x15, waiting for transfers between devices, exchange(): return [lax.ppermute(a, 'elem', p) for a, p in zip(arrays, pairings(size))]  9.22 us
    unnamed x17, local copies, waits for them, and re-layouts  5.57 us
  transfers between devices with their start and end apart: 15, of which 4 were waited for; matrix products, arithmetic and copies ran while one was open for 2% of the time, Pallas kernels for 1%

profile of v1, /device:TPU:0, one launch (start us, length us, event | category | flops | bytes accessed | tf_op | source)
XLA Modules:
  0.0 64.5 jit_solution(11188189970510850820)
XLA Ops:
  1.4 4.0 %collective-permute-start.2 = (s32[1,32]{1,0:T(1,128)S(1)}, s32[1,32]{1,0:T(1,128)S(1)}, u32[]{:S(2)}, u32[]{:S(2)}) collective-permute-start(s32[1,32]{1,0:T(1,128)S(1)} %get-tuple-element.40), channel_id=1, source_target_pairs={{0,8},{4,12},{8,0},{12,4},{1,9},{5,13},{9,1},{13,5},{2,10},{6,14},... | collective-permute-start | bytes 392 | tf_op jit(solution)/shard_map/ppermute | solution.py:288
  6.1 2.9 %collective-permute-start = (s32[1,32]{1,0:T(1,128)S(1)}, s32[1,32]{1,0:T(1,128)S(1)}, u32[]{:S(2)}, u32[]{:S(2)}) collective-permute-start(s32[1,32]{1,0:T(1,128)S(1)} %get-tuple-element.42), channel_id=1, source_target_pairs={{0,4},{4,0},{8,12},{12,8},{1,5},{5,1},{9,13},{13,9},{2,6},{6,2},{1... | collective-permute-start | bytes 392 | tf_op jit(solution)/shard_map/ppermute | solution.py:288
  9.6 0.8 %collective-permute-done.wa_ref = s32[1,32]{1,0:T(1,128)S(1)} collective-permute-done((s32[1,32]{1,0:T(1,128)S(1)}, s32[1,32]{1,0:T(1,128)S(1)}, u32[]{:S(2)}, u32[]{:S(2)}) %collective-permute-start) | collective-permute-done | bytes 160 | tf_op jit(solution)/shard_map/ppermute | solution.py:288
  10.5 1.1 %copy-done = bf16[384,1024]{1,0:T(8,128)(2,1)S(1)} copy-done((bf16[384,1024]{1,0:T(8,128)(2,1)S(1)}, bf16[384,1024]{1,0:T(8,128)(2,1)}, u32[]{:S(2)}) %copy-start) | copy-done | bytes 786456
  12.9 2.1 %collective-permute-start.3 = (bf16[32,1024]{1,0:T(8,128)(2,1)S(1)}, bf16[32,1024]{1,0:T(8,128)(2,1)S(1)}, u32[]{:S(2)}, u32[]{:S(2)}) collective-permute-start(bf16[32,1024]{1,0:T(8,128)(2,1)S(1)} %get-tuple-element.22), channel_id=1, source_target_pairs={{0,4},{4,0},{8,12},{12,8},{1,5},{5,1},{9,13},{13,9},{2,6},{6,2},{1... | collective-permute-start | bytes 196616 | tf_op jit(solution)/shard_map/ppermute | solution.py:288
  15.7 2.8 %collective-permute-start.5 = (bf16[32,1024]{1,0:T(8,128)(2,1)S(1)}, bf16[32,1024]{1,0:T(8,128)(2,1)S(1)}, u32[]{:S(2)}, u32[]{:S(2)}) collective-permute-start(bf16[32,1024]{1,0:T(8,128)(2,1)S(1)} %get-tuple-element.24), channel_id=1, source_target_pairs={{0,8},{4,12},{8,0},{12,4},{1,9},{5,13},{9,1},{13,5},{2,10},{6,14},... | collective-permute-start | bytes 196616 | tf_op jit(solution)/shard_map/ppermute | solution.py:288
  19.1 0.8 %copy.13.faces_ref = s32[128,6]{1,0:T(8,128)S(1)} copy(s32[128,6]{0,1:T(8,128)} %param.15) | data formatting | bytes 6144 | tf_op args[4]
  19.9 1.0 %copy-done.1 = bf16[384,512]{1,0:T(8,128)(2,1)S(1)} copy-done((bf16[384,512]{1,0:T(8,128)(2,1)S(1)}, bf16[384,512]{1,0:T(8,128)(2,1)}, u32[]{:S(2)}) %copy-start.1) | copy-done | bytes 393240
  20.9 1.0 %copy-done.2 = bf16[384,384]{1,0:T(8,128)(2,1)S(1)} copy-done((bf16[384,384]{1,0:T(8,128)(2,1)S(1)}, bf16[384,384]{1,0:T(8,128)(2,1)}, u32[]{:S(2)}) %copy-start.2) | copy-done | bytes 294936
  21.9 1.0 %copy-done.3 = bf16[384,384]{1,0:T(8,128)(2,1)S(1)} copy-done((bf16[384,384]{1,0:T(8,128)(2,1)S(1)}, bf16[384,384]{1,0:T(8,128)(2,1)}, u32[]{:S(2)}) %copy-start.3) | copy-done | bytes 294936
  23.4 4.5 %operator.1 = (f32[384,1024]{1,0:T(8,128)S(1)}, bf16[32,1024]{1,0:T(8,128)(2,1)S(1)}, bf16[32,1024]{1,0:T(8,128)(2,1)S(1)}, bf16[32,1024]{1,0:T(8,128)(2,1)S(1)}) custom-call(s32[1]{0:T(128)S(6)} %copy.15.count_ref, s32[1]{0:T(128)} %bitcast.par_ref, bf16[384,1024]{1,0:T(8,128)(2,1)S(1)} %get-tuple-element.21.z_ref, ...), custom_call_target="tpu_custom_call" | custom-call | flops 2415919104 | bytes 3346432 | tf_op jit(solution)/shard_map/operator/pallas_call | solution.py:265
  27.9 0.9 %collective-permute-start.6 = (bf16[32,1024]{1,0:T(8,128)(2,1)S(1)}, bf16[32,1024]{1,0:T(8,128)(2,1)S(1)}, u32[]{:S(2)}, u32[]{:S(2)}) collective-permute-start(bf16[32,1024]{1,0:T(8,128)(2,1)S(1)} %get-tuple-element.27), channel_id=1, source_target_pairs={{0,4},{4,0},{8,12},{12,8},{1,5},{5,1},{9,13},{13,9},{2,6},{6,2},{1... | collective-permute-start | bytes 196616 | tf_op jit(solution)/shard_map/ppermute | solution.py:288
  29.5 4.0 %collective-permute-start.8 = (bf16[32,1024]{1,0:T(8,128)(2,1)S(1)}, bf16[32,1024]{1,0:T(8,128)(2,1)S(1)}, u32[]{:S(2)}, u32[]{:S(2)}) collective-permute-start(bf16[32,1024]{1,0:T(8,128)(2,1)S(1)} %get-tuple-element.29), channel_id=1, source_target_pairs={{0,8},{4,12},{8,0},{12,4},{1,9},{5,13},{9,1},{13,5},{2,10},{6,14},... | collective-permute-start | bytes 196616 | tf_op jit(solution)/shard_map/ppermute | solution.py:288
  33.5 2.8 %collective-permute-done.8.bc_ref = bf16[32,1024]{1,0:T(8,128)(2,1)S(1)} collective-permute-done((bf16[32,1024]{1,0:T(8,128)(2,1)S(1)}, bf16[32,1024]{1,0:T(8,128)(2,1)S(1)}, u32[]{:S(2)}, u32[]{:S(2)}) %collective-permute-start.8) | collective-permute-done | bytes 65568 | tf_op jit(solution)/shard_map/ppermute | solution.py:288
  36.3 0.8 %middle.1 = (bf16[384,1024]{1,0:T(8,128)(2,1)S(1)}, bf16[32,1024]{1,0:T(8,128)(2,1)S(1)}, bf16[32,1024]{1,0:T(8,128)(2,1)S(1)}, bf16[32,1024]{1,0:T(8,128)(2,1)S(1)}) custom-call(f32[384,1024]{1,0:T(8,128)S(1)} %get-tuple-element.26.own_ref, bf16[32,1024]{1,0:T(8,128)(2,1)S(1)} %collective-permute-done.6.ba_ref, ...), custom_call_target="tpu_custom_call" | custom-call | flops 201326592 | bytes 1779584 | tf_op jit(solution)/shard_map/middle/pallas_call | solution.py:265
  37.1 3.5 %collective-permute-start.9 = (bf16[32,1024]{1,0:T(8,128)(2,1)S(1)}, bf16[32,1024]{1,0:T(8,128)(2,1)S(1)}, u32[]{:S(2)}, u32[]{:S(2)}) collective-permute-start(bf16[32,1024]{1,0:T(8,128)(2,1)S(1)} %get-tuple-element.31), channel_id=1, source_target_pairs={{0,4},{4,0},{8,12},{12,8},{1,5},{5,1},{9,13},{13,9},{2,6},{6,2},{1... | collective-permute-start | bytes 196616 | tf_op jit(solution)/shard_map/ppermute | solution.py:288
  40.6 0.8 %collective-permute-start.10 = (bf16[32,1024]{1,0:T(8,128)(2,1)S(1)}, bf16[32,1024]{1,0:T(8,128)(2,1)S(1)}, u32[]{:S(2)}, u32[]{:S(2)}) collective-permute-start(bf16[32,1024]{1,0:T(8,128)(2,1)S(1)} %get-tuple-element.32), channel_id=1, source_target_pairs={{4,8},{8,4},{5,9},{9,5},{6,10},{10,6},{7,11},{11,7},{20,24},{24,20... | collective-permute-start | bytes 196616 | tf_op jit(solution)/shard_map/ppermute | solution.py:288
  41.5 2.8 %collective-permute-start.11 = (bf16[32,1024]{1,0:T(8,128)(2,1)S(1)}, bf16[32,1024]{1,0:T(8,128)(2,1)S(1)}, u32[]{:S(2)}, u32[]{:S(2)}) collective-permute-start(bf16[32,1024]{1,0:T(8,128)(2,1)S(1)} %get-tuple-element.33), channel_id=1, source_target_pairs={{0,8},{4,12},{8,0},{12,4},{1,9},{5,13},{9,1},{13,5},{2,10},{6,14},... | collective-permute-start | bytes 196616 | tf_op jit(solution)/shard_map/ppermute | solution.py:288
  44.3 2.7 %collective-permute-done.11.ac_ref = bf16[32,1024]{1,0:T(8,128)(2,1)S(1)} collective-permute-done((bf16[32,1024]{1,0:T(8,128)(2,1)S(1)}, bf16[32,1024]{1,0:T(8,128)(2,1)S(1)}, u32[]{:S(2)}, u32[]{:S(2)}) %collective-permute-start.11) | collective-permute-done | bytes 65568 | tf_op jit(solution)/shard_map/ppermute | solution.py:288
  46.9 7.6 %operator_interior.1 = (f32[384,1024]{1,0:T(8,128)S(1)}, bf16[32,1024]{1,0:T(8,128)(2,1)S(1)}, bf16[32,1024]{1,0:T(8,128)(2,1)S(1)}, bf16[32,1024]{1,0:T(8,128)(2,1)S(1)}, bf16[128,8192]{1,0:T(8,128)(2,1)}) custom-call(s32[1]{0:T(128)S(6)} %copy.15.count_ref, s32[1]{0:T(128)} %bitcast.par_ref, bf16[384,1024]{1,0:T(8,128)(2,1)S(1)} %get-tuple-element.30.z_ref, ...), custom_call_target="tpu_custom_call" | custom-call | flops 2415919104 | bytes 4919296 | tf_op jit(solution)/shard_map/operator_interior/pallas_call | solution.py:265
  54.5 2.4 %collective-permute-start.12 = (bf16[32,1024]{1,0:T(8,128)(2,1)S(1)}, bf16[32,1024]{1,0:T(8,128)(2,1)S(1)}, u32[]{:S(2)}, u32[]{:S(2)}) collective-permute-start(bf16[32,1024]{1,0:T(8,128)(2,1)S(1)} %get-tuple-element.36), channel_id=1, source_target_pairs={{0,4},{4,0},{8,12},{12,8},{1,5},{5,1},{9,13},{13,9},{2,6},{6,2},{1... | collective-permute-start | bytes 196616 | tf_op jit(solution)/shard_map/ppermute | solution.py:288
  57.6 2.8 %collective-permute-start.14 = (bf16[32,1024]{1,0:T(8,128)(2,1)S(1)}, bf16[32,1024]{1,0:T(8,128)(2,1)S(1)}, u32[]{:S(2)}, u32[]{:S(2)}) collective-permute-start(bf16[32,1024]{1,0:T(8,128)(2,1)S(1)} %get-tuple-element.38), channel_id=1, source_target_pairs={{0,8},{4,12},{8,0},{12,4},{1,9},{5,13},{9,1},{13,5},{2,10},{6,14},... | collective-permute-start | bytes 196616 | tf_op jit(solution)/shard_map/ppermute | solution.py:288
  60.4 2.8 %collective-permute-done.14.bc_ref = bf16[32,1024]{1,0:T(8,128)(2,1)S(1)} collective-permute-done((bf16[32,1024]{1,0:T(8,128)(2,1)S(1)}, bf16[32,1024]{1,0:T(8,128)(2,1)S(1)}, u32[]{:S(2)}, u32[]{:S(2)}) %collective-permute-start.14) | collective-permute-done | bytes 65568 | tf_op jit(solution)/shard_map/ppermute | solution.py:288
  63.2 1.3 %last.1 = bf16[384,1024]{1,0:T(8,128)(2,1)} custom-call(f32[384,1024]{1,0:T(8,128)S(1)} %get-tuple-element.35.own_ref, bf16[32,1024]{1,0:T(8,128)(2,1)S(1)} %collective-permute-done.12.ba_ref, bf16[32,1024]{1,0:T(8,128)(2,1)S(1)} %collective-permute-done.13.bb_ref, bf16[32,1024]{1,0:T(8,128)(2,1)S(1)} %collective-permute-done.14.bc_ref, ...), custom_call_target="tpu_custom_call" | custom-call | flops 100663296 | bytes 1769856 | tf_op jit(solution)/shard_map/last/pallas_call | solution.py:265
  (31 shorter events, 5.8 us)
Async XLA Ops:
  0.6 22.7 %copy-start.7 = (f32[128]{0:T(128)S(1)}, f32[128]{0:T(128)}, u32[]{:S(2)}) copy-start(f32[128]{0:T(128)} %param.14) | copy-start | bytes 1540
  0.6 22.7 %copy-start.6 = (f32[128]{0:T(128)S(1)}, f32[128]{0:T(128)}, u32[]{:S(2)}) copy-start(f32[128]{0:T(128)} %param.13) | copy-start | bytes 1540
  1.4 8.3 %collective-permute-start.2 = (s32[1,32]{1,0:T(1,128)S(1)}, s32[1,32]{1,0:T(1,128)S(1)}, u32[]{:S(2)}, u32[]{:S(2)}) collective-permute-start(s32[1,32]{1,0:T(1,128)S(1)} %get-tuple-element.40), channel_id=1, source_target_pairs={{0,8},{4,12},{8,0},{12,4},{1,9},{5,13},{9,1},{13,5},{2,10},{6,14},... | collective-permute-start | bytes 392 | tf_op jit(solution)/shard_map/ppermute | solution.py:288
  5.4 4.2 %collective-permute-start.1 = (s32[1,32]{1,0:T(1,128)S(1)}, s32[1,32]{1,0:T(1,128)S(1)}, u32[]{:S(2)}, u32[]{:S(2)}) collective-permute-start(s32[1,32]{1,0:T(1,128)S(1)} %get-tuple-element.41), channel_id=1, source_target_pairs={{4,8},{8,4},{5,9},{9,5},{6,10},{10,6},{7,11},{11,7},{20,24},{24,20... | collective-permute-start | bytes 392 | tf_op jit(solution)/shard_map/ppermute | solution.py:288
  6.1 4.4 %collective-permute-start = (s32[1,32]{1,0:T(1,128)S(1)}, s32[1,32]{1,0:T(1,128)S(1)}, u32[]{:S(2)}, u32[]{:S(2)}) collective-permute-start(s32[1,32]{1,0:T(1,128)S(1)} %get-tuple-element.42), channel_id=1, source_target_pairs={{0,4},{4,0},{8,12},{12,8},{1,5},{5,1},{9,13},{13,9},{2,6},{6,2},{1... | collective-permute-start | bytes 392 | tf_op jit(solution)/shard_map/ppermute | solution.py:288
  10.5 1.1 %copy-start = (bf16[384,1024]{1,0:T(8,128)(2,1)S(1)}, bf16[384,1024]{1,0:T(8,128)(2,1)}, u32[]{:S(2)}) copy-start(bf16[384,1024]{1,0:T(8,128)(2,1)} %rhs_ref.1) | copy-start | bytes 2359300
  11.6 0.7 %copy-start.4 = (bf16[64,64]{1,0:T(8,128)(2,1)S(1)}, bf16[64,64]{1,0:T(8,128)(2,1)}, u32[]{:S(2)}) copy-start(bf16[64,64]{1,0:T(8,128)(2,1)} %jacobi_ref.3) | copy-start | bytes 24580
  12.9 10.4 %collective-permute-start.3 = (bf16[32,1024]{1,0:T(8,128)(2,1)S(1)}, bf16[32,1024]{1,0:T(8,128)(2,1)S(1)}, u32[]{:S(2)}, u32[]{:S(2)}) collective-permute-start(bf16[32,1024]{1,0:T(8,128)(2,1)S(1)} %get-tuple-element.22), channel_id=1, source_target_pairs={{0,4},{4,0},{8,12},{12,8},{1,5},{5,1},{9,13},{13,9},{2,6},{6,2},{1... | collective-permute-start | bytes 196616 | tf_op jit(solution)/shard_map/ppermute | solution.py:288
  15.0 8.3 %collective-permute-start.4 = (bf16[32,1024]{1,0:T(8,128)(2,1)S(1)}, bf16[32,1024]{1,0:T(8,128)(2,1)S(1)}, u32[]{:S(2)}, u32[]{:S(2)}) collective-permute-start(bf16[32,1024]{1,0:T(8,128)(2,1)S(1)} %get-tuple-element.23), channel_id=1, source_target_pairs={{4,8},{8,4},{5,9},{9,5},{6,10},{10,6},{7,11},{11,7},{20,24},{24,20... | collective-permute-start | bytes 196616 | tf_op jit(solution)/shard_map/ppermute | solution.py:288
  15.7 7.7 %collective-permute-start.5 = (bf16[32,1024]{1,0:T(8,128)(2,1)S(1)}, bf16[32,1024]{1,0:T(8,128)(2,1)S(1)}, u32[]{:S(2)}, u32[]{:S(2)}) collective-permute-start(bf16[32,1024]{1,0:T(8,128)(2,1)S(1)} %get-tuple-element.24), channel_id=1, source_target_pairs={{0,8},{4,12},{8,0},{12,4},{1,9},{5,13},{9,1},{13,5},{2,10},{6,14},... | collective-permute-start | bytes 196616 | tf_op jit(solution)/shard_map/ppermute | solution.py:288
  19.9 1.0 %copy-start.1 = (bf16[384,512]{1,0:T(8,128)(2,1)S(1)}, bf16[384,512]{1,0:T(8,128)(2,1)}, u32[]{:S(2)}) copy-start(bf16[384,512]{1,0:T(8,128)(2,1)} %lift_ref.1) | copy-start | bytes 1179652
  20.9 1.0 %copy-start.2 = (bf16[384,384]{1,0:T(8,128)(2,1)S(1)}, bf16[384,384]{1,0:T(8,128)(2,1)}, u32[]{:S(2)}) copy-start(bf16[384,384]{1,0:T(8,128)(2,1)} %stiff_ref.1) | copy-start | bytes 884740
  21.9 1.0 %copy-start.3 = (bf16[384,384]{1,0:T(8,128)(2,1)S(1)}, bf16[384,384]{1,0:T(8,128)(2,1)}, u32[]{:S(2)}) copy-start(bf16[384,384]{1,0:T(8,128)(2,1)} %mass_ref.1) | copy-start | bytes 884740
  23.4 12.9 %copy-start.5 = (bf16[64,64]{1,0:T(8,128)(2,1)S(1)}, bf16[64,64]{1,0:T(8,128)(2,1)}, u32[]{:S(2)}) copy-start(bf16[64,64]{1,0:T(8,128)(2,1)} %jacobi_ref.3) | copy-start | bytes 24580
  27.9 5.5 %collective-permute-start.6 = (bf16[32,1024]{1,0:T(8,128)(2,1)S(1)}, bf16[32,1024]{1,0:T(8,128)(2,1)S(1)}, u32[]{:S(2)}, u32[]{:S(2)}) collective-permute-start(bf16[32,1024]{1,0:T(8,128)(2,1)S(1)} %get-tuple-element.27), channel_id=1, source_target_pairs={{0,4},{4,0},{8,12},{12,8},{1,5},{5,1},{9,13},{13,9},{2,6},{6,2},{1... | collective-permute-start | bytes 196616 | tf_op jit(solution)/shard_map/ppermute | solution.py:288
  28.8 4.7 %collective-permute-start.7 = (bf16[32,1024]{1,0:T(8,128)(2,1)S(1)}, bf16[32,1024]{1,0:T(8,128)(2,1)S(1)}, u32[]{:S(2)}, u32[]{:S(2)}) collective-permute-start(bf16[32,1024]{1,0:T(8,128)(2,1)S(1)} %get-tuple-element.28), channel_id=1, source_target_pairs={{4,8},{8,4},{5,9},{9,5},{6,10},{10,6},{7,11},{11,7},{20,24},{24,20... | collective-permute-start | bytes 196616 | tf_op jit(solution)/shard_map/ppermute | solution.py:288
  29.5 6.9 %collective-permute-start.8 = (bf16[32,1024]{1,0:T(8,128)(2,1)S(1)}, bf16[32,1024]{1,0:T(8,128)(2,1)S(1)}, u32[]{:S(2)}, u32[]{:S(2)}) collective-permute-start(bf16[32,1024]{1,0:T(8,128)(2,1)S(1)} %get-tuple-element.29), channel_id=1, source_target_pairs={{0,8},{4,12},{8,0},{12,4},{1,9},{5,13},{9,1},{13,5},{2,10},{6,14},... | collective-permute-start | bytes 196616 | tf_op jit(solution)/shard_map/ppermute | solution.py:288
  37.1 7.1 %collective-permute-start.9 = (bf16[32,1024]{1,0:T(8,128)(2,1)S(1)}, bf16[32,1024]{1,0:T(8,128)(2,1)S(1)}, u32[]{:S(2)}, u32[]{:S(2)}) collective-permute-start(bf16[32,1024]{1,0:T(8,128)(2,1)S(1)} %get-tuple-element.31), channel_id=1, source_target_pairs={{0,4},{4,0},{8,12},{12,8},{1,5},{5,1},{9,13},{13,9},{2,6},{6,2},{1... | collective-permute-start | bytes 196616 | tf_op jit(solution)/shard_map/ppermute | solution.py:288
  40.6 3.6 %collective-permute-start.10 = (bf16[32,1024]{1,0:T(8,128)(2,1)S(1)}, bf16[32,1024]{1,0:T(8,128)(2,1)S(1)}, u32[]{:S(2)}, u32[]{:S(2)}) collective-permute-start(bf16[32,1024]{1,0:T(8,128)(2,1)S(1)} %get-tuple-element.32), channel_id=1, source_target_pairs={{4,8},{8,4},{5,9},{9,5},{6,10},{10,6},{7,11},{11,7},{20,24},{24,20... | collective-permute-start | bytes 196616 | tf_op jit(solution)/shard_map/ppermute | solution.py:288
  41.5 5.5 %collective-permute-start.11 = (bf16[32,1024]{1,0:T(8,128)(2,1)S(1)}, bf16[32,1024]{1,0:T(8,128)(2,1)S(1)}, u32[]{:S(2)}, u32[]{:S(2)}) collective-permute-start(bf16[32,1024]{1,0:T(8,128)(2,1)S(1)} %get-tuple-element.33), channel_id=1, source_target_pairs={{0,8},{4,12},{8,0},{12,4},{1,9},{5,13},{9,1},{13,5},{2,10},{6,14},... | collective-permute-start | bytes 196616 | tf_op jit(solution)/shard_map/ppermute | solution.py:288
  54.5 5.9 %collective-permute-start.12 = (bf16[32,1024]{1,0:T(8,128)(2,1)S(1)}, bf16[32,1024]{1,0:T(8,128)(2,1)S(1)}, u32[]{:S(2)}, u32[]{:S(2)}) collective-permute-start(bf16[32,1024]{1,0:T(8,128)(2,1)S(1)} %get-tuple-element.36), channel_id=1, source_target_pairs={{0,4},{4,0},{8,12},{12,8},{1,5},{5,1},{9,13},{13,9},{2,6},{6,2},{1... | collective-permute-start | bytes 196616 | tf_op jit(solution)/shard_map/ppermute | solution.py:288
  56.9 3.4 %collective-permute-start.13 = (bf16[32,1024]{1,0:T(8,128)(2,1)S(1)}, bf16[32,1024]{1,0:T(8,128)(2,1)S(1)}, u32[]{:S(2)}, u32[]{:S(2)}) collective-permute-start(bf16[32,1024]{1,0:T(8,128)(2,1)S(1)} %get-tuple-element.37), channel_id=1, source_target_pairs={{4,8},{8,4},{5,9},{9,5},{6,10},{10,6},{7,11},{11,7},{20,24},{24,20... | collective-permute-start | bytes 196616 | tf_op jit(solution)/shard_map/ppermute | solution.py:288
  57.6 5.6 %collective-permute-start.14 = (bf16[32,1024]{1,0:T(8,128)(2,1)S(1)}, bf16[32,1024]{1,0:T(8,128)(2,1)S(1)}, u32[]{:S(2)}, u32[]{:S(2)}) collective-permute-start(bf16[32,1024]{1,0:T(8,128)(2,1)S(1)} %get-tuple-element.38), channel_id=1, source_target_pairs={{0,8},{4,12},{8,0},{12,4},{1,9},{5,13},{9,1},{13,5},{2,10},{6,14},... | collective-permute-start | bytes 196616 | tf_op jit(solution)/shard_map/ppermute | solution.py:288

commit v2 on v1

v2 whole, which is shorter than its diff:
```python
import functools

import jax
import jax.numpy as jnp
from jax import lax
from jax.experimental import pallas as pl
from jax.experimental.pallas import tpu as pltpu
from jax.sharding import PartitionSpec as P

F32 = jnp.float32
BF16 = jnp.bfloat16
I32 = jnp.int32
LANES = 128
VMEM = pltpu.VMEM
SMEM = pltpu.SMEM
HBM = pltpu.HBM


def iota(shape, dim):
    return lax.broadcasted_iota(I32, shape, dim)


def one_hot(condition):
    return jnp.where(condition, 1.0, 0.0).astype(BF16)


def matmul(a, b):
    return jnp.dot(a, b, preferred_element_type=F32)


def column_tiles(row):
    count = row.shape[1] // LANES
    return [
        jnp.transpose(
            jnp.broadcast_to(row[:, t * LANES : (t + 1) * LANES].astype(F32), (LANES, LANES))
        )
        for t in range(count)
    ]


def block_diagonal(block, copies):
    rows, cols = block.shape
    wide = jnp.concatenate([block] * copies, axis=1)
    full = jnp.concatenate([wide] * copies, axis=0)
    shape = (rows * copies, cols * copies)
    keep = (iota(shape, 0) // rows) == (iota(shape, 1) // cols)
    return jnp.where(keep, full, jnp.zeros_like(full))


def precondition(traces_ref, scale_ref, jacobi_ref, z_ref):
    width = traces_ref.shape[1]
    block = block_diagonal(jacobi_ref[...].astype(F32), 4).astype(BF16)
    scales = column_tiles(scale_ref[...])
    step = block.shape[0]
    for start in range(0, width, step):
        product = matmul(traces_ref[:, start : start + step], block)
        for t, scale in enumerate(scales):
            part = product[t * LANES : (t + 1) * LANES, :]
            both = jnp.concatenate([scale, scale], axis=1)
            z_ref[t * LANES : (t + 1) * LANES, start : start + step] = (part * both).astype(BF16)


def paired_weight(src_ref, dst_ref, offset, face_dofs):
    rows, cols = src_ref.shape
    low = iota((face_dofs, LANES), 1) < face_dofs
    zero = jnp.zeros((face_dofs, LANES), F32)
    for k in range(rows // face_dofs):
        top = k * 2 * face_dofs
        for t in range(cols // LANES):
            tile = src_ref[k * face_dofs : (k + 1) * face_dofs, t * LANES : (t + 1) * LANES]
            tile = tile.astype(F32)
            turned = pltpu.roll(tile, face_dofs, 1)
            at = offset + 2 * t * LANES
            pieces = (
                (0, 0, jnp.where(low, tile, zero)),
                (1, 0, jnp.where(low, zero, turned)),
                (0, 1, jnp.where(low, turned, zero)),
                (1, 1, jnp.where(low, zero, tile)),
            )
            for half, odd, piece in pieces:
                dst_ref[
                    top + half * face_dofs : top + (half + 1) * face_dofs,
                    at + odd * LANES : at + (odd + 1) * LANES,
                ] = piece.astype(BF16)


def paired_lifting(src_ref, dst_ref, face_dofs):
    rows, inside = src_ref.shape
    zero = jnp.zeros((face_dofs, inside), BF16)
    for k in range(rows // face_dofs):
        part = src_ref[k * face_dofs : (k + 1) * face_dofs, :]
        top = 2 * k * face_dofs
        dst_ref[top : top + face_dofs, :inside] = part
        dst_ref[top : top + face_dofs, inside:] = zero
        dst_ref[top + face_dofs : top + 2 * face_dofs, :inside] = zero
        dst_ref[top + face_dofs : top + 2 * face_dofs, inside:] = part


def prepare_kernel(
    rhs_hbm, jacobi_hbm, stiff_hbm, mass_hbm, scale_hbm, z_ref, w_ref, scale_ref,
    rhs_ref, jacobi_ref, stiff_ref, mass_ref, line_ref, sems
):
    sources = (stiff_hbm, mass_hbm, jacobi_hbm, scale_hbm, rhs_hbm)
    targets = (stiff_ref, mass_ref, jacobi_ref, line_ref, rhs_ref)
    copies = [
        pltpu.make_async_copy(src, dst, sems.at[i])
        for i, (src, dst) in enumerate(zip(sources, targets))
    ]
    for copy in copies:
        copy.start()
    face_dofs = jacobi_ref.shape[0]
    copies[0].wait()
    paired_weight(stiff_ref, w_ref, 0, face_dofs)
    copies[1].wait()
    paired_weight(mass_ref, w_ref, w_ref.shape[1] // 2, face_dofs)
    copies[2].wait()
    copies[3].wait()
    scale_ref[...] = line_ref[...].reshape(scale_ref.shape)
    copies[4].wait()
    precondition(rhs_ref, scale_ref, jacobi_ref, z_ref)


def wanted_row(par, list_refs):
    picked = [jnp.where(par == 0, list_refs[0][0], list_refs[0][1])]
    picked.append(jnp.where(par == 0, list_refs[1][1], list_refs[1][0]))
    picked.append(list_refs[2][2])
    row = jnp.concatenate(picked, axis=1)
    pad = jnp.full((1, LANES - row.shape[1]), -1, I32)
    return jnp.concatenate([row, pad], axis=1)


def send_rows(wanted, z_ref, out_refs):
    faces = z_ref.shape[0]
    (column,) = column_tiles(wanted)
    column = column.astype(I32)
    lane = iota((LANES, LANES), 1)
    picks = jnp.concatenate(
        [one_hot(column == lane + t * LANES) for t in range(faces // LANES)], axis=1
    )
    rows = matmul(picks, z_ref[...]).astype(BF16)
    slots = out_refs[0].shape[0]
    for c, out_ref in enumerate(out_refs):
        out_ref[...] = rows[c * slots : (c + 1) * slots, :]


def send_kernel(par_ref, z_ref, la_ref, lb_ref, lc_ref, oa_ref, ob_ref, oc_ref, wanted_ref):
    wanted = wanted_row(par_ref[0], [la_ref, lb_ref, lc_ref])
    wanted_ref[...] = wanted
    send_rows(wanted, z_ref, [oa_ref, ob_ref, oc_ref])


def column_ids(par, faces, slots, tile, axis):
    index = iota((LANES, LANES), axis) + tile * LANES
    shift = slots * (1 - par)
    first = (index >= faces) & (index < faces + slots)
    second = (index >= faces + slots) & (index < faces + 2 * slots)
    return index + jnp.where(first, shift, 0) - jnp.where(second, shift, 0)


def tables_kernel(slots, faces, count_ref, par_ref, ids_ref, pick_ref, spread_ref):
    par = par_ref[0]
    ids_all = jnp.where(iota(ids_ref.shape, 1) < count_ref[0], ids_ref[...], -1)
    tiles = spread_ref.shape[0] // LANES
    lanes = [column_ids(par, faces, slots, t, 1) for t in range(tiles)]
    rows = [column_ids(par, faces, slots, t, 0) for t in range(tiles)]
    for k in range(ids_ref.shape[0]):
        across = jnp.broadcast_to(ids_all[k : k + 1, :], (LANES, LANES))
        down = jnp.transpose(across.astype(F32)).astype(I32)
        for t in range(tiles):
            pick_ref[k * LANES : (k + 1) * LANES, t * LANES : (t + 1) * LANES] = one_hot(
                down == lanes[t]
            )
            spread_ref[t * LANES : (t + 1) * LANES, k * LANES : (k + 1) * LANES] = one_hot(
                across == rows[t]
            )


def gather_kernel(pick_ref, z_ref, x_ref):
    faces, width = z_ref.shape
    for k in range(pick_ref.shape[0] // LANES):
        rows = matmul(pick_ref[k * LANES : (k + 1) * LANES, :faces], z_ref[...]).astype(BF16)
        for p in range(width // LANES):
            x_ref[p * LANES : (p + 1) * LANES, k * LANES : (k + 1) * LANES] = rows[
                :, p * LANES : (p + 1) * LANES
            ]


def operator_kernel(
    pick_ref, spread_ref, own_x_ref, aa_ref, ab_ref, ac_ref, stiff_scale_ref, mass_scale_ref,
    w_ref, y_ref, ba_ref, bb_ref, bc_ref, x_ref, halo_ref
):
    slots, width = aa_ref.shape
    for c, ref in enumerate((aa_ref, ab_ref, ac_ref)):
        halo_ref[c * slots : (c + 1) * slots, :] = ref[...]
    halo_ref[3 * slots :, :] = jnp.zeros((halo_ref.shape[0] - 3 * slots, width), BF16)
    faces = spread_ref.shape[0] - halo_ref.shape[0]
    for k in range(6):
        rows = matmul(pick_ref[k * LANES : (k + 1) * LANES, faces:], halo_ref[...]).astype(BF16)
        for p in range(width // LANES):
            at = (slice(p * LANES, (p + 1) * LANES), slice(k * LANES, (k + 1) * LANES))
            x_ref[at] = own_x_ref[at] + rows[:, p * LANES : (p + 1) * LANES]
    (stiff_scale,) = column_tiles(stiff_scale_ref[...])
    (mass_scale,) = column_tiles(mass_scale_ref[...])
    half = w_ref.shape[1] // 2
    stiff = jnp.concatenate([stiff_scale] * 6, axis=1)
    mass = jnp.concatenate([mass_scale] * 6, axis=1)
    step = 2 * LANES
    for start in range(0, x_ref.shape[0], step):
        product = matmul(x_ref[start : start + step, :], w_ref[...])
        for r in range(step // LANES):
            p = start // LANES + r
            part = product[r * LANES : (r + 1) * LANES, :]
            term = (stiff * part[:, :half] - mass * part[:, half:]).astype(BF16)
            for k in range(6):
                y_ref[k * LANES : (k + 1) * LANES, p * LANES : (p + 1) * LANES] = term[
                    :, k * LANES : (k + 1) * LANES
                ]
    rows = matmul(spread_ref[faces:, :], y_ref[...]).astype(BF16)
    for c, ref in enumerate((ba_ref, bb_ref, bc_ref)):
        ref[...] = rows[c * slots : (c + 1) * slots, :]


def own_sums(spread_ref, y_ref, own_ref):
    for t in range(own_ref.shape[0] // LANES):
        own_ref[t * LANES : (t + 1) * LANES, :] = matmul(
            spread_ref[t * LANES : (t + 1) * LANES, :], y_ref[...]
        )


def sums_kernel(spread_ref, y_ref, own_ref):
    own_sums(spread_ref, y_ref, own_ref)


def finish_kernel(
    face_dofs, spread_ref, y_ref, x_ref, lift_hbm, own_ref, interior_hbm,
    inside_ref, plain_ref, lift_ref, lift_sem, sems
):
    load = pltpu.make_async_copy(lift_hbm, plain_ref, lift_sem)
    load.start()
    own_sums(spread_ref, y_ref, own_ref)
    load.wait()
    paired_lifting(plain_ref, lift_ref, face_dofs)
    wide = lift_ref.shape[1]
    step = 2 * LANES
    copies = []
    for start in range(0, x_ref.shape[0], step):
        product = matmul(x_ref[start : start + step, :], lift_ref[...]).astype(BF16)
        first = start // LANES
        for r in range(step // LANES):
            inside_ref[:, (first + r) * wide : (first + r + 1) * wide] = product[
                r * LANES : (r + 1) * LANES, :
            ]
        span = pl.ds(first * wide, step // LANES * wide)
        copy = pltpu.make_async_copy(
            inside_ref.at[:, span], interior_hbm.at[:, span], sems.at[len(copies)]
        )
        copy.start()
        copies.append(copy)
    for copy in copies:
        copy.wait()


def collect(own_ref, back_refs, wanted, gathered_ref):
    slots, width = back_refs[0].shape
    for c, ref in enumerate(back_refs):
        gathered_ref[c * slots : (c + 1) * slots, :] = ref[...]
    gathered_ref[3 * slots :, :] = jnp.zeros((LANES - 3 * slots, width), BF16)
    faces = own_ref.shape[0]
    target = jnp.broadcast_to(wanted, (faces, LANES))
    picks = one_hot(target == iota((faces, LANES), 0))
    return (own_ref[...] + matmul(picks, gathered_ref[...])).astype(BF16)


def middle_kernel(
    own_ref, ba_ref, bb_ref, bc_ref, wanted_ref, scale_ref, jacobi_ref, z_ref,
    oa_ref, ob_ref, oc_ref, gathered_ref, v_ref
):
    wanted = wanted_ref[...]
    v_ref[...] = collect(own_ref, [ba_ref, bb_ref, bc_ref], wanted, gathered_ref)
    precondition(v_ref, scale_ref, jacobi_ref, z_ref)
    send_rows(wanted, z_ref, [oa_ref, ob_ref, oc_ref])


def last_kernel(own_ref, ba_ref, bb_ref, bc_ref, wanted_ref, out_ref, gathered_ref):
    out_ref[...] = collect(own_ref, [ba_ref, bb_ref, bc_ref], wanted_ref[...], gathered_ref)


def call(kernel, operands, spaces, outs, scratch, flops, name, out_spaces=None, grant=12):
    out_spaces = out_spaces or [VMEM] * len(outs)
    moved = sum(a.size * a.dtype.itemsize for a in operands)
    return pl.pallas_call(
        kernel,
        out_shape=[jax.ShapeDtypeStruct(s, d) for s, d in outs],
        in_specs=[pl.BlockSpec(memory_space=s) for s in spaces],
        out_specs=[pl.BlockSpec(memory_space=s) for s in out_spaces],
        scratch_shapes=scratch,
        compiler_params=pltpu.CompilerParams(vmem_limit_bytes=grant * 1024 * 1024),
        cost_estimate=pl.CostEstimate(flops=flops, bytes_accessed=moved, transcendentals=0),
        name=name,
    )(*operands)


def in_hbm(array):
    return pltpu.with_memory_space_constraint(array, HBM)


def pairings(size):
    def both(pairs):
        return [pair for a, b in pairs for pair in ((a, b), (b, a))]

    even = both([(i, i + 1) for i in range(0, size - 1, 2)])
    odd = both([(i, i + 1) for i in range(1, size - 1, 2)])
    opposite = [(i, (i + size // 2) % size) for i in range(size)]
    return (even, odd, opposite)


def exchange(arrays, size):
    return [lax.ppermute(a, "elem", p) for a, p in zip(arrays, pairings(size))]


def per_device(
    size,
    trace_rhs,
    face_scale,
    stiff_scale,
    mass_scale,
    elem_faces,
    halo_faces,
    elem_count,
    jacobi_block,
    stiffness,
    mass,
    lifting,
):
    faces, width = trace_rhs.shape
    slots = halo_faces.shape[2]
    elems = elem_faces.shape[0]
    face_dofs = jacobi_block.shape[0]
    eld, inside = lifting.shape
    pairs = width // LANES
    halo_rows = LANES
    ext_rows = faces + halo_rows
    slots_all = 6 * elems
    lists = exchange([halo_faces.transpose(1, 0, 2)] * 3, size)
    par = (lax.axis_index("elem") % 2).astype(I32).reshape(1)
    stiff_row = stiff_scale.reshape(1, elems)
    mass_row = mass_scale.reshape(1, elems)
    field = ((faces, width), BF16)
    rows = [((slots, width), BF16)] * 3
    x_shape = ((pairs * elems, 6 * LANES), BF16)
    y_shape = ((slots_all, width), BF16)
    own_shape = ((faces, width), F32)
    element_flops = 4 * pairs * elems * 768 * 768

    first, paired, scale = call(
        prepare_kernel,
        [in_hbm(a) for a in (trace_rhs, jacobi_block, stiffness, mass, face_scale)],
        [HBM] * 5,
        [field, ((2 * eld, 4 * eld), BF16), ((1, faces), F32)],
        [
            VMEM(trace_rhs.shape, BF16),
            VMEM(jacobi_block.shape, BF16),
            VMEM(stiffness.shape, BF16),
            VMEM(mass.shape, BF16),
            VMEM(face_scale.shape, F32),
            pltpu.SemaphoreType.DMA((5,)),
        ],
        2 * faces * width * 256,
        "prepare",
    )
    *outgoing, wanted = call(
        send_kernel,
        [par, first, *lists],
        [SMEM] + [VMEM] * 4,
        [*rows, ((1, LANES), I32)],
        [],
        2 * LANES * faces * width,
        "send",
    )
    arrived = exchange(outgoing, size)
    pick, spread = call(
        functools.partial(tables_kernel, slots, faces),
        [elem_count, par, elem_faces.T],
        [SMEM, SMEM, VMEM],
        [((slots_all, ext_rows), BF16), ((ext_rows, slots_all), BF16)],
        [],
        slots_all * ext_rows * 4,
        "tables",
    )

    def gather(z, name):
        (own_x,) = call(
            gather_kernel,
            [pick, z],
            [VMEM] * 2,
            [x_shape],
            [],
            2 * slots_all * faces * width,
            name,
        )
        return own_x

    def operator(own_x, arrived, keep_x, name):
        halo = VMEM((halo_rows, width), BF16)
        return call(
            operator_kernel,
            [pick, spread, own_x, *arrived, stiff_row, mass_row, paired],
            [VMEM] * 9,
            [y_shape, *rows] + ([x_shape] if keep_x else []),
            [halo] if keep_x else [VMEM(*x_shape), halo],
            element_flops,
            name,
        )

    own_x = gather(first, "gather1")
    y, *back = operator(own_x, arrived, False, "operator1")
    returned = exchange(back, size)
    (own,) = call(
        sums_kernel,
        [spread, y],
        [VMEM] * 2,
        [own_shape],
        [],
        2 * faces * slots_all * width,
        "sums1",
    )
    second, *outgoing = call(
        middle_kernel,
        [own, *returned, wanted, scale, jacobi_block],
        [VMEM] * 7,
        [field, *rows],
        [VMEM((LANES, width), BF16), VMEM((faces, width), BF16)],
        2 * faces * width * 256,
        "middle",
    )
    arrived = exchange(outgoing, size)
    own_x = gather(second, "gather2")
    y, *back, x = operator(own_x, arrived, True, "operator2")
    returned = exchange(back, size)
    own, interior = call(
        functools.partial(finish_kernel, face_dofs),
        [spread, y, x, in_hbm(lifting)],
        [VMEM] * 3 + [HBM],
        [own_shape, ((elems, width // face_dofs * inside), BF16)],
        [
            VMEM((elems, width // face_dofs * inside), BF16),
            VMEM(lifting.shape, BF16),
            VMEM((2 * eld, 2 * inside), BF16),
            pltpu.SemaphoreType.DMA,
            pltpu.SemaphoreType.DMA((pairs // 2,)),
        ],
        2 * pairs * elems * 768 * 1024,
        "finish",
        [VMEM, HBM],
    )
    (applied,) = call(
        last_kernel,
        [own, *returned, wanted],
        [VMEM] * 5,
        [field],
        [VMEM((LANES, width), BF16)],
        2 * faces * width * 128,
        "last",
    )
    return (applied, interior)


def solution(mesh):
    rows = P(("grp", "elem", "sub"))
    split = P(("grp", "elem", "sub"), "src")
    in_specs = (
        split,
        rows,
        rows,
        rows,
        P(("grp", "elem", "sub"), None),
        P(("grp", "elem", "sub"), None, None),
        rows,
        P(),
        P(),
        P(),
        P(),
    )
    return jax.shard_map(
        functools.partial(per_device, mesh.shape["elem"]),
        mesh=mesh,
        in_specs=in_specs,
        out_specs=(split, split),
        check_vma=False,
    )
```

time: 65 us -> 56.5 us (0.87)
  local copies, waits for them, and re-layouts: 6.26 us -> 0.02 us
  waiting for transfers between devices: 9.22 us -> 5.34 us
  Pallas kernels: 15.3 us -> 17.9 us
  other arithmetic: 0.69 us -> 0 us
    unnamed x17 -> x8, local copies, waits for them, and re-layouts: 5.57 us -> 0.02 us
    ppermute x15, waiting for transfers between devices: 9.22 us -> 5.34 us  [exchange(): return [lax.ppermute(a, 'elem', p) for a, p in zip(arrays, pairings(size))]]
    pallas_call x6 -> x11, Pallas kernels: 15.3 us -> 17.9 us  [call(): pl.pallas_call(kernel, out_shape=[jax.ShapeDtypeStruct(s, d) for s, d in...]
    squeeze x1 -> x0, other arithmetic: 0.69 us -> none  [per_device(): halo_faces[:, 2, :]]
    reshape x1 -> x0, local copies, waits for them, and re-layouts: 0.68 us -> none  [per_device(): scale = face_scale.reshape(1, faces)]
  transfers between devices with their start and end apart: 15 -> 15, of which waited for: 4 -> 3; matrix products, arithmetic and copies ran while one was open for 2% -> 0% of each run, Pallas kernels for 1% -> 15%
where the time goes in v2:
time: 56.5 us; the launch traced here: 56.2 us
  starting transfers between devices  31.4 us (56%)
  Pallas kernels  17.9 us (32%)
  waiting for transfers between devices  5.34 us (9%)
  between operations  1.54 us (3%)
    ppermute x15, starting transfers between devices, exchange(): return [lax.ppermute(a, 'elem', p) for a, p in zip(arrays, pairings(size))]  31.4 us
    pallas_call x11, Pallas kernels, call(): pl.pallas_call(kernel, out_shape=[jax.ShapeDtypeStruct(s, d) for s, d in...  17.9 us
    ppermute x15, waiting for transfers between devices, exchange(): return [lax.ppermute(a, 'elem', p) for a, p in zip(arrays, pairings(size))]  5.34 us
  transfers between devices with their start and end apart: 15, of which 3 were waited for; matrix products, arithmetic and copies ran while one was open for 0% of the time, Pallas kernels for 15%

profile of v2, /device:TPU:0, one launch (start us, length us, event | category | flops | bytes accessed | tf_op | source)
XLA Modules:
  0.0 56.2 jit_solution(10779032064427009948)
XLA Ops:
  0.6 4.1 %collective-permute-start.2 = (s32[3,1,32]{2,1,0:T(1,128)}, s32[3,1,32]{2,1,0:T(1,128)S(1)}, u32[]{:S(2)}, u32[]{:S(2)}) collective-permute-start(s32[3,1,32]{2,1,0:T(1,128)} %bitcast.10), channel_id=1, source_target_pairs={{0,8},{4,12},{8,0},{12,4},{1,9},{5,13},{9,1},{13,5},{2,10},{6,14},... | collective-permute-start | bytes 1160 | tf_op jit(solution)/shard_map/ppermute | solution.py:318
  5.4 2.9 %collective-permute-start = (s32[3,1,32]{2,1,0:T(1,128)}, s32[3,1,32]{2,1,0:T(1,128)S(1)}, u32[]{:S(2)}, u32[]{:S(2)}) collective-permute-start(s32[3,1,32]{2,1,0:T(1,128)} %bitcast.12), channel_id=1, source_target_pairs={{0,4},{4,0},{8,12},{12,8},{1,5},{5,1},{9,13},{13,9},{2,6},{6,2},{1... | collective-permute-start | bytes 1160 | tf_op jit(solution)/shard_map/ppermute | solution.py:318
  8.3 1.9 %prepare.1 = (bf16[384,1024]{1,0:T(8,128)(2,1)S(1)}, bf16[768,1536]{1,0:T(8,128)(2,1)S(1)}, f32[1,384]{1,0:T(1,128)S(1)}) custom-call(bf16[384,1024]{1,0:T(8,128)(2,1)} %rhs_hbm.1, bf16[64,64]{1,0:T(8,128)(2,1)} %jacobi_ref.1, bf16[384,384]{1,0:T(8,128)(2,1)} %stiff_hbm.1, bf16[384,384]{1,0:T(8,128)(2,1)} %mass_hbm.1, f32[384]{0:T(512)} %scale_hbm.1), custom_call_target="tpu_custom_call" | custom-call | flops 201326592 | bytes 1385984 | tf_op jit(solution)/shard_map/prepare/pallas_call | solution.py:291
  10.6 2.0 %collective-permute-start.3 = (bf16[32,1024]{1,0:T(8,128)(2,1)S(1)}, bf16[32,1024]{1,0:T(8,128)(2,1)S(1)}, u32[]{:S(2)}, u32[]{:S(2)}) collective-permute-start(bf16[32,1024]{1,0:T(8,128)(2,1)S(1)} %get-tuple-element.29), channel_id=1, source_target_pairs={{0,4},{4,0},{8,12},{12,8},{1,5},{5,1},{9,13},{13,9},{2,6},{6,2},{1... | collective-permute-start | bytes 196616 | tf_op jit(solution)/shard_map/ppermute | solution.py:318
  12.6 0.7 %collective-permute-start.4 = (bf16[32,1024]{1,0:T(8,128)(2,1)S(1)}, bf16[32,1024]{1,0:T(8,128)(2,1)S(1)}, u32[]{:S(2)}, u32[]{:S(2)}) collective-permute-start(bf16[32,1024]{1,0:T(8,128)(2,1)S(1)} %get-tuple-element.30), channel_id=1, source_target_pairs={{4,8},{8,4},{5,9},{9,5},{6,10},{10,6},{7,11},{11,7},{20,24},{24,20... | collective-permute-start | bytes 196616 | tf_op jit(solution)/shard_map/ppermute | solution.py:318
  13.3 2.9 %collective-permute-start.5 = (bf16[32,1024]{1,0:T(8,128)(2,1)S(1)}, bf16[32,1024]{1,0:T(8,128)(2,1)S(1)}, u32[]{:S(2)}, u32[]{:S(2)}) collective-permute-start(bf16[32,1024]{1,0:T(8,128)(2,1)S(1)} %get-tuple-element.31), channel_id=1, source_target_pairs={{0,8},{4,12},{8,0},{12,4},{1,9},{5,13},{9,1},{13,5},{2,10},{6,14},... | collective-permute-start | bytes 196616 | tf_op jit(solution)/shard_map/ppermute | solution.py:318
  17.2 1.0 %gather1.1.own_x_ref = bf16[1024,768]{1,0:T(8,128)(2,1)S(1)} custom-call(bf16[768,512]{1,0:T(8,128)(2,1)S(1)} %get-tuple-element.27.pick_ref, bf16[384,1024]{1,0:T(8,128)(2,1)S(1)} %get-tuple-element.28.z_ref), custom_call_target="tpu_custom_call" | custom-call | flops 603979776 | bytes 1572864 | tf_op jit(solution)/shard_map/gather1/pallas_call | solution.py:291
  18.3 1.4 %collective-permute-done.5.ac_ref = bf16[32,1024]{1,0:T(8,128)(2,1)S(1)} collective-permute-done((bf16[32,1024]{1,0:T(8,128)(2,1)S(1)}, bf16[32,1024]{1,0:T(8,128)(2,1)S(1)}, u32[]{:S(2)}, u32[]{:S(2)}) %collective-permute-start.5) | collective-permute-done | bytes 65568 | tf_op jit(solution)/shard_map/ppermute | solution.py:318
  19.7 3.4 %operator1.1 = (bf16[768,1024]{1,0:T(8,128)(2,1)S(1)}, bf16[32,1024]{1,0:T(8,128)(2,1)S(1)}, bf16[32,1024]{1,0:T(8,128)(2,1)S(1)}, bf16[32,1024]{1,0:T(8,128)(2,1)S(1)}) custom-call(bf16[768,512]{1,0:T(8,128)(2,1)S(1)} %get-tuple-element.27.pick_ref, bf16[512,768]{1,0:T(8,128)(2,1)S(1)} %get-tuple-element.26.spread_ref, ...), custom_call_target="tpu_custom_call" | custom-call | flops 2415919104 | bytes 5702656 | tf_op jit(solution)/shard_map/operator1/pallas_call | solution.py:291
  23.1 2.2 %collective-permute-start.6 = (bf16[32,1024]{1,0:T(8,128)(2,1)S(1)}, bf16[32,1024]{1,0:T(8,128)(2,1)S(1)}, u32[]{:S(2)}, u32[]{:S(2)}) collective-permute-start(bf16[32,1024]{1,0:T(8,128)(2,1)S(1)} %get-tuple-element.34), channel_id=1, source_target_pairs={{0,4},{4,0},{8,12},{12,8},{1,5},{5,1},{9,13},{13,9},{2,6},{6,2},{1... | collective-permute-start | bytes 196616 | tf_op jit(solution)/shard_map/ppermute | solution.py:318
  25.4 0.7 %collective-permute-start.7 = (bf16[32,1024]{1,0:T(8,128)(2,1)S(1)}, bf16[32,1024]{1,0:T(8,128)(2,1)S(1)}, u32[]{:S(2)}, u32[]{:S(2)}) collective-permute-start(bf16[32,1024]{1,0:T(8,128)(2,1)S(1)} %get-tuple-element.35), channel_id=1, source_target_pairs={{4,8},{8,4},{5,9},{9,5},{6,10},{10,6},{7,11},{11,7},{20,24},{24,20... | collective-permute-start | bytes 196616 | tf_op jit(solution)/shard_map/ppermute | solution.py:318
  26.0 2.8 %collective-permute-start.8 = (bf16[32,1024]{1,0:T(8,128)(2,1)S(1)}, bf16[32,1024]{1,0:T(8,128)(2,1)S(1)}, u32[]{:S(2)}, u32[]{:S(2)}) collective-permute-start(bf16[32,1024]{1,0:T(8,128)(2,1)S(1)} %get-tuple-element.36), channel_id=1, source_target_pairs={{0,8},{4,12},{8,0},{12,4},{1,9},{5,13},{9,1},{13,5},{2,10},{6,14},... | collective-permute-start | bytes 196616 | tf_op jit(solution)/shard_map/ppermute | solution.py:318
  28.8 0.8 %sums1.1.own_ref = f32[384,1024]{1,0:T(8,128)S(1)} custom-call(bf16[512,768]{1,0:T(8,128)(2,1)S(1)} %get-tuple-element.26.spread_ref, bf16[768,1024]{1,0:T(8,128)(2,1)S(1)} %get-tuple-element.33.y_ref), custom_call_target="tpu_custom_call" | custom-call | flops 603979776 | bytes 2359296 | tf_op jit(solution)/shard_map/sums1/pallas_call | solution.py:291
  29.6 2.0 %collective-permute-done.8.bc_ref = bf16[32,1024]{1,0:T(8,128)(2,1)S(1)} collective-permute-done((bf16[32,1024]{1,0:T(8,128)(2,1)S(1)}, bf16[32,1024]{1,0:T(8,128)(2,1)S(1)}, u32[]{:S(2)}, u32[]{:S(2)}) %collective-permute-start.8) | collective-permute-done | bytes 65568 | tf_op jit(solution)/shard_map/ppermute | solution.py:318
  31.7 0.7 %middle.1 = (bf16[384,1024]{1,0:T(8,128)(2,1)S(1)}, bf16[32,1024]{1,0:T(8,128)(2,1)S(1)}, bf16[32,1024]{1,0:T(8,128)(2,1)S(1)}, bf16[32,1024]{1,0:T(8,128)(2,1)S(1)}) custom-call(f32[384,1024]{1,0:T(8,128)S(1)} %sums1.1.own_ref, bf16[32,1024]{1,0:T(8,128)(2,1)S(1)} %collective-permute-done.6.ba_ref, bf16[32,1024]{1,0:T(8,128)(2,1)S(1)} %collective-permute-done.7.bb_ref, ...), custom_call_target="tpu_custom_call" | custom-call | flops 201326592 | bytes 1779712 | tf_op jit(solution)/shard_map/middle/pallas_call | solution.py:291
  32.4 3.4 %collective-permute-start.9 = (bf16[32,1024]{1,0:T(8,128)(2,1)S(1)}, bf16[32,1024]{1,0:T(8,128)(2,1)S(1)}, u32[]{:S(2)}, u32[]{:S(2)}) collective-permute-start(bf16[32,1024]{1,0:T(8,128)(2,1)S(1)} %get-tuple-element.40), channel_id=1, source_target_pairs={{0,4},{4,0},{8,12},{12,8},{1,5},{5,1},{9,13},{13,9},{2,6},{6,2},{1... | collective-permute-start | bytes 196616 | tf_op jit(solution)/shard_map/ppermute | solution.py:318
  36.4 2.8 %collective-permute-start.11 = (bf16[32,1024]{1,0:T(8,128)(2,1)S(1)}, bf16[32,1024]{1,0:T(8,128)(2,1)S(1)}, u32[]{:S(2)}, u32[]{:S(2)}) collective-permute-start(bf16[32,1024]{1,0:T(8,128)(2,1)S(1)} %get-tuple-element.42), channel_id=1, source_target_pairs={{0,8},{4,12},{8,0},{12,4},{1,9},{5,13},{9,1},{13,5},{2,10},{6,14},... | collective-permute-start | bytes 196616 | tf_op jit(solution)/shard_map/ppermute | solution.py:318
  39.2 1.0 %gather2.1.own_x_ref = bf16[1024,768]{1,0:T(8,128)(2,1)S(1)} custom-call(bf16[768,512]{1,0:T(8,128)(2,1)S(1)} %get-tuple-element.27.pick_ref, bf16[384,1024]{1,0:T(8,128)(2,1)S(1)} %get-tuple-element.39.z_ref), custom_call_target="tpu_custom_call" | custom-call | flops 603979776 | bytes 1572864 | tf_op jit(solution)/shard_map/gather2/pallas_call | solution.py:291
  40.3 1.8 %collective-permute-done.11.ac_ref = bf16[32,1024]{1,0:T(8,128)(2,1)S(1)} collective-permute-done((bf16[32,1024]{1,0:T(8,128)(2,1)S(1)}, bf16[32,1024]{1,0:T(8,128)(2,1)S(1)}, u32[]{:S(2)}, u32[]{:S(2)}) %collective-permute-start.11) | collective-permute-done | bytes 65568 | tf_op jit(solution)/shard_map/ppermute | solution.py:318
  42.1 3.4 %operator2.1 = (bf16[768,1024]{1,0:T(8,128)(2,1)S(1)}, bf16[32,1024]{1,0:T(8,128)(2,1)S(1)}, bf16[32,1024]{1,0:T(8,128)(2,1)S(1)}, bf16[32,1024]{1,0:T(8,128)(2,1)S(1)}, bf16[1024,768]{1,0:T(8,128)(2,1)S(1)}) custom-call(bf16[768,512]{1,0:T(8,128)(2,1)S(1)} %get-tuple-element.27.pick_ref, bf16[512,768]{1,0:T(8,128)(2,1)S(1)} %get-tuple-element.26.spread_ref, ...), custom_call_target="tpu_custom_call" | custom-call | flops 2415919104 | bytes 5702656 | tf_op jit(solution)/shard_map/operator2/pallas_call | solution.py:291
  45.5 2.3 %collective-permute-start.12 = (bf16[32,1024]{1,0:T(8,128)(2,1)S(1)}, bf16[32,1024]{1,0:T(8,128)(2,1)S(1)}, u32[]{:S(2)}, u32[]{:S(2)}) collective-permute-start(bf16[32,1024]{1,0:T(8,128)(2,1)S(1)} %get-tuple-element.46), channel_id=1, source_target_pairs={{0,4},{4,0},{8,12},{12,8},{1,5},{5,1},{9,13},{13,9},{2,6},{6,2},{1... | collective-permute-start | bytes 196616 | tf_op jit(solution)/shard_map/ppermute | solution.py:318
  48.5 2.8 %collective-permute-start.14 = (bf16[32,1024]{1,0:T(8,128)(2,1)S(1)}, bf16[32,1024]{1,0:T(8,128)(2,1)S(1)}, u32[]{:S(2)}, u32[]{:S(2)}) collective-permute-start(bf16[32,1024]{1,0:T(8,128)(2,1)S(1)} %get-tuple-element.48), channel_id=1, source_target_pairs={{0,8},{4,12},{8,0},{12,4},{1,9},{5,13},{9,1},{13,5},{2,10},{6,14},... | collective-permute-start | bytes 196616 | tf_op jit(solution)/shard_map/ppermute | solution.py:318
  51.3 3.6 %finish.1 = (f32[384,1024]{1,0:T(8,128)S(1)}, bf16[128,8192]{1,0:T(8,128)(2,1)}) custom-call(bf16[512,768]{1,0:T(8,128)(2,1)S(1)} %get-tuple-element.26.spread_ref, bf16[768,1024]{1,0:T(8,128)(2,1)S(1)} %get-tuple-element.43.y_ref, bf16[1024,768]{1,0:T(8,128)(2,1)S(1)} %get-tuple-element.44.x_ref, bf16[384,512]{1,0:T(8,128)(2,1)} %lift_hbm.1), custom_call_target="tpu_custom_call" | custom-call | flops 1610612736 | bytes 4325376 | tf_op jit(solution)/shard_map/finish/pallas_call | solution.py:291
  54.9 1.2 %last.1 = bf16[384,1024]{1,0:T(8,128)(2,1)} custom-call(f32[384,1024]{1,0:T(8,128)S(1)} %get-tuple-element.45.own_ref, bf16[32,1024]{1,0:T(8,128)(2,1)S(1)} %collective-permute-done.12.ba_ref, bf16[32,1024]{1,0:T(8,128)(2,1)S(1)} %collective-permute-done.13.bb_ref, bf16[32,1024]{1,0:T(8,128)(2,1)S(1)} %collective-permute-done.14.bc_ref, ...), custom_call_target="tpu_custom_call" | custom-call | flops 100663296 | bytes 1769984 | tf_op jit(solution)/shard_map/last/pallas_call | solution.py:291
  (25 shorter events, 2.8 us)
Async XLA Ops:
  0.6 16.2 %copy-start.1 = (s32[128,6]{0,1:T(8,128)S(1)}, s32[128,6]{0,1:T(8,128)}, u32[]{:S(2)}) copy-start(s32[128,6]{0,1:T(8,128)} %param.15) | copy-start | bytes 9220
  0.6 9.5 %collective-permute-start.2 = (s32[3,1,32]{2,1,0:T(1,128)}, s32[3,1,32]{2,1,0:T(1,128)S(1)}, u32[]{:S(2)}, u32[]{:S(2)}) collective-permute-start(s32[3,1,32]{2,1,0:T(1,128)} %bitcast.10), channel_id=1, source_target_pairs={{0,8},{4,12},{8,0},{12,4},{1,9},{5,13},{9,1},{13,5},{2,10},{6,14},... | collective-permute-start | bytes 1160 | tf_op jit(solution)/shard_map/ppermute | solution.py:318
  4.7 5.5 %collective-permute-start.1 = (s32[3,1,32]{2,1,0:T(1,128)}, s32[3,1,32]{2,1,0:T(1,128)S(1)}, u32[]{:S(2)}, u32[]{:S(2)}) collective-permute-start(s32[3,1,32]{2,1,0:T(1,128)} %bitcast.11), channel_id=1, source_target_pairs={{4,8},{8,4},{5,9},{9,5},{6,10},{10,6},{7,11},{11,7},{20,24},{24,20... | collective-permute-start | bytes 1160 | tf_op jit(solution)/shard_map/ppermute | solution.py:318
  5.4 4.8 %collective-permute-start = (s32[3,1,32]{2,1,0:T(1,128)}, s32[3,1,32]{2,1,0:T(1,128)S(1)}, u32[]{:S(2)}, u32[]{:S(2)}) collective-permute-start(s32[3,1,32]{2,1,0:T(1,128)} %bitcast.12), channel_id=1, source_target_pairs={{0,4},{4,0},{8,12},{12,8},{1,5},{5,1},{9,13},{13,9},{2,6},{6,2},{1... | collective-permute-start | bytes 1160 | tf_op jit(solution)/shard_map/ppermute | solution.py:318
  10.6 7.6 %collective-permute-start.3 = (bf16[32,1024]{1,0:T(8,128)(2,1)S(1)}, bf16[32,1024]{1,0:T(8,128)(2,1)S(1)}, u32[]{:S(2)}, u32[]{:S(2)}) collective-permute-start(bf16[32,1024]{1,0:T(8,128)(2,1)S(1)} %get-tuple-element.29), channel_id=1, source_target_pairs={{0,4},{4,0},{8,12},{12,8},{1,5},{5,1},{9,13},{13,9},{2,6},{6,2},{1... | collective-permute-start | bytes 196616 | tf_op jit(solution)/shard_map/ppermute | solution.py:318
  12.6 5.7 %collective-permute-start.4 = (bf16[32,1024]{1,0:T(8,128)(2,1)S(1)}, bf16[32,1024]{1,0:T(8,128)(2,1)S(1)}, u32[]{:S(2)}, u32[]{:S(2)}) collective-permute-start(bf16[32,1024]{1,0:T(8,128)(2,1)S(1)} %get-tuple-element.30), channel_id=1, source_target_pairs={{4,8},{8,4},{5,9},{9,5},{6,10},{10,6},{7,11},{11,7},{20,24},{24,20... | collective-permute-start | bytes 196616 | tf_op jit(solution)/shard_map/ppermute | solution.py:318
  13.3 6.5 %collective-permute-start.5 = (bf16[32,1024]{1,0:T(8,128)(2,1)S(1)}, bf16[32,1024]{1,0:T(8,128)(2,1)S(1)}, u32[]{:S(2)}, u32[]{:S(2)}) collective-permute-start(bf16[32,1024]{1,0:T(8,128)(2,1)S(1)} %get-tuple-element.31), channel_id=1, source_target_pairs={{0,8},{4,12},{8,0},{12,4},{1,9},{5,13},{9,1},{13,5},{2,10},{6,14},... | collective-permute-start | bytes 196616 | tf_op jit(solution)/shard_map/ppermute | solution.py:318
  17.2 2.5 %copy-start.2 = (f32[128]{0:T(128)S(1)}, f32[128]{0:T(128)}, u32[]{:S(2)}) copy-start(f32[128]{0:T(128)} %param.13) | copy-start | bytes 1540
  17.2 2.5 %copy-start.3 = (f32[128]{0:T(128)S(1)}, f32[128]{0:T(128)}, u32[]{:S(2)}) copy-start(f32[128]{0:T(128)} %param.14) | copy-start | bytes 1540
  23.1 6.5 %collective-permute-start.6 = (bf16[32,1024]{1,0:T(8,128)(2,1)S(1)}, bf16[32,1024]{1,0:T(8,128)(2,1)S(1)}, u32[]{:S(2)}, u32[]{:S(2)}) collective-permute-start(bf16[32,1024]{1,0:T(8,128)(2,1)S(1)} %get-tuple-element.34), channel_id=1, source_target_pairs={{0,4},{4,0},{8,12},{12,8},{1,5},{5,1},{9,13},{13,9},{2,6},{6,2},{1... | collective-permute-start | bytes 196616 | tf_op jit(solution)/shard_map/ppermute | solution.py:318
  25.4 4.3 %collective-permute-start.7 = (bf16[32,1024]{1,0:T(8,128)(2,1)S(1)}, bf16[32,1024]{1,0:T(8,128)(2,1)S(1)}, u32[]{:S(2)}, u32[]{:S(2)}) collective-permute-start(bf16[32,1024]{1,0:T(8,128)(2,1)S(1)} %get-tuple-element.35), channel_id=1, source_target_pairs={{4,8},{8,4},{5,9},{9,5},{6,10},{10,6},{7,11},{11,7},{20,24},{24,20... | collective-permute-start | bytes 196616 | tf_op jit(solution)/shard_map/ppermute | solution.py:318
  26.0 5.7 %collective-permute-start.8 = (bf16[32,1024]{1,0:T(8,128)(2,1)S(1)}, bf16[32,1024]{1,0:T(8,128)(2,1)S(1)}, u32[]{:S(2)}, u32[]{:S(2)}) collective-permute-start(bf16[32,1024]{1,0:T(8,128)(2,1)S(1)} %get-tuple-element.36), channel_id=1, source_target_pairs={{0,8},{4,12},{8,0},{12,4},{1,9},{5,13},{9,1},{13,5},{2,10},{6,14},... | collective-permute-start | bytes 196616 | tf_op jit(solution)/shard_map/ppermute | solution.py:318
  28.8 2.9 %copy-start = (bf16[64,64]{1,0:T(8,128)(2,1)S(1)}, bf16[64,64]{1,0:T(8,128)(2,1)}, u32[]{:S(2)}) copy-start(bf16[64,64]{1,0:T(8,128)(2,1)} %jacobi_ref.1) | copy-start | bytes 24580
  32.4 7.8 %collective-permute-start.9 = (bf16[32,1024]{1,0:T(8,128)(2,1)S(1)}, bf16[32,1024]{1,0:T(8,128)(2,1)S(1)}, u32[]{:S(2)}, u32[]{:S(2)}) collective-permute-start(bf16[32,1024]{1,0:T(8,128)(2,1)S(1)} %get-tuple-element.40), channel_id=1, source_target_pairs={{0,4},{4,0},{8,12},{12,8},{1,5},{5,1},{9,13},{13,9},{2,6},{6,2},{1... | collective-permute-start | bytes 196616 | tf_op jit(solution)/shard_map/ppermute | solution.py:318
  35.8 4.5 %collective-permute-start.10 = (bf16[32,1024]{1,0:T(8,128)(2,1)S(1)}, bf16[32,1024]{1,0:T(8,128)(2,1)S(1)}, u32[]{:S(2)}, u32[]{:S(2)}) collective-permute-start(bf16[32,1024]{1,0:T(8,128)(2,1)S(1)} %get-tuple-element.41), channel_id=1, source_target_pairs={{4,8},{8,4},{5,9},{9,5},{6,10},{10,6},{7,11},{11,7},{20,24},{24,20... | collective-permute-start | bytes 196616 | tf_op jit(solution)/shard_map/ppermute | solution.py:318
  36.4 5.7 %collective-permute-start.11 = (bf16[32,1024]{1,0:T(8,128)(2,1)S(1)}, bf16[32,1024]{1,0:T(8,128)(2,1)S(1)}, u32[]{:S(2)}, u32[]{:S(2)}) collective-permute-start(bf16[32,1024]{1,0:T(8,128)(2,1)S(1)} %get-tuple-element.42), channel_id=1, source_target_pairs={{0,8},{4,12},{8,0},{12,4},{1,9},{5,13},{9,1},{13,5},{2,10},{6,14},... | collective-permute-start | bytes 196616 | tf_op jit(solution)/shard_map/ppermute | solution.py:318
  45.5 9.4 %collective-permute-start.12 = (bf16[32,1024]{1,0:T(8,128)(2,1)S(1)}, bf16[32,1024]{1,0:T(8,128)(2,1)S(1)}, u32[]{:S(2)}, u32[]{:S(2)}) collective-permute-start(bf16[32,1024]{1,0:T(8,128)(2,1)S(1)} %get-tuple-element.46), channel_id=1, source_target_pairs={{0,4},{4,0},{8,12},{12,8},{1,5},{5,1},{9,13},{13,9},{2,6},{6,2},{1... | collective-permute-start | bytes 196616 | tf_op jit(solution)/shard_map/ppermute | solution.py:318
  47.8 7.1 %collective-permute-start.13 = (bf16[32,1024]{1,0:T(8,128)(2,1)S(1)}, bf16[32,1024]{1,0:T(8,128)(2,1)S(1)}, u32[]{:S(2)}, u32[]{:S(2)}) collective-permute-start(bf16[32,1024]{1,0:T(8,128)(2,1)S(1)} %get-tuple-element.47), channel_id=1, source_target_pairs={{4,8},{8,4},{5,9},{9,5},{6,10},{10,6},{7,11},{11,7},{20,24},{24,20... | collective-permute-start | bytes 196616 | tf_op jit(solution)/shard_map/ppermute | solution.py:318
  48.5 6.5 %collective-permute-start.14 = (bf16[32,1024]{1,0:T(8,128)(2,1)S(1)}, bf16[32,1024]{1,0:T(8,128)(2,1)S(1)}, u32[]{:S(2)}, u32[]{:S(2)}) collective-permute-start(bf16[32,1024]{1,0:T(8,128)(2,1)S(1)} %get-tuple-element.48), channel_id=1, source_target_pairs={{0,8},{4,12},{8,0},{12,4},{1,9},{5,13},{9,1},{13,5},{2,10},{6,14},... | collective-permute-start | bytes 196616 | tf_op jit(solution)/shard_map/ppermute | solution.py:318

commit v3 on v2

v3 whole, which is shorter than its diff:
```python
import functools

import jax
import jax.numpy as jnp
from jax import lax
from jax.experimental import pallas as pl
from jax.experimental.pallas import tpu as pltpu
from jax.sharding import PartitionSpec as P

F32 = jnp.float32
BF16 = jnp.bfloat16
I32 = jnp.int32
LANES = 128
VMEM = pltpu.VMEM
SMEM = pltpu.SMEM
HBM = pltpu.HBM


def iota(shape, dim):
    return lax.broadcasted_iota(I32, shape, dim)


def one_hot(condition):
    return jnp.where(condition, 1.0, 0.0).astype(BF16)


def matmul(a, b):
    return jnp.dot(a, b, preferred_element_type=F32)


def column_tiles(row):
    count = row.shape[1] // LANES
    return [
        jnp.transpose(
            jnp.broadcast_to(row[:, t * LANES : (t + 1) * LANES].astype(F32), (LANES, LANES))
        )
        for t in range(count)
    ]


def block_diagonal(block, copies):
    rows, cols = block.shape
    wide = jnp.concatenate([block] * copies, axis=1)
    full = jnp.concatenate([wide] * copies, axis=0)
    shape = (rows * copies, cols * copies)
    keep = (iota(shape, 0) // rows) == (iota(shape, 1) // cols)
    return jnp.where(keep, full, jnp.zeros_like(full))


def precondition(traces_ref, scale_ref, jacobi_ref, z_ref):
    width = traces_ref.shape[1]
    block = block_diagonal(jacobi_ref[...].astype(F32), 4).astype(BF16)
    scales = column_tiles(scale_ref[...])
    step = block.shape[0]
    for start in range(0, width, step):
        product = matmul(traces_ref[:, start : start + step], block)
        for t, scale in enumerate(scales):
            part = product[t * LANES : (t + 1) * LANES, :]
            both = jnp.concatenate([scale, scale], axis=1)
            z_ref[t * LANES : (t + 1) * LANES, start : start + step] = (part * both).astype(BF16)


def swap_halves(even, odd, low):
    turn = lambda tile: pltpu.roll(tile, LANES // 2, 1)
    return jnp.where(low, even, turn(odd)), jnp.where(low, turn(even), odd)


def prepare_kernel(
    rhs_hbm, jacobi_hbm, stiff_hbm, mass_hbm, scale_hbm, z_ref, w_ref, scale_ref,
    rhs_ref, jacobi_ref, line_ref, sems
):
    half = w_ref.shape[1] // 2
    sources = (jacobi_hbm, scale_hbm, rhs_hbm, stiff_hbm, mass_hbm)
    targets = (jacobi_ref, line_ref, rhs_ref, w_ref.at[:, :half], w_ref.at[:, half:])
    copies = [
        pltpu.make_async_copy(src, dst, sems.at[i])
        for i, (src, dst) in enumerate(zip(sources, targets))
    ]
    for copy in copies:
        copy.start()
    copies[0].wait()
    copies[1].wait()
    scale_ref[...] = line_ref[...].reshape(scale_ref.shape)
    copies[2].wait()
    precondition(rhs_ref, scale_ref, jacobi_ref, z_ref)
    copies[3].wait()
    copies[4].wait()


def wanted_part(par, list_ref, colour):
    if colour == 2:
        return list_ref[2]
    return jnp.where(par == colour, list_ref[0], list_ref[1])


def padded(row):
    return jnp.concatenate([row, jnp.full((1, LANES - row.shape[1]), -1, I32)], axis=1)


def wanted_row(par, list_refs):
    parts = [wanted_part(par, ref, c) for c, ref in enumerate(list_refs)]
    return padded(jnp.concatenate(parts, axis=1))


def picked_rows(wanted, z_ref, count):
    (column,) = column_tiles(wanted)
    column = column[:count].astype(I32)
    lane = iota((count, LANES), 1)
    picks = jnp.concatenate(
        [one_hot(column == lane + t * LANES) for t in range(z_ref.shape[0] // LANES)], axis=1
    )
    return matmul(picks, z_ref[...]).astype(BF16)


def send_kernel(colour, par_ref, z_ref, list_ref, *refs):
    out_ref = refs[-1]
    wanted = padded(wanted_part(par_ref[0], list_ref, colour))
    out_ref[...] = picked_rows(wanted, z_ref, out_ref.shape[0])


def column_ids(par, faces, slots, tile, axis):
    index = iota((LANES, LANES), axis) + tile * LANES
    shift = slots * (1 - par)
    first = (index >= faces) & (index < faces + slots)
    second = (index >= faces + slots) & (index < faces + 2 * slots)
    return index + jnp.where(first, shift, 0) - jnp.where(second, shift, 0)


def tables_kernel(slots, faces, count_ref, par_ref, ids_ref, own_ref, halo_ref, spread_ref):
    par = par_ref[0]
    ids_all = jnp.where(iota(ids_ref.shape, 1) < count_ref[0], ids_ref[...], -1)
    tiles = spread_ref.shape[0] // LANES
    owned = faces // LANES
    lanes = [column_ids(par, faces, slots, t, 1) for t in range(tiles)]
    rows = [column_ids(par, faces, slots, t, 0) for t in range(tiles)]
    span = lambda i: slice(i * LANES, (i + 1) * LANES)
    for k in range(ids_ref.shape[0]):
        across = jnp.broadcast_to(ids_all[k : k + 1, :], (LANES, LANES))
        down = jnp.transpose(across.astype(F32)).astype(I32)
        for t in range(tiles):
            pick = one_hot(down == lanes[t])
            if t < owned:
                own_ref[span(k), span(t)] = pick
            else:
                halo_ref[span(k // 2), span(k % 2)] = pick
            spread_ref[span(t), span(k)] = one_hot(across == rows[t])


def gather_kernel(pick_ref, z_ref, x_ref):
    width = z_ref.shape[1]
    low = iota((LANES, LANES), 1) < LANES // 2
    for t in range(x_ref.shape[1] // LANES):
        rows = matmul(pick_ref[2 * t * LANES : 2 * (t + 1) * LANES, :], z_ref[...])
        for p in range(width // LANES):
            pair = rows[:, p * LANES : (p + 1) * LANES]
            even, odd = swap_halves(pair[:LANES], pair[LANES:], low)
            at = 2 * p * LANES
            x_ref[at : at + LANES, t * LANES : (t + 1) * LANES] = even.astype(BF16)
            x_ref[at + LANES : at + 2 * LANES, t * LANES : (t + 1) * LANES] = odd.astype(BF16)


def operator_kernel(
    pick_ref, spread_ref, own_x_ref, aa_ref, ab_ref, ac_ref, stiff_scale_ref, mass_scale_ref,
    w_ref, y_ref, ba_ref, bb_ref, bc_ref, x_ref, halo_ref
):
    slots, width = aa_ref.shape
    pairs = width // LANES
    filled = 3 * slots
    arrived = jnp.concatenate([aa_ref[...], ab_ref[...], ac_ref[...]], axis=0).astype(F32)
    low = iota((filled, LANES), 1) < LANES // 2
    zero = jnp.zeros((filled, LANES), F32)
    for first in (0, LANES):
        halo_ref[first + filled : first + LANES, :] = jnp.zeros(
            (LANES - filled, halo_ref.shape[1]), BF16
        )
    for p in range(pairs):
        tile = arrived[:, p * LANES : (p + 1) * LANES]
        turned = pltpu.roll(tile, LANES // 2, 1)
        even = slice(2 * p * LANES, (2 * p + 1) * LANES)
        odd = slice((2 * p + 1) * LANES, (2 * p + 2) * LANES)
        halo_ref[:filled, even] = jnp.where(low, tile, zero).astype(BF16)
        halo_ref[LANES : LANES + filled, even] = jnp.where(low, zero, turned).astype(BF16)
        halo_ref[:filled, odd] = jnp.where(low, turned, zero).astype(BF16)
        halo_ref[LANES : LANES + filled, odd] = jnp.where(low, zero, tile).astype(BF16)
    for t in range(x_ref.shape[1] // LANES):
        rows = matmul(pick_ref[t * LANES : (t + 1) * LANES, :], halo_ref[...]).astype(BF16)
        for s in range(2 * pairs):
            at = (slice(s * LANES, (s + 1) * LANES), slice(t * LANES, (t + 1) * LANES))
            x_ref[at] = own_x_ref[at] + rows[:, s * LANES : (s + 1) * LANES]
    (stiff_scale,) = column_tiles(stiff_scale_ref[...])
    (mass_scale,) = column_tiles(mass_scale_ref[...])
    stiff = jnp.concatenate([stiff_scale] * 2, axis=0)
    mass = jnp.concatenate([mass_scale] * 2, axis=0)
    low = iota((LANES, LANES), 1) < LANES // 2
    half = w_ref.shape[1] // 2
    for p in range(pairs):
        product = matmul(x_ref[2 * p * LANES : 2 * (p + 1) * LANES, :], w_ref[...])
        for t in range(half // LANES):
            at = t * LANES
            term = (
                stiff * product[:, at : at + LANES]
                - mass * product[:, half + at : half + at + LANES]
            )
            first, second = swap_halves(term[:LANES], term[LANES:], low)
            place = slice(p * LANES, (p + 1) * LANES)
            y_ref[2 * at : 2 * at + LANES, place] = first.astype(BF16)
            y_ref[2 * at + LANES : 2 * at + 2 * LANES, place] = second.astype(BF16)
    rows = matmul(spread_ref[spread_ref.shape[0] - LANES :, :], y_ref[...]).astype(BF16)
    for c, ref in enumerate((ba_ref, bb_ref, bc_ref)):
        ref[...] = rows[c * slots : (c + 1) * slots, :]


def own_sums(spread_ref, y_ref, own_ref):
    for t in range(own_ref.shape[0] // LANES):
        own_ref[t * LANES : (t + 1) * LANES, :] = matmul(
            spread_ref[t * LANES : (t + 1) * LANES, :], y_ref[...]
        )


def sums_kernel(spread_ref, y_ref, own_ref):
    own_sums(spread_ref, y_ref, own_ref)


def finish_kernel(
    spread_ref, y_ref, x_ref, lift_hbm, own_ref, interior_hbm, inside_ref, lift_ref, lift_sem, sems
):
    load = pltpu.make_async_copy(lift_hbm, lift_ref, lift_sem)
    load.start()
    own_sums(spread_ref, y_ref, own_ref)
    load.wait()
    wide = lift_ref.shape[1]
    step = 4
    copies = []
    for start in range(0, x_ref.shape[0] // LANES, step):
        rows = x_ref[start * LANES : (start + step) * LANES, :]
        product = matmul(rows, lift_ref[...]).astype(BF16)
        for r in range(step):
            inside_ref[:, (start + r) * wide : (start + r + 1) * wide] = product[
                r * LANES : (r + 1) * LANES, :
            ]
        span = pl.ds(start * wide, step * wide)
        copy = pltpu.make_async_copy(
            inside_ref.at[:, span], interior_hbm.at[:, span], sems.at[len(copies)]
        )
        copy.start()
        copies.append(copy)
    for copy in copies:
        copy.wait()


def gather_back(back_refs, gathered_ref):
    slots, width = back_refs[0].shape
    for c, ref in enumerate(back_refs):
        gathered_ref[c * slots : (c + 1) * slots, :] = ref[...]
    gathered_ref[3 * slots :, :] = jnp.zeros((LANES - 3 * slots, width), BF16)


def collected(own_ref, wanted, gathered_ref, tile):
    target = jnp.broadcast_to(wanted, (LANES, LANES))
    picks = one_hot(target == iota((LANES, LANES), 0) + tile * LANES)
    own = own_ref[tile * LANES : (tile + 1) * LANES, :]
    return (own + matmul(picks, gathered_ref[...])).astype(BF16)


def middle_kernel(
    par_ref, own_ref, ba_ref, bb_ref, bc_ref, la_ref, lb_ref, lc_ref, scale_ref, jacobi_ref, z_ref,
    oa_ref, ob_ref, oc_ref, gathered_ref, v_ref
):
    wanted = wanted_row(par_ref[0], [la_ref, lb_ref, lc_ref])
    gather_back([ba_ref, bb_ref, bc_ref], gathered_ref)
    for t in range(own_ref.shape[0] // LANES):
        v_ref[t * LANES : (t + 1) * LANES, :] = collected(own_ref, wanted, gathered_ref, t)
    precondition(v_ref, scale_ref, jacobi_ref, z_ref)
    rows = picked_rows(wanted, z_ref, LANES)
    slots = oa_ref.shape[0]
    for c, ref in enumerate((oa_ref, ob_ref, oc_ref)):
        ref[...] = rows[c * slots : (c + 1) * slots, :]


def last_kernel(
    par_ref, own_ref, ba_ref, bb_ref, bc_ref, la_ref, lb_ref, lc_ref, out_hbm, gathered_ref,
    out_ref, sems
):
    wanted = wanted_row(par_ref[0], [la_ref, lb_ref, lc_ref])
    gather_back([ba_ref, bb_ref, bc_ref], gathered_ref)
    copies = []
    for t in range(own_ref.shape[0] // LANES):
        span = pl.ds(t * LANES, LANES)
        out_ref[span, :] = collected(own_ref, wanted, gathered_ref, t)
        copy = pltpu.make_async_copy(out_ref.at[span, :], out_hbm.at[span, :], sems.at[t])
        copy.start()
        copies.append(copy)
    for copy in copies:
        copy.wait()


def call(kernel, operands, spaces, outs, scratch, flops, name, out_spaces=None, grant=12):
    out_spaces = out_spaces or [VMEM] * len(outs)
    moved = sum(a.size * a.dtype.itemsize for a in operands)
    return pl.pallas_call(
        kernel,
        out_shape=[jax.ShapeDtypeStruct(s, d) for s, d in outs],
        in_specs=[pl.BlockSpec(memory_space=s) for s in spaces],
        out_specs=[pl.BlockSpec(memory_space=s) for s in out_spaces],
        scratch_shapes=scratch,
        compiler_params=pltpu.CompilerParams(vmem_limit_bytes=grant * 1024 * 1024),
        cost_estimate=pl.CostEstimate(flops=flops, bytes_accessed=moved, transcendentals=0),
        name=name,
    )(*operands)


def in_hbm(array):
    return pltpu.with_memory_space_constraint(array, HBM)


def pairings(size):
    def both(pairs):
        return [pair for a, b in pairs for pair in ((a, b), (b, a))]

    even = both([(i, i + 1) for i in range(0, size - 1, 2)])
    odd = both([(i, i + 1) for i in range(1, size - 1, 2)])
    opposite = [(i, (i + size // 2) % size) for i in range(size)]
    return (even, odd, opposite)


def exchange(arrays, size):
    ways = pairings(size)
    got = {c: lax.ppermute(arrays[c], "elem", ways[c]) for c in (2, 1, 0)}
    return [got[c] for c in range(3)]


def per_device(
    size,
    trace_rhs,
    face_scale,
    stiff_scale,
    mass_scale,
    elem_faces,
    halo_faces,
    elem_count,
    jacobi_block,
    stiffness,
    mass,
    lifting,
):
    faces, width = trace_rhs.shape
    slots = halo_faces.shape[2]
    elems = elem_faces.shape[0]
    face_dofs = jacobi_block.shape[0]
    eld, inside = lifting.shape
    pairs = width // LANES
    halo_rows = LANES
    ext_rows = faces + halo_rows
    slots_all = 6 * elems
    lists = exchange([halo_faces.transpose(1, 0, 2)] * 3, size)
    par = (lax.axis_index("elem") % 2).astype(I32).reshape(1)
    stiff_row = stiff_scale.reshape(1, elems)
    mass_row = mass_scale.reshape(1, elems)
    field = ((faces, width), BF16)
    rows = [((slots, width), BF16)] * 3
    x_shape = ((2 * pairs * elems, eld), BF16)
    y_shape = ((slots_all, width), BF16)
    own_shape = ((faces, width), F32)
    element_flops = 4 * 2 * pairs * elems * eld * eld

    first, weights, scale = call(
        prepare_kernel,
        [in_hbm(a) for a in (trace_rhs, jacobi_block, stiffness, mass, face_scale)],
        [HBM] * 5,
        [field, ((eld, 2 * eld), BF16), ((1, faces), F32)],
        [
            VMEM(trace_rhs.shape, BF16),
            VMEM(jacobi_block.shape, BF16),
            VMEM(face_scale.shape, F32),
            pltpu.SemaphoreType.DMA((5,)),
        ],
        2 * faces * width * 256,
        "prepare",
    )
    outgoing = [None] * 3
    before = []
    for c in (2, 1, 0):
        (outgoing[c],) = call(
            functools.partial(send_kernel, c),
            [par, first, lists[c], *before],
            [SMEM] + [VMEM] * 2 + [pl.ANY] * len(before),
            rows[:1],
            [],
            2 * LANES * faces * width,
            f"send{c}",
        )
        before = [outgoing[c]]
    arrived = exchange(outgoing, size)
    own_pick, halo_pick, spread = call(
        functools.partial(tables_kernel, slots, faces),
        [elem_count, par, elem_faces.T],
        [SMEM, SMEM, VMEM],
        [
            ((slots_all, faces), BF16),
            ((slots_all // 2, 2 * halo_rows), BF16),
            ((ext_rows, slots_all), BF16),
        ],
        [],
        slots_all * ext_rows * 4,
        "tables",
    )

    def gather(z, name):
        (own_x,) = call(
            gather_kernel,
            [own_pick, z],
            [VMEM] * 2,
            [x_shape],
            [],
            2 * slots_all * faces * width,
            name,
        )
        return own_x

    def operator(own_x, arrived, keep_x, name):
        halo = VMEM((2 * halo_rows, 2 * width), BF16)
        return call(
            operator_kernel,
            [halo_pick, spread, own_x, *arrived, stiff_row, mass_row, weights],
            [VMEM] * 9,
            [y_shape, *rows] + ([x_shape] if keep_x else []),
            [halo] if keep_x else [VMEM(*x_shape), halo],
            element_flops,
            name,
        )

    own_x = gather(first, "gather1")
    y, *back = operator(own_x, arrived, False, "operator1")
    returned = exchange(back, size)
    (own,) = call(
        sums_kernel,
        [spread, y],
        [VMEM] * 2,
        [own_shape],
        [],
        2 * faces * slots_all * width,
        "sums1",
    )
    second, *outgoing = call(
        middle_kernel,
        [par, own, *returned, *lists, scale, jacobi_block],
        [SMEM] + [VMEM] * 9,
        [field, *rows],
        [VMEM((LANES, width), BF16), VMEM((faces, width), BF16)],
        2 * faces * width * 256,
        "middle",
    )
    arrived = exchange(outgoing, size)
    own_x = gather(second, "gather2")
    y, *back, x = operator(own_x, arrived, True, "operator2")
    returned = exchange(back, size)
    own, interior = call(
        finish_kernel,
        [spread, y, x, in_hbm(lifting)],
        [VMEM] * 3 + [HBM],
        [own_shape, ((elems, width // face_dofs * inside), BF16)],
        [
            VMEM((elems, width // face_dofs * inside), BF16),
            VMEM(lifting.shape, BF16),
            pltpu.SemaphoreType.DMA,
            pltpu.SemaphoreType.DMA((pairs // 2,)),
        ],
        4 * pairs * elems * eld * inside,
        "finish",
        [VMEM, HBM],
    )
    (applied,) = call(
        last_kernel,
        [par, own, *returned, *lists],
        [SMEM] + [VMEM] * 7,
        [field],
        [
            VMEM((LANES, width), BF16),
            VMEM((faces, width), BF16),
            pltpu.SemaphoreType.DMA((faces // LANES,)),
        ],
        2 * faces * width * 128,
        "last",
        [HBM],
    )
    return (applied, interior)


def solution(mesh):
    rows = P(("grp", "elem", "sub"))
    split = P(("grp", "elem", "sub"), "src")
    in_specs = (
        split,
        rows,
        rows,
        rows,
        P(("grp", "elem", "sub"), None),
        P(("grp", "elem", "sub"), None, None),
        rows,
        P(),
        P(),
        P(),
        P(),
    )
    return jax.shard_map(
        functools.partial(per_device, mesh.shape["elem"]),
        mesh=mesh,
        in_specs=in_specs,
        out_specs=(split, split),
        check_vma=False,
    )
```

time: 56.5 us -> 55.3 us (0.979)
  Pallas kernels: 17.9 us -> 16.5 us
    pallas_call x11 -> x13, Pallas kernels: 17.9 us -> 16.5 us  [call(): pl.pallas_call(kernel, out_shape=[jax.ShapeDtypeStruct(s, d) for s, d in...]
  transfers between devices with their start and end apart: 15 -> 15, of which waited for: 3 -> 3; matrix products, arithmetic and copies ran while one was open for 0% -> 0% of each run, Pallas kernels for 15% -> 16%
where the time goes in v3:
time: 55.3 us; the launch traced here: 55.1 us
  starting transfers between devices  31.7 us (57%)
  Pallas kernels  16.5 us (30%)
  waiting for transfers between devices  5.26 us (10%)
  between operations  1.53 us (3%)
    ppermute x15, starting transfers between devices, exchange(): got = {c: lax.ppermute(arrays[c], 'elem', ways[c]) for c in (2, 1, 0)}  31.7 us
    pallas_call x13, Pallas kernels, call(): pl.pallas_call(kernel, out_shape=[jax.ShapeDtypeStruct(s, d) for s, d in...  16.5 us
    ppermute x15, waiting for transfers between devices, exchange(): got = {c: lax.ppermute(arrays[c], 'elem', ways[c]) for c in (2, 1, 0)}  5.26 us
  transfers between devices with their start and end apart: 15, of which 3 were waited for; matrix products, arithmetic and copies ran while one was open for 0% of the time, Pallas kernels for 16%

profile of v3, /device:TPU:0, one launch (start us, length us, event | category | flops | bytes accessed | tf_op | source)
XLA Modules:
  0.0 55.1 jit_solution(17964038832627714218)
XLA Ops:
  0.6 4.1 %collective-permute-start.2 = (s32[3,1,32]{2,1,0:T(1,128)}, s32[3,1,32]{2,1,0:T(1,128)S(1)}, u32[]{:S(2)}, u32[]{:S(2)}) collective-permute-start(s32[3,1,32]{2,1,0:T(1,128)} %bitcast.10), channel_id=1, source_target_pairs={{0,8},{4,12},{8,0},{12,4},{1,9},{5,13},{9,1},{13,5},{2,10},{6,14},... | collective-permute-start | bytes 1160 | tf_op jit(solution)/shard_map/ppermute | solution.py:328
  5.4 2.9 %collective-permute-start = (s32[3,1,32]{2,1,0:T(1,128)}, s32[3,1,32]{2,1,0:T(1,128)S(1)}, u32[]{:S(2)}, u32[]{:S(2)}) collective-permute-start(s32[3,1,32]{2,1,0:T(1,128)} %bitcast.12), channel_id=1, source_target_pairs={{0,4},{4,0},{8,12},{12,8},{1,5},{5,1},{9,13},{13,9},{2,6},{6,2},{1... | collective-permute-start | bytes 1160 | tf_op jit(solution)/shard_map/ppermute | solution.py:328
  8.3 1.7 %prepare.1 = (bf16[384,1024]{1,0:T(8,128)(2,1)S(1)}, bf16[384,768]{1,0:T(8,128)(2,1)S(1)}, f32[1,384]{1,0:T(1,128)S(1)}) custom-call(bf16[384,1024]{1,0:T(8,128)(2,1)} %rhs_hbm.1, bf16[64,64]{1,0:T(8,128)(2,1)} %jacobi_ref.1, bf16[384,384]{1,0:T(8,128)(2,1)} %stiff_hbm.1, bf16[384,384]{1,0:T(8,128)(2,1)} %mass_hbm.1, f32[384]{0:T(512)} %scale_hbm.1), custom_call_target="tpu_custom_call" | custom-call | flops 201326592 | bytes 1385984 | tf_op jit(solution)/shard_map/prepare/pallas_call | solution.py:300
  10.9 1.8 %collective-permute-start.3 = (bf16[32,1024]{1,0:T(8,128)(2,1)S(1)}, bf16[32,1024]{1,0:T(8,128)(2,1)S(1)}, u32[]{:S(2)}, u32[]{:S(2)}) collective-permute-start(bf16[32,1024]{1,0:T(8,128)(2,1)S(1)} %send0.1), channel_id=1, source_target_pairs={{0,4},{4,0},{8,12},{12,8},{1,5},{5,1},{9,13},{13,9},{2,6},{6,2},{1... | collective-permute-start | bytes 196616 | tf_op jit(solution)/shard_map/ppermute | solution.py:328
  12.7 0.7 %collective-permute-start.4 = (bf16[32,1024]{1,0:T(8,128)(2,1)S(1)}, bf16[32,1024]{1,0:T(8,128)(2,1)S(1)}, u32[]{:S(2)}, u32[]{:S(2)}) collective-permute-start(bf16[32,1024]{1,0:T(8,128)(2,1)S(1)} %send1.1.refs_0_), channel_id=1, source_target_pairs={{4,8},{8,4},{5,9},{9,5},{6,10},{10,6},{7,11},{11,7},{20,24},{24,20... | collective-permute-start | bytes 196616 | tf_op jit(solution)/shard_map/ppermute | solution.py:328
  13.3 3.1 %collective-permute-start.5 = (bf16[32,1024]{1,0:T(8,128)(2,1)S(1)}, bf16[32,1024]{1,0:T(8,128)(2,1)S(1)}, u32[]{:S(2)}, u32[]{:S(2)}) collective-permute-start(bf16[32,1024]{1,0:T(8,128)(2,1)S(1)} %send2.1.refs_0_), channel_id=1, source_target_pairs={{0,8},{4,12},{8,0},{12,4},{1,9},{5,13},{9,1},{13,5},{2,10},{6,14},... | collective-permute-start | bytes 196616 | tf_op jit(solution)/shard_map/ppermute | solution.py:328
  17.5 1.1 %gather1.1.own_x_ref = bf16[2048,384]{1,0:T(8,128)(2,1)S(1)} custom-call(bf16[768,384]{1,0:T(8,128)(2,1)S(1)} %get-tuple-element.25.pick_ref, bf16[384,1024]{1,0:T(8,128)(2,1)S(1)} %get-tuple-element.26.z_ref), custom_call_target="tpu_custom_call" | custom-call | flops 603979776 | bytes 1376256 | tf_op jit(solution)/shard_map/gather1/pallas_call | solution.py:300
  18.6 1.4 %collective-permute-done.5.ac_ref = bf16[32,1024]{1,0:T(8,128)(2,1)S(1)} collective-permute-done((bf16[32,1024]{1,0:T(8,128)(2,1)S(1)}, bf16[32,1024]{1,0:T(8,128)(2,1)S(1)}, u32[]{:S(2)}, u32[]{:S(2)}) %collective-permute-start.5) | collective-permute-done | bytes 65568 | tf_op jit(solution)/shard_map/ppermute | solution.py:328
  20.0 2.8 %operator1.1 = (bf16[768,1024]{1,0:T(8,128)(2,1)S(1)}, bf16[32,1024]{1,0:T(8,128)(2,1)S(1)}, bf16[32,1024]{1,0:T(8,128)(2,1)S(1)}, bf16[32,1024]{1,0:T(8,128)(2,1)S(1)}) custom-call(bf16[384,256]{1,0:T(8,128)(2,1)S(1)} %get-tuple-element.24.pick_ref, bf16[512,768]{1,0:T(8,128)(2,1)S(1)} %get-tuple-element.23.spread_ref, ...), custom_call_target="tpu_custom_call" | custom-call | flops 1207959552 | bytes 3343360 | tf_op jit(solution)/shard_map/operator1/pallas_call | solution.py:300
  22.8 2.2 %collective-permute-start.6 = (bf16[32,1024]{1,0:T(8,128)(2,1)S(1)}, bf16[32,1024]{1,0:T(8,128)(2,1)S(1)}, u32[]{:S(2)}, u32[]{:S(2)}) collective-permute-start(bf16[32,1024]{1,0:T(8,128)(2,1)S(1)} %get-tuple-element.29), channel_id=1, source_target_pairs={{0,4},{4,0},{8,12},{12,8},{1,5},{5,1},{9,13},{13,9},{2,6},{6,2},{1... | collective-permute-start | bytes 196616 | tf_op jit(solution)/shard_map/ppermute | solution.py:328
  25.0 0.7 %collective-permute-start.7 = (bf16[32,1024]{1,0:T(8,128)(2,1)S(1)}, bf16[32,1024]{1,0:T(8,128)(2,1)S(1)}, u32[]{:S(2)}, u32[]{:S(2)}) collective-permute-start(bf16[32,1024]{1,0:T(8,128)(2,1)S(1)} %get-tuple-element.30), channel_id=1, source_target_pairs={{4,8},{8,4},{5,9},{9,5},{6,10},{10,6},{7,11},{11,7},{20,24},{24,20... | collective-permute-start | bytes 196616 | tf_op jit(solution)/shard_map/ppermute | solution.py:328
  25.7 2.8 %collective-permute-start.8 = (bf16[32,1024]{1,0:T(8,128)(2,1)S(1)}, bf16[32,1024]{1,0:T(8,128)(2,1)S(1)}, u32[]{:S(2)}, u32[]{:S(2)}) collective-permute-start(bf16[32,1024]{1,0:T(8,128)(2,1)S(1)} %get-tuple-element.31), channel_id=1, source_target_pairs={{0,8},{4,12},{8,0},{12,4},{1,9},{5,13},{9,1},{13,5},{2,10},{6,14},... | collective-permute-start | bytes 196616 | tf_op jit(solution)/shard_map/ppermute | solution.py:328
  28.5 0.8 %sums1.1.own_ref = f32[384,1024]{1,0:T(8,128)S(1)} custom-call(bf16[512,768]{1,0:T(8,128)(2,1)S(1)} %get-tuple-element.23.spread_ref, bf16[768,1024]{1,0:T(8,128)(2,1)S(1)} %get-tuple-element.28.y_ref), custom_call_target="tpu_custom_call" | custom-call | flops 603979776 | bytes 2359296 | tf_op jit(solution)/shard_map/sums1/pallas_call | solution.py:300
  29.3 2.0 %collective-permute-done.8.bc_ref = bf16[32,1024]{1,0:T(8,128)(2,1)S(1)} collective-permute-done((bf16[32,1024]{1,0:T(8,128)(2,1)S(1)}, bf16[32,1024]{1,0:T(8,128)(2,1)S(1)}, u32[]{:S(2)}, u32[]{:S(2)}) %collective-permute-start.8) | collective-permute-done | bytes 65568 | tf_op jit(solution)/shard_map/ppermute | solution.py:328
  31.3 0.8 %middle.1 = (bf16[384,1024]{1,0:T(8,128)(2,1)S(1)}, bf16[32,1024]{1,0:T(8,128)(2,1)S(1)}, bf16[32,1024]{1,0:T(8,128)(2,1)S(1)}, bf16[32,1024]{1,0:T(8,128)(2,1)S(1)}) custom-call(s32[1]{0:T(128)} %bitcast.par_ref, f32[384,1024]{1,0:T(8,128)S(1)} %sums1.1.own_ref, bf16[32,1024]{1,0:T(8,128)(2,1)S(1)} %collective-permute-done.6.ba_ref, ...), custom_call_target="tpu_custom_call" | custom-call | flops 201326592 | bytes 1780356 | tf_op jit(solution)/shard_map/middle/pallas_call | solution.py:300
  32.1 3.3 %collective-permute-start.9 = (bf16[32,1024]{1,0:T(8,128)(2,1)S(1)}, bf16[32,1024]{1,0:T(8,128)(2,1)S(1)}, u32[]{:S(2)}, u32[]{:S(2)}) collective-permute-start(bf16[32,1024]{1,0:T(8,128)(2,1)S(1)} %get-tuple-element.34), channel_id=1, source_target_pairs={{0,4},{4,0},{8,12},{12,8},{1,5},{5,1},{9,13},{13,9},{2,6},{6,2},{1... | collective-permute-start | bytes 196616 | tf_op jit(solution)/shard_map/ppermute | solution.py:328
  36.1 2.8 %collective-permute-start.11 = (bf16[32,1024]{1,0:T(8,128)(2,1)S(1)}, bf16[32,1024]{1,0:T(8,128)(2,1)S(1)}, u32[]{:S(2)}, u32[]{:S(2)}) collective-permute-start(bf16[32,1024]{1,0:T(8,128)(2,1)S(1)} %get-tuple-element.36), channel_id=1, source_target_pairs={{0,8},{4,12},{8,0},{12,4},{1,9},{5,13},{9,1},{13,5},{2,10},{6,14},... | collective-permute-start | bytes 196616 | tf_op jit(solution)/shard_map/ppermute | solution.py:328
  38.9 1.1 %gather2.1.own_x_ref = bf16[2048,384]{1,0:T(8,128)(2,1)S(1)} custom-call(bf16[768,384]{1,0:T(8,128)(2,1)S(1)} %get-tuple-element.25.pick_ref, bf16[384,1024]{1,0:T(8,128)(2,1)S(1)} %get-tuple-element.33.z_ref), custom_call_target="tpu_custom_call" | custom-call | flops 603979776 | bytes 1376256 | tf_op jit(solution)/shard_map/gather2/pallas_call | solution.py:300
  40.0 1.8 %collective-permute-done.11.ac_ref = bf16[32,1024]{1,0:T(8,128)(2,1)S(1)} collective-permute-done((bf16[32,1024]{1,0:T(8,128)(2,1)S(1)}, bf16[32,1024]{1,0:T(8,128)(2,1)S(1)}, u32[]{:S(2)}, u32[]{:S(2)}) %collective-permute-start.11) | collective-permute-done | bytes 65568 | tf_op jit(solution)/shard_map/ppermute | solution.py:328
  41.8 2.9 %operator2.1 = (bf16[768,1024]{1,0:T(8,128)(2,1)S(1)}, bf16[32,1024]{1,0:T(8,128)(2,1)S(1)}, bf16[32,1024]{1,0:T(8,128)(2,1)S(1)}, bf16[32,1024]{1,0:T(8,128)(2,1)S(1)}, bf16[2048,384]{1,0:T(8,128)(2,1)S(1)}) custom-call(bf16[384,256]{1,0:T(8,128)(2,1)S(1)} %get-tuple-element.24.pick_ref, bf16[512,768]{1,0:T(8,128)(2,1)S(1)} %get-tuple-element.23.spread_ref, ...), custom_call_target="tpu_custom_call" | custom-call | flops 1207959552 | bytes 3343360 | tf_op jit(solution)/shard_map/operator2/pallas_call | solution.py:300
  44.7 2.6 %collective-permute-start.12 = (bf16[32,1024]{1,0:T(8,128)(2,1)S(1)}, bf16[32,1024]{1,0:T(8,128)(2,1)S(1)}, u32[]{:S(2)}, u32[]{:S(2)}) collective-permute-start(bf16[32,1024]{1,0:T(8,128)(2,1)S(1)} %get-tuple-element.40), channel_id=1, source_target_pairs={{0,4},{4,0},{8,12},{12,8},{1,5},{5,1},{9,13},{13,9},{2,6},{6,2},{1... | collective-permute-start | bytes 196616 | tf_op jit(solution)/shard_map/ppermute | solution.py:328
  47.9 2.8 %collective-permute-start.14 = (bf16[32,1024]{1,0:T(8,128)(2,1)S(1)}, bf16[32,1024]{1,0:T(8,128)(2,1)S(1)}, u32[]{:S(2)}, u32[]{:S(2)}) collective-permute-start(bf16[32,1024]{1,0:T(8,128)(2,1)S(1)} %get-tuple-element.42), channel_id=1, source_target_pairs={{0,8},{4,12},{8,0},{12,4},{1,9},{5,13},{9,1},{13,5},{2,10},{6,14},... | collective-permute-start | bytes 196616 | tf_op jit(solution)/shard_map/ppermute | solution.py:328
  50.7 3.1 %finish.1 = (f32[384,1024]{1,0:T(8,128)S(1)}, bf16[128,8192]{1,0:T(8,128)(2,1)}) custom-call(bf16[512,768]{1,0:T(8,128)(2,1)S(1)} %get-tuple-element.23.spread_ref, bf16[768,1024]{1,0:T(8,128)(2,1)S(1)} %get-tuple-element.37.y_ref, bf16[2048,384]{1,0:T(8,128)(2,1)S(1)} %get-tuple-element.38.x_ref, bf16[384,512]{1,0:T(8,128)(2,1)} %lift_hbm.1), custom_call_target="tpu_custom_call" | custom-call | flops 805306368 | bytes 4325376 | tf_op jit(solution)/shard_map/finish/pallas_call | solution.py:300
  53.9 1.2 %last.1 = bf16[384,1024]{1,0:T(8,128)(2,1)} custom-call(s32[1]{0:T(128)} %bitcast.par_ref, f32[384,1024]{1,0:T(8,128)S(1)} %get-tuple-element.39.own_ref, bf16[32,1024]{1,0:T(8,128)(2,1)S(1)} %collective-permute-done.12.ba_ref, bf16[32,1024]{1,0:T(8,128)(2,1)S(1)} %collective-permute-done.13.bb_ref, bf16[32,1024]{1,0:T(8,128)(2,1)S(1)} %collective-permute-done.14.bc_ref, ...), custom_call_target="tpu_custom_call" | custom-call | flops 100663296 | bytes 1770628 | tf_op jit(solution)/shard_map/last/pallas_call | solution.py:300
  (27 shorter events, 3.3 us)
Async XLA Ops:
  0.6 9.4 %collective-permute-start.2 = (s32[3,1,32]{2,1,0:T(1,128)}, s32[3,1,32]{2,1,0:T(1,128)S(1)}, u32[]{:S(2)}, u32[]{:S(2)}) collective-permute-start(s32[3,1,32]{2,1,0:T(1,128)} %bitcast.10), channel_id=1, source_target_pairs={{0,8},{4,12},{8,0},{12,4},{1,9},{5,13},{9,1},{13,5},{2,10},{6,14},... | collective-permute-start | bytes 1160 | tf_op jit(solution)/shard_map/ppermute | solution.py:328
  4.7 5.6 %collective-permute-start.1 = (s32[3,1,32]{2,1,0:T(1,128)}, s32[3,1,32]{2,1,0:T(1,128)S(1)}, u32[]{:S(2)}, u32[]{:S(2)}) collective-permute-start(s32[3,1,32]{2,1,0:T(1,128)} %bitcast.11), channel_id=1, source_target_pairs={{4,8},{8,4},{5,9},{9,5},{6,10},{10,6},{7,11},{11,7},{20,24},{24,20... | collective-permute-start | bytes 1160 | tf_op jit(solution)/shard_map/ppermute | solution.py:328
  5.4 5.2 %collective-permute-start = (s32[3,1,32]{2,1,0:T(1,128)}, s32[3,1,32]{2,1,0:T(1,128)S(1)}, u32[]{:S(2)}, u32[]{:S(2)}) collective-permute-start(s32[3,1,32]{2,1,0:T(1,128)} %bitcast.12), channel_id=1, source_target_pairs={{0,4},{4,0},{8,12},{12,8},{1,5},{5,1},{9,13},{13,9},{2,6},{6,2},{1... | collective-permute-start | bytes 1160 | tf_op jit(solution)/shard_map/ppermute | solution.py:328
  10.0 7.1 %copy-start.1 = (s32[128,6]{0,1:T(8,128)S(1)}, s32[128,6]{0,1:T(8,128)}, u32[]{:S(2)}) copy-start(s32[128,6]{0,1:T(8,128)} %param.15) | copy-start | bytes 9220
  10.9 9.1 %copy-start.2 = (f32[128]{0:T(128)S(1)}, f32[128]{0:T(128)}, u32[]{:S(2)}) copy-start(f32[128]{0:T(128)} %param.13) | copy-start | bytes 1540
  10.9 9.1 %copy-start.3 = (f32[128]{0:T(128)S(1)}, f32[128]{0:T(128)}, u32[]{:S(2)}) copy-start(f32[128]{0:T(128)} %param.14) | copy-start | bytes 1540
  10.9 7.7 %collective-permute-start.3 = (bf16[32,1024]{1,0:T(8,128)(2,1)S(1)}, bf16[32,1024]{1,0:T(8,128)(2,1)S(1)}, u32[]{:S(2)}, u32[]{:S(2)}) collective-permute-start(bf16[32,1024]{1,0:T(8,128)(2,1)S(1)} %send0.1), channel_id=1, source_target_pairs={{0,4},{4,0},{8,12},{12,8},{1,5},{5,1},{9,13},{13,9},{2,6},{6,2},{1... | collective-permute-start | bytes 196616 | tf_op jit(solution)/shard_map/ppermute | solution.py:328
  12.7 5.9 %collective-permute-start.4 = (bf16[32,1024]{1,0:T(8,128)(2,1)S(1)}, bf16[32,1024]{1,0:T(8,128)(2,1)S(1)}, u32[]{:S(2)}, u32[]{:S(2)}) collective-permute-start(bf16[32,1024]{1,0:T(8,128)(2,1)S(1)} %send1.1.refs_0_), channel_id=1, source_target_pairs={{4,8},{8,4},{5,9},{9,5},{6,10},{10,6},{7,11},{11,7},{20,24},{24,20... | collective-permute-start | bytes 196616 | tf_op jit(solution)/shard_map/ppermute | solution.py:328
  13.3 6.7 %collective-permute-start.5 = (bf16[32,1024]{1,0:T(8,128)(2,1)S(1)}, bf16[32,1024]{1,0:T(8,128)(2,1)S(1)}, u32[]{:S(2)}, u32[]{:S(2)}) collective-permute-start(bf16[32,1024]{1,0:T(8,128)(2,1)S(1)} %send2.1.refs_0_), channel_id=1, source_target_pairs={{0,8},{4,12},{8,0},{12,4},{1,9},{5,13},{9,1},{13,5},{2,10},{6,14},... | collective-permute-start | bytes 196616 | tf_op jit(solution)/shard_map/ppermute | solution.py:328
  22.8 6.5 %collective-permute-start.6 = (bf16[32,1024]{1,0:T(8,128)(2,1)S(1)}, bf16[32,1024]{1,0:T(8,128)(2,1)S(1)}, u32[]{:S(2)}, u32[]{:S(2)}) collective-permute-start(bf16[32,1024]{1,0:T(8,128)(2,1)S(1)} %get-tuple-element.29), channel_id=1, source_target_pairs={{0,4},{4,0},{8,12},{12,8},{1,5},{5,1},{9,13},{13,9},{2,6},{6,2},{1... | collective-permute-start | bytes 196616 | tf_op jit(solution)/shard_map/ppermute | solution.py:328
  25.0 4.3 %collective-permute-start.7 = (bf16[32,1024]{1,0:T(8,128)(2,1)S(1)}, bf16[32,1024]{1,0:T(8,128)(2,1)S(1)}, u32[]{:S(2)}, u32[]{:S(2)}) collective-permute-start(bf16[32,1024]{1,0:T(8,128)(2,1)S(1)} %get-tuple-element.30), channel_id=1, source_target_pairs={{4,8},{8,4},{5,9},{9,5},{6,10},{10,6},{7,11},{11,7},{20,24},{24,20... | collective-permute-start | bytes 196616 | tf_op jit(solution)/shard_map/ppermute | solution.py:328
  25.7 5.7 %collective-permute-start.8 = (bf16[32,1024]{1,0:T(8,128)(2,1)S(1)}, bf16[32,1024]{1,0:T(8,128)(2,1)S(1)}, u32[]{:S(2)}, u32[]{:S(2)}) collective-permute-start(bf16[32,1024]{1,0:T(8,128)(2,1)S(1)} %get-tuple-element.31), channel_id=1, source_target_pairs={{0,8},{4,12},{8,0},{12,4},{1,9},{5,13},{9,1},{13,5},{2,10},{6,14},... | collective-permute-start | bytes 196616 | tf_op jit(solution)/shard_map/ppermute | solution.py:328
  28.5 2.9 %copy-start = (bf16[64,64]{1,0:T(8,128)(2,1)S(1)}, bf16[64,64]{1,0:T(8,128)(2,1)}, u32[]{:S(2)}) copy-start(bf16[64,64]{1,0:T(8,128)(2,1)} %jacobi_ref.1) | copy-start | bytes 24580
  32.1 7.8 %collective-permute-start.9 = (bf16[32,1024]{1,0:T(8,128)(2,1)S(1)}, bf16[32,1024]{1,0:T(8,128)(2,1)S(1)}, u32[]{:S(2)}, u32[]{:S(2)}) collective-permute-start(bf16[32,1024]{1,0:T(8,128)(2,1)S(1)} %get-tuple-element.34), channel_id=1, source_target_pairs={{0,4},{4,0},{8,12},{12,8},{1,5},{5,1},{9,13},{13,9},{2,6},{6,2},{1... | collective-permute-start | bytes 196616 | tf_op jit(solution)/shard_map/ppermute | solution.py:328
  35.4 4.5 %collective-permute-start.10 = (bf16[32,1024]{1,0:T(8,128)(2,1)S(1)}, bf16[32,1024]{1,0:T(8,128)(2,1)S(1)}, u32[]{:S(2)}, u32[]{:S(2)}) collective-permute-start(bf16[32,1024]{1,0:T(8,128)(2,1)S(1)} %get-tuple-element.35), channel_id=1, source_target_pairs={{4,8},{8,4},{5,9},{9,5},{6,10},{10,6},{7,11},{11,7},{20,24},{24,20... | collective-permute-start | bytes 196616 | tf_op jit(solution)/shard_map/ppermute | solution.py:328
  36.1 5.7 %collective-permute-start.11 = (bf16[32,1024]{1,0:T(8,128)(2,1)S(1)}, bf16[32,1024]{1,0:T(8,128)(2,1)S(1)}, u32[]{:S(2)}, u32[]{:S(2)}) collective-permute-start(bf16[32,1024]{1,0:T(8,128)(2,1)S(1)} %get-tuple-element.36), channel_id=1, source_target_pairs={{0,8},{4,12},{8,0},{12,4},{1,9},{5,13},{9,1},{13,5},{2,10},{6,14},... | collective-permute-start | bytes 196616 | tf_op jit(solution)/shard_map/ppermute | solution.py:328
  44.7 9.2 %collective-permute-start.12 = (bf16[32,1024]{1,0:T(8,128)(2,1)S(1)}, bf16[32,1024]{1,0:T(8,128)(2,1)S(1)}, u32[]{:S(2)}, u32[]{:S(2)}) collective-permute-start(bf16[32,1024]{1,0:T(8,128)(2,1)S(1)} %get-tuple-element.40), channel_id=1, source_target_pairs={{0,4},{4,0},{8,12},{12,8},{1,5},{5,1},{9,13},{13,9},{2,6},{6,2},{1... | collective-permute-start | bytes 196616 | tf_op jit(solution)/shard_map/ppermute | solution.py:328
  47.3 6.6 %collective-permute-start.13 = (bf16[32,1024]{1,0:T(8,128)(2,1)S(1)}, bf16[32,1024]{1,0:T(8,128)(2,1)S(1)}, u32[]{:S(2)}, u32[]{:S(2)}) collective-permute-start(bf16[32,1024]{1,0:T(8,128)(2,1)S(1)} %get-tuple-element.41), channel_id=1, source_target_pairs={{4,8},{8,4},{5,9},{9,5},{6,10},{10,6},{7,11},{11,7},{20,24},{24,20... | collective-permute-start | bytes 196616 | tf_op jit(solution)/shard_map/ppermute | solution.py:328
  47.9 5.9 %collective-permute-start.14 = (bf16[32,1024]{1,0:T(8,128)(2,1)S(1)}, bf16[32,1024]{1,0:T(8,128)(2,1)S(1)}, u32[]{:S(2)}, u32[]{:S(2)}) collective-permute-start(bf16[32,1024]{1,0:T(8,128)(2,1)S(1)} %get-tuple-element.42), channel_id=1, source_target_pairs={{0,8},{4,12},{8,0},{12,4},{1,9},{5,13},{9,1},{13,5},{2,10},{6,14},... | collective-permute-start | bytes 196616 | tf_op jit(solution)/shard_map/ppermute | solution.py:328

commit v4 on v3

--- a/solution.py
+++ b/solution.py
@@ -88,9 +88,9 @@
 
 
 def wanted_part(par, list_ref, colour):
-    if colour == 2:
+    if colour == 0:
         return list_ref[2]
-    return jnp.where(par == colour, list_ref[0], list_ref[1])
+    return jnp.where(par == 2 - colour, list_ref[0], list_ref[1])
 
 
 def padded(row):
@@ -102,28 +102,28 @@
     return padded(jnp.concatenate(parts, axis=1))
 
 
-def picked_rows(wanted, z_ref, count):
+def send_rows(wanted, z_ref, out_refs):
     (column,) = column_tiles(wanted)
-    column = column[:count].astype(I32)
-    lane = iota((count, LANES), 1)
+    column = column.astype(I32)
+    lane = iota((LANES, LANES), 1)
     picks = jnp.concatenate(
         [one_hot(column == lane + t * LANES) for t in range(z_ref.shape[0] // LANES)], axis=1
     )
-    return matmul(picks, z_ref[...]).astype(BF16)
-
-
-def send_kernel(colour, par_ref, z_ref, list_ref, *refs):
-    out_ref = refs[-1]
-    wanted = padded(wanted_part(par_ref[0], list_ref, colour))
-    out_ref[...] = picked_rows(wanted, z_ref, out_ref.shape[0])
+    rows = matmul(picks, z_ref[...]).astype(BF16)
+    slots = out_refs[0].shape[0]
+    for c, ref in enumerate(out_refs):
+        ref[...] = rows[c * slots : (c + 1) * slots, :]
+
+
+def send_kernel(par_ref, z_ref, la_ref, lb_ref, lc_ref, *out_refs):
+    send_rows(wanted_row(par_ref[0], [la_ref, lb_ref, lc_ref]), z_ref, out_refs)
 
 
 def column_ids(par, faces, slots, tile, axis):
     index = iota((LANES, LANES), axis) + tile * LANES
-    shift = slots * (1 - par)
-    first = (index >= faces) & (index < faces + slots)
-    second = (index >= faces + slots) & (index < faces + 2 * slots)
-    return index + jnp.where(first, shift, 0) - jnp.where(second, shift, 0)
+    moved = jnp.where(index < faces + slots, 2 * slots, slots * par - slots)
+    moved = jnp.where(index < faces + 2 * slots, moved, -slots - slots * par)
+    return jnp.where(index < faces, index, index + moved)
 
 
 def tables_kernel(slots, faces, count_ref, par_ref, ids_ref, own_ref, halo_ref, spread_ref):
@@ -144,6 +144,13 @@
             else:
                 halo_ref[span(k // 2), span(k % 2)] = pick
             spread_ref[span(t), span(k)] = one_hot(across == rows[t])
+
+
+def gather_lift_kernel(pick_ref, z_ref, lift_hbm, x_ref, lift_ref, sem):
+    load = pltpu.make_async_copy(lift_hbm, lift_ref, sem)
+    load.start()
+    gather_kernel(pick_ref, z_ref, x_ref)
+    load.wait()
 
 
 def gather_kernel(pick_ref, z_ref, x_ref):
@@ -222,12 +229,8 @@
 
 
 def finish_kernel(
-    spread_ref, y_ref, x_ref, lift_hbm, own_ref, interior_hbm, inside_ref, lift_ref, lift_sem, sems
+    spread_ref, y_ref, x_ref, lift_ref, own_ref, interior_hbm, inside_ref, sems
 ):
-    load = pltpu.make_async_copy(lift_hbm, lift_ref, lift_sem)
-    load.start()
-    own_sums(spread_ref, y_ref, own_ref)
-    load.wait()
     wide = lift_ref.shape[1]
     step = 4
     copies = []
@@ -244,6 +247,7 @@
         )
         copy.start()
         copies.append(copy)
+    own_sums(spread_ref, y_ref, own_ref)
     for copy in copies:
         copy.wait()
 
@@ -271,10 +275,7 @@
     for t in range(own_ref.shape[0] // LANES):
         v_ref[t * LANES : (t + 1) * LANES, :] = collected(own_ref, wanted, gathered_ref, t)
     precondition(v_ref, scale_ref, jacobi_ref, z_ref)
-    rows = picked_rows(wanted, z_ref, LANES)
-    slots = oa_ref.shape[0]
-    for c, ref in enumerate((oa_ref, ob_ref, oc_ref)):
-        ref[...] = rows[c * slots : (c + 1) * slots, :]
+    send_rows(wanted, z_ref, [oa_ref, ob_ref, oc_ref])
 
 
 def last_kernel(
@@ -320,12 +321,13 @@
     even = both([(i, i + 1) for i in range(0, size - 1, 2)])
     odd = both([(i, i + 1) for i in range(1, size - 1, 2)])
     opposite = [(i, (i + size // 2) % size) for i in range(size)]
-    return (even, odd, opposite)
-
-
-def exchange(arrays, size):
+    return (opposite, odd, even)
+
+
+def exchange(arrays, size, reverse=False):
     ways = pairings(size)
-    got = {c: lax.ppermute(arrays[c], "elem", ways[c]) for c in (2, 1, 0)}
+    order = (2, 1, 0) if reverse else (0, 1, 2)
+    got = {c: lax.ppermute(arrays[c], "elem", ways[c]) for c in order}
     return [got[c] for c in range(3)]
 
 
@@ -352,7 +354,7 @@
     halo_rows = LANES
     ext_rows = faces + halo_rows
     slots_all = 6 * elems
-    lists = exchange([halo_faces.transpose(1, 0, 2)] * 3, size)
+    lists = exchange([halo_faces.transpose(1, 0, 2)] * 3, size, reverse=True)
     par = (lax.axis_index("elem") % 2).astype(I32).reshape(1)
     stiff_row = stiff_scale.reshape(1, elems)
     mass_row = mass_scale.reshape(1, elems)
@@ -377,19 +379,15 @@
         2 * faces * width * 256,
         "prepare",
     )
-    outgoing = [None] * 3
-    before = []
-    for c in (2, 1, 0):
-        (outgoing[c],) = call(
-            functools.partial(send_kernel, c),
-            [par, first, lists[c], *before],
-            [SMEM] + [VMEM] * 2 + [pl.ANY] * len(before),
-            rows[:1],
-            [],
-            2 * LANES * faces * width,
-            f"send{c}",
-        )
-        before = [outgoing[c]]
+    outgoing = call(
+        send_kernel,
+        [par, first, *lists],
+        [SMEM] + [VMEM] * 4,
+        rows,
+        [],
+        2 * LANES * faces * width,
+        "send",
+    )
     arrived = exchange(outgoing, size)
     own_pick, halo_pick, spread = call(
         functools.partial(tables_kernel, slots, faces),
@@ -405,18 +403,6 @@
         "tables",
     )
 
-    def gather(z, name):
-        (own_x,) = call(
-            gather_kernel,
-            [own_pick, z],
-            [VMEM] * 2,
-            [x_shape],
-            [],
-            2 * slots_all * faces * width,
-            name,
-        )
-        return own_x
-
     def operator(own_x, arrived, keep_x, name):
         halo = VMEM((2 * halo_rows, 2 * width), BF16)
         return call(
@@ -429,7 +415,10 @@
             name,
         )
 
-    own_x = gather(first, "gather1")
+    gather_flops = 2 * slots_all * faces * width
+    (own_x,) = call(
+        gather_kernel, [own_pick, first], [VMEM] * 2, [x_shape], [], gather_flops, "gather1"
+    )
     y, *back = operator(own_x, arrived, False, "operator1")
     returned = exchange(back, size)
     (own,) = call(
@@ -451,18 +440,24 @@
         "middle",
     )
     arrived = exchange(outgoing, size)
-    own_x = gather(second, "gather2")
+    own_x, lift = call(
+        gather_lift_kernel,
+        [own_pick, second, in_hbm(lifting)],
+        [VMEM] * 2 + [HBM],
+        [x_shape, (lifting.shape, BF16)],
+        [pltpu.SemaphoreType.DMA],
+        gather_flops,
+        "gather2",
+    )
     y, *back, x = operator(own_x, arrived, True, "operator2")
     returned = exchange(back, size)
     own, interior = call(
         finish_kernel,
-        [spread, y, x, in_hbm(lifting)],
-        [VMEM] * 3 + [HBM],
+        [spread, y, x, lift],
+        [VMEM] * 4,
         [own_shape, ((elems, width // face_dofs * inside), BF16)],
         [
             VMEM((elems, width // face_dofs * inside), BF16),
-            VMEM(lifting.shape, BF16),
-            pltpu.SemaphoreType.DMA,
             pltpu.SemaphoreType.DMA((pairs // 2,)),
         ],
         4 * pairs * elems * eld * inside,

time: 55.3 us -> 50.5 us (0.913)
  waiting for transfers between devices: 5.26 us -> 3.41 us
  starting transfers between devices: 31.7 us -> 30.1 us
  Pallas kernels: 16.5 us -> 15.1 us
    ppermute x15, waiting for transfers between devices: 5.26 us -> 3.41 us  [exchange(): got = {c: lax.ppermute(arrays[c], 'elem', ways[c]) for c in order}]
    ppermute x15, starting transfers between devices: 31.7 us -> 30.1 us  [exchange(): got = {c: lax.ppermute(arrays[c], 'elem', ways[c]) for c in order}]
    pallas_call x13 -> x11, Pallas kernels: 16.5 us -> 15.1 us  [call(): pl.pallas_call(kernel, out_shape=[jax.ShapeDtypeStruct(s, d) for s, d in...]
  transfers between devices with their start and end apart: 15 -> 15, of which waited for: 3 -> 5; matrix products, arithmetic and copies ran while one was open for 0% -> 0% of each run, Pallas kernels for 16% -> 14%
where the time goes in v4:
time: 50.5 us; the launch traced here: 50.2 us
  starting transfers between devices  30.1 us (60%)
  Pallas kernels  15.1 us (30%)
  waiting for transfers between devices  3.41 us (7%)
  between operations  1.53 us (3%)
    ppermute x15, starting transfers between devices, exchange(): got = {c: lax.ppermute(arrays[c], 'elem', ways[c]) for c in order}  30.1 us
    pallas_call x11, Pallas kernels, call(): pl.pallas_call(kernel, out_shape=[jax.ShapeDtypeStruct(s, d) for s, d in...  15.1 us
    ppermute x15, waiting for transfers between devices, exchange(): got = {c: lax.ppermute(arrays[c], 'elem', ways[c]) for c in order}  3.41 us
  transfers between devices with their start and end apart: 15, of which 5 were waited for; matrix products, arithmetic and copies ran while one was open for 0% of the time, Pallas kernels for 14%

profile of v4, /device:TPU:0, one launch (start us, length us, event | category | flops | bytes accessed | tf_op | source)
XLA Modules:
  0.0 50.2 jit_solution(14198185463275850051)
XLA Ops:
  0.6 3.1 %collective-permute-start.2 = (s32[3,1,32]{2,1,0:T(1,128)}, s32[3,1,32]{2,1,0:T(1,128)S(1)}, u32[]{:S(2)}, u32[]{:S(2)}) collective-permute-start(s32[3,1,32]{2,1,0:T(1,128)} %bitcast.10), channel_id=1, source_target_pairs={{0,4},{4,0},{8,12},{12,8},{1,5},{5,1},{9,13},{13,9},{2,6},{6,2},{1... | collective-permute-start | bytes 1160 | tf_op jit(solution)/shard_map/ppermute | solution.py:330
  4.4 3.9 %collective-permute-start = (s32[3,1,32]{2,1,0:T(1,128)}, s32[3,1,32]{2,1,0:T(1,128)S(1)}, u32[]{:S(2)}, u32[]{:S(2)}) collective-permute-start(s32[3,1,32]{2,1,0:T(1,128)} %bitcast.12), channel_id=1, source_target_pairs={{0,8},{4,12},{8,0},{12,4},{1,9},{5,13},{9,1},{13,5},{2,10},{6,14},... | collective-permute-start | bytes 1160 | tf_op jit(solution)/shard_map/ppermute | solution.py:330
  8.3 1.7 %prepare.1 = (bf16[384,1024]{1,0:T(8,128)(2,1)S(1)}, bf16[384,768]{1,0:T(8,128)(2,1)S(1)}, f32[1,384]{1,0:T(1,128)S(1)}) custom-call(bf16[384,1024]{1,0:T(8,128)(2,1)} %rhs_hbm.1, bf16[64,64]{1,0:T(8,128)(2,1)} %jacobi_ref.1, bf16[384,384]{1,0:T(8,128)(2,1)} %stiff_hbm.1, bf16[384,384]{1,0:T(8,128)(2,1)} %mass_hbm.1, f32[384]{0:T(512)} %scale_hbm.1), custom_call_target="tpu_custom_call" | custom-call | flops 201326592 | bytes 1385984 | tf_op jit(solution)/shard_map/prepare/pallas_call | solution.py:301
  10.5 3.0 %collective-permute-start.3 = (bf16[32,1024]{1,0:T(8,128)(2,1)S(1)}, bf16[32,1024]{1,0:T(8,128)(2,1)S(1)}, u32[]{:S(2)}, u32[]{:S(2)}) collective-permute-start(bf16[32,1024]{1,0:T(8,128)(2,1)S(1)} %get-tuple-element.32), channel_id=1, source_target_pairs={{0,8},{4,12},{8,0},{12,4},{1,9},{5,13},{9,1},{13,5},{2,10},{6,14},... | collective-permute-start | bytes 196616 | tf_op jit(solution)/shard_map/ppermute | solution.py:330
  13.5 0.7 %collective-permute-start.4 = (bf16[32,1024]{1,0:T(8,128)(2,1)S(1)}, bf16[32,1024]{1,0:T(8,128)(2,1)S(1)}, u32[]{:S(2)}, u32[]{:S(2)}) collective-permute-start(bf16[32,1024]{1,0:T(8,128)(2,1)S(1)} %get-tuple-element.33), channel_id=1, source_target_pairs={{4,8},{8,4},{5,9},{9,5},{6,10},{10,6},{7,11},{11,7},{20,24},{24,20... | collective-permute-start | bytes 196616 | tf_op jit(solution)/shard_map/ppermute | solution.py:330
  14.2 1.9 %collective-permute-start.5 = (bf16[32,1024]{1,0:T(8,128)(2,1)S(1)}, bf16[32,1024]{1,0:T(8,128)(2,1)S(1)}, u32[]{:S(2)}, u32[]{:S(2)}) collective-permute-start(bf16[32,1024]{1,0:T(8,128)(2,1)S(1)} %get-tuple-element.34), channel_id=1, source_target_pairs={{0,4},{4,0},{8,12},{12,8},{1,5},{5,1},{9,13},{13,9},{2,6},{6,2},{1... | collective-permute-start | bytes 196616 | tf_op jit(solution)/shard_map/ppermute | solution.py:330
  17.1 1.1 %gather1.1.own_x_ref = bf16[2048,384]{1,0:T(8,128)(2,1)S(1)} custom-call(bf16[768,384]{1,0:T(8,128)(2,1)S(1)} %get-tuple-element.30.pick_ref, bf16[384,1024]{1,0:T(8,128)(2,1)S(1)} %get-tuple-element.31.z_ref), custom_call_target="tpu_custom_call" | custom-call | flops 603979776 | bytes 1376256 | tf_op jit(solution)/shard_map/gather1/pallas_call | solution.py:301
  18.5 2.8 %operator1.1 = (bf16[768,1024]{1,0:T(8,128)(2,1)S(1)}, bf16[32,1024]{1,0:T(8,128)(2,1)S(1)}, bf16[32,1024]{1,0:T(8,128)(2,1)S(1)}, bf16[32,1024]{1,0:T(8,128)(2,1)S(1)}) custom-call(bf16[384,256]{1,0:T(8,128)(2,1)S(1)} %get-tuple-element.29.pick_ref, bf16[512,768]{1,0:T(8,128)(2,1)S(1)} %get-tuple-element.28.spread_ref, ...), custom_call_target="tpu_custom_call" | custom-call | flops 1207959552 | bytes 3343360 | tf_op jit(solution)/shard_map/operator1/pallas_call | solution.py:301
  21.3 3.4 %collective-permute-start.6 = (bf16[32,1024]{1,0:T(8,128)(2,1)S(1)}, bf16[32,1024]{1,0:T(8,128)(2,1)S(1)}, u32[]{:S(2)}, u32[]{:S(2)}) collective-permute-start(bf16[32,1024]{1,0:T(8,128)(2,1)S(1)} %get-tuple-element.37), channel_id=1, source_target_pairs={{0,8},{4,12},{8,0},{12,4},{1,9},{5,13},{9,1},{13,5},{2,10},{6,14},... | collective-permute-start | bytes 196616 | tf_op jit(solution)/shard_map/ppermute | solution.py:330
  24.6 0.7 %collective-permute-start.7 = (bf16[32,1024]{1,0:T(8,128)(2,1)S(1)}, bf16[32,1024]{1,0:T(8,128)(2,1)S(1)}, u32[]{:S(2)}, u32[]{:S(2)}) collective-permute-start(bf16[32,1024]{1,0:T(8,128)(2,1)S(1)} %get-tuple-element.38), channel_id=1, source_target_pairs={{4,8},{8,4},{5,9},{9,5},{6,10},{10,6},{7,11},{11,7},{20,24},{24,20... | collective-permute-start | bytes 196616 | tf_op jit(solution)/shard_map/ppermute | solution.py:330
  25.3 1.9 %collective-permute-start.8 = (bf16[32,1024]{1,0:T(8,128)(2,1)S(1)}, bf16[32,1024]{1,0:T(8,128)(2,1)S(1)}, u32[]{:S(2)}, u32[]{:S(2)}) collective-permute-start(bf16[32,1024]{1,0:T(8,128)(2,1)S(1)} %get-tuple-element.39), channel_id=1, source_target_pairs={{0,4},{4,0},{8,12},{12,8},{1,5},{5,1},{9,13},{13,9},{2,6},{6,2},{1... | collective-permute-start | bytes 196616 | tf_op jit(solution)/shard_map/ppermute | solution.py:330
  27.2 0.8 %sums1.1.own_ref = f32[384,1024]{1,0:T(8,128)S(1)} custom-call(bf16[512,768]{1,0:T(8,128)(2,1)S(1)} %get-tuple-element.28.spread_ref, bf16[768,1024]{1,0:T(8,128)(2,1)S(1)} %get-tuple-element.36.y_ref), custom_call_target="tpu_custom_call" | custom-call | flops 603979776 | bytes 2359296 | tf_op jit(solution)/shard_map/sums1/pallas_call | solution.py:301
  28.0 1.6 %collective-permute-done.8.bc_ref = bf16[32,1024]{1,0:T(8,128)(2,1)S(1)} collective-permute-done((bf16[32,1024]{1,0:T(8,128)(2,1)S(1)}, bf16[32,1024]{1,0:T(8,128)(2,1)S(1)}, u32[]{:S(2)}, u32[]{:S(2)}) %collective-permute-start.8) | collective-permute-done | bytes 65568 | tf_op jit(solution)/shard_map/ppermute | solution.py:330
  29.6 0.8 %middle.1 = (bf16[384,1024]{1,0:T(8,128)(2,1)S(1)}, bf16[32,1024]{1,0:T(8,128)(2,1)S(1)}, bf16[32,1024]{1,0:T(8,128)(2,1)S(1)}, bf16[32,1024]{1,0:T(8,128)(2,1)S(1)}) custom-call(s32[1]{0:T(128)} %bitcast.par_ref, f32[384,1024]{1,0:T(8,128)S(1)} %sums1.1.own_ref, bf16[32,1024]{1,0:T(8,128)(2,1)S(1)} %collective-permute-done.6.ba_ref, ...), custom_call_target="tpu_custom_call" | custom-call | flops 201326592 | bytes 1780356 | tf_op jit(solution)/shard_map/middle/pallas_call | solution.py:301
  30.4 3.0 %collective-permute-start.9 = (bf16[32,1024]{1,0:T(8,128)(2,1)S(1)}, bf16[32,1024]{1,0:T(8,128)(2,1)S(1)}, u32[]{:S(2)}, u32[]{:S(2)}) collective-permute-start(bf16[32,1024]{1,0:T(8,128)(2,1)S(1)} %get-tuple-element.43), channel_id=1, source_target_pairs={{0,8},{4,12},{8,0},{12,4},{1,9},{5,13},{9,1},{13,5},{2,10},{6,14},... | collective-permute-start | bytes 196616 | tf_op jit(solution)/shard_map/ppermute | solution.py:330
  33.4 0.7 %collective-permute-start.10 = (bf16[32,1024]{1,0:T(8,128)(2,1)S(1)}, bf16[32,1024]{1,0:T(8,128)(2,1)S(1)}, u32[]{:S(2)}, u32[]{:S(2)}) collective-permute-start(bf16[32,1024]{1,0:T(8,128)(2,1)S(1)} %get-tuple-element.44), channel_id=1, source_target_pairs={{4,8},{8,4},{5,9},{9,5},{6,10},{10,6},{7,11},{11,7},{20,24},{24,20... | collective-permute-start | bytes 196616 | tf_op jit(solution)/shard_map/ppermute | solution.py:330
  34.0 1.9 %collective-permute-start.11 = (bf16[32,1024]{1,0:T(8,128)(2,1)S(1)}, bf16[32,1024]{1,0:T(8,128)(2,1)S(1)}, u32[]{:S(2)}, u32[]{:S(2)}) collective-permute-start(bf16[32,1024]{1,0:T(8,128)(2,1)S(1)} %get-tuple-element.45), channel_id=1, source_target_pairs={{0,4},{4,0},{8,12},{12,8},{1,5},{5,1},{9,13},{13,9},{2,6},{6,2},{1... | collective-permute-start | bytes 196616 | tf_op jit(solution)/shard_map/ppermute | solution.py:330
  35.9 1.1 %gather2.1 = (bf16[2048,384]{1,0:T(8,128)(2,1)S(1)}, bf16[384,512]{1,0:T(8,128)(2,1)S(1)}) custom-call(bf16[768,384]{1,0:T(8,128)(2,1)S(1)} %get-tuple-element.30.pick_ref, bf16[384,1024]{1,0:T(8,128)(2,1)S(1)} %get-tuple-element.41.z_ref, bf16[384,512]{1,0:T(8,128)(2,1)} %lift_hbm.1), custom_call_target="tpu_custom_call" | custom-call | flops 603979776 | bytes 1769472 | tf_op jit(solution)/shard_map/gather2/pallas_call | solution.py:301
  37.1 1.3 %collective-permute-done.11.ac_ref = bf16[32,1024]{1,0:T(8,128)(2,1)S(1)} collective-permute-done((bf16[32,1024]{1,0:T(8,128)(2,1)S(1)}, bf16[32,1024]{1,0:T(8,128)(2,1)S(1)}, u32[]{:S(2)}, u32[]{:S(2)}) %collective-permute-start.11) | collective-permute-done | bytes 65568 | tf_op jit(solution)/shard_map/ppermute | solution.py:330
  38.4 2.8 %operator2.1 = (bf16[768,1024]{1,0:T(8,128)(2,1)S(1)}, bf16[32,1024]{1,0:T(8,128)(2,1)S(1)}, bf16[32,1024]{1,0:T(8,128)(2,1)S(1)}, bf16[32,1024]{1,0:T(8,128)(2,1)S(1)}, bf16[2048,384]{1,0:T(8,128)(2,1)S(1)}) custom-call(bf16[384,256]{1,0:T(8,128)(2,1)S(1)} %get-tuple-element.29.pick_ref, bf16[512,768]{1,0:T(8,128)(2,1)S(1)} %get-tuple-element.28.spread_ref, ...), custom_call_target="tpu_custom_call" | custom-call | flops 1207959552 | bytes 3343360 | tf_op jit(solution)/shard_map/operator2/pallas_call | solution.py:301
  41.2 2.8 %collective-permute-start.12 = (bf16[32,1024]{1,0:T(8,128)(2,1)S(1)}, bf16[32,1024]{1,0:T(8,128)(2,1)S(1)}, u32[]{:S(2)}, u32[]{:S(2)}) collective-permute-start(bf16[32,1024]{1,0:T(8,128)(2,1)S(1)} %get-tuple-element.50), channel_id=1, source_target_pairs={{0,8},{4,12},{8,0},{12,4},{1,9},{5,13},{9,1},{13,5},{2,10},{6,14},... | collective-permute-start | bytes 196616 | tf_op jit(solution)/shard_map/ppermute | solution.py:330
  44.7 2.1 %collective-permute-start.14 = (bf16[32,1024]{1,0:T(8,128)(2,1)S(1)}, bf16[32,1024]{1,0:T(8,128)(2,1)S(1)}, u32[]{:S(2)}, u32[]{:S(2)}) collective-permute-start(bf16[32,1024]{1,0:T(8,128)(2,1)S(1)} %get-tuple-element.52), channel_id=1, source_target_pairs={{0,4},{4,0},{8,12},{12,8},{1,5},{5,1},{9,13},{13,9},{2,6},{6,2},{1... | collective-permute-start | bytes 196616 | tf_op jit(solution)/shard_map/ppermute | solution.py:330
  46.8 2.1 %finish.1 = (f32[384,1024]{1,0:T(8,128)S(1)}, bf16[128,8192]{1,0:T(8,128)(2,1)}) custom-call(bf16[512,768]{1,0:T(8,128)(2,1)S(1)} %get-tuple-element.28.spread_ref, bf16[768,1024]{1,0:T(8,128)(2,1)S(1)} %get-tuple-element.46.y_ref, bf16[2048,384]{1,0:T(8,128)(2,1)S(1)} %get-tuple-element.47.x_ref, bf16[384,512]{1,0:T(8,128)(2,1)S(1)} %get-tuple-element.48.lift_ref), custom_call_target="tpu_custom_call" | custom-call | flops 805306368 | bytes 4325376 | tf_op jit(solution)/shard_map/finish/pallas_call | solution.py:301
  49.0 1.2 %last.1 = bf16[384,1024]{1,0:T(8,128)(2,1)} custom-call(s32[1]{0:T(128)} %bitcast.par_ref, f32[384,1024]{1,0:T(8,128)S(1)} %get-tuple-element.49.own_ref, bf16[32,1024]{1,0:T(8,128)(2,1)S(1)} %collective-permute-done.12.ba_ref, bf16[32,1024]{1,0:T(8,128)(2,1)S(1)} %collective-permute-done.13.bb_ref, bf16[32,1024]{1,0:T(8,128)(2,1)S(1)} %collective-permute-done.14.bc_ref, ...), custom_call_target="tpu_custom_call" | custom-call | flops 100663296 | bytes 1770628 | tf_op jit(solution)/shard_map/last/pallas_call | solution.py:301
  (25 shorter events, 2.6 us)
Async XLA Ops:
  0.6 16.1 %copy-start.1 = (s32[128,6]{0,1:T(8,128)S(1)}, s32[128,6]{0,1:T(8,128)}, u32[]{:S(2)}) copy-start(s32[128,6]{0,1:T(8,128)} %param.15) | copy-start | bytes 9220
  0.6 9.3 %collective-permute-start.2 = (s32[3,1,32]{2,1,0:T(1,128)}, s32[3,1,32]{2,1,0:T(1,128)S(1)}, u32[]{:S(2)}, u32[]{:S(2)}) collective-permute-start(s32[3,1,32]{2,1,0:T(1,128)} %bitcast.10), channel_id=1, source_target_pairs={{0,4},{4,0},{8,12},{12,8},{1,5},{5,1},{9,13},{13,9},{2,6},{6,2},{1... | collective-permute-start | bytes 1160 | tf_op jit(solution)/shard_map/ppermute | solution.py:330
  3.7 6.3 %collective-permute-start.1 = (s32[3,1,32]{2,1,0:T(1,128)}, s32[3,1,32]{2,1,0:T(1,128)S(1)}, u32[]{:S(2)}, u32[]{:S(2)}) collective-permute-start(s32[3,1,32]{2,1,0:T(1,128)} %bitcast.11), channel_id=1, source_target_pairs={{4,8},{8,4},{5,9},{9,5},{6,10},{10,6},{7,11},{11,7},{20,24},{24,20... | collective-permute-start | bytes 1160 | tf_op jit(solution)/shard_map/ppermute | solution.py:330
  4.4 5.7 %collective-permute-start = (s32[3,1,32]{2,1,0:T(1,128)}, s32[3,1,32]{2,1,0:T(1,128)S(1)}, u32[]{:S(2)}, u32[]{:S(2)}) collective-permute-start(s32[3,1,32]{2,1,0:T(1,128)} %bitcast.12), channel_id=1, source_target_pairs={{0,8},{4,12},{8,0},{12,4},{1,9},{5,13},{9,1},{13,5},{2,10},{6,14},... | collective-permute-start | bytes 1160 | tf_op jit(solution)/shard_map/ppermute | solution.py:330
  10.5 8.0 %copy-start.2 = (f32[128]{0:T(128)S(1)}, f32[128]{0:T(128)}, u32[]{:S(2)}) copy-start(f32[128]{0:T(128)} %param.13) | copy-start | bytes 1540
  10.5 8.0 %copy-start.3 = (f32[128]{0:T(128)S(1)}, f32[128]{0:T(128)}, u32[]{:S(2)}) copy-start(f32[128]{0:T(128)} %param.14) | copy-start | bytes 1540
  10.5 7.7 %collective-permute-start.3 = (bf16[32,1024]{1,0:T(8,128)(2,1)S(1)}, bf16[32,1024]{1,0:T(8,128)(2,1)S(1)}, u32[]{:S(2)}, u32[]{:S(2)}) collective-permute-start(bf16[32,1024]{1,0:T(8,128)(2,1)S(1)} %get-tuple-element.32), channel_id=1, source_target_pairs={{0,8},{4,12},{8,0},{12,4},{1,9},{5,13},{9,1},{13,5},{2,10},{6,14},... | collective-permute-start | bytes 196616 | tf_op jit(solution)/shard_map/ppermute | solution.py:330
  13.5 4.7 %collective-permute-start.4 = (bf16[32,1024]{1,0:T(8,128)(2,1)S(1)}, bf16[32,1024]{1,0:T(8,128)(2,1)S(1)}, u32[]{:S(2)}, u32[]{:S(2)}) collective-permute-start(bf16[32,1024]{1,0:T(8,128)(2,1)S(1)} %get-tuple-element.33), channel_id=1, source_target_pairs={{4,8},{8,4},{5,9},{9,5},{6,10},{10,6},{7,11},{11,7},{20,24},{24,20... | collective-permute-start | bytes 196616 | tf_op jit(solution)/shard_map/ppermute | solution.py:330
  14.2 4.3 %collective-permute-start.5 = (bf16[32,1024]{1,0:T(8,128)(2,1)S(1)}, bf16[32,1024]{1,0:T(8,128)(2,1)S(1)}, u32[]{:S(2)}, u32[]{:S(2)}) collective-permute-start(bf16[32,1024]{1,0:T(8,128)(2,1)S(1)} %get-tuple-element.34), channel_id=1, source_target_pairs={{0,4},{4,0},{8,12},{12,8},{1,5},{5,1},{9,13},{13,9},{2,6},{6,2},{1... | collective-permute-start | bytes 196616 | tf_op jit(solution)/shard_map/ppermute | solution.py:330
  21.3 6.7 %collective-permute-start.6 = (bf16[32,1024]{1,0:T(8,128)(2,1)S(1)}, bf16[32,1024]{1,0:T(8,128)(2,1)S(1)}, u32[]{:S(2)}, u32[]{:S(2)}) collective-permute-start(bf16[32,1024]{1,0:T(8,128)(2,1)S(1)} %get-tuple-element.37), channel_id=1, source_target_pairs={{0,8},{4,12},{8,0},{12,4},{1,9},{5,13},{9,1},{13,5},{2,10},{6,14},... | collective-permute-start | bytes 196616 | tf_op jit(solution)/shard_map/ppermute | solution.py:330
  24.6 3.4 %collective-permute-start.7 = (bf16[32,1024]{1,0:T(8,128)(2,1)S(1)}, bf16[32,1024]{1,0:T(8,128)(2,1)S(1)}, u32[]{:S(2)}, u32[]{:S(2)}) collective-permute-start(bf16[32,1024]{1,0:T(8,128)(2,1)S(1)} %get-tuple-element.38), channel_id=1, source_target_pairs={{4,8},{8,4},{5,9},{9,5},{6,10},{10,6},{7,11},{11,7},{20,24},{24,20... | collective-permute-start | bytes 196616 | tf_op jit(solution)/shard_map/ppermute | solution.py:330
  25.3 4.3 %collective-permute-start.8 = (bf16[32,1024]{1,0:T(8,128)(2,1)S(1)}, bf16[32,1024]{1,0:T(8,128)(2,1)S(1)}, u32[]{:S(2)}, u32[]{:S(2)}) collective-permute-start(bf16[32,1024]{1,0:T(8,128)(2,1)S(1)} %get-tuple-element.39), channel_id=1, source_target_pairs={{0,4},{4,0},{8,12},{12,8},{1,5},{5,1},{9,13},{13,9},{2,6},{6,2},{1... | collective-permute-start | bytes 196616 | tf_op jit(solution)/shard_map/ppermute | solution.py:330
  27.2 2.4 %copy-start = (bf16[64,64]{1,0:T(8,128)(2,1)S(1)}, bf16[64,64]{1,0:T(8,128)(2,1)}, u32[]{:S(2)}) copy-start(bf16[64,64]{1,0:T(8,128)(2,1)} %jacobi_ref.1) | copy-start | bytes 24580
  30.4 6.6 %collective-permute-start.9 = (bf16[32,1024]{1,0:T(8,128)(2,1)S(1)}, bf16[32,1024]{1,0:T(8,128)(2,1)S(1)}, u32[]{:S(2)}, u32[]{:S(2)}) collective-permute-start(bf16[32,1024]{1,0:T(8,128)(2,1)S(1)} %get-tuple-element.43), channel_id=1, source_target_pairs={{0,8},{4,12},{8,0},{12,4},{1,9},{5,13},{9,1},{13,5},{2,10},{6,14},... | collective-permute-start | bytes 196616 | tf_op jit(solution)/shard_map/ppermute | solution.py:330
  33.4 3.7 %collective-permute-start.10 = (bf16[32,1024]{1,0:T(8,128)(2,1)S(1)}, bf16[32,1024]{1,0:T(8,128)(2,1)S(1)}, u32[]{:S(2)}, u32[]{:S(2)}) collective-permute-start(bf16[32,1024]{1,0:T(8,128)(2,1)S(1)} %get-tuple-element.44), channel_id=1, source_target_pairs={{4,8},{8,4},{5,9},{9,5},{6,10},{10,6},{7,11},{11,7},{20,24},{24,20... | collective-permute-start | bytes 196616 | tf_op jit(solution)/shard_map/ppermute | solution.py:330
  34.0 4.3 %collective-permute-start.11 = (bf16[32,1024]{1,0:T(8,128)(2,1)S(1)}, bf16[32,1024]{1,0:T(8,128)(2,1)S(1)}, u32[]{:S(2)}, u32[]{:S(2)}) collective-permute-start(bf16[32,1024]{1,0:T(8,128)(2,1)S(1)} %get-tuple-element.45), channel_id=1, source_target_pairs={{0,4},{4,0},{8,12},{12,8},{1,5},{5,1},{9,13},{13,9},{2,6},{6,2},{1... | collective-permute-start | bytes 196616 | tf_op jit(solution)/shard_map/ppermute | solution.py:330
  41.2 7.6 %collective-permute-start.12 = (bf16[32,1024]{1,0:T(8,128)(2,1)S(1)}, bf16[32,1024]{1,0:T(8,128)(2,1)S(1)}, u32[]{:S(2)}, u32[]{:S(2)}) collective-permute-start(bf16[32,1024]{1,0:T(8,128)(2,1)S(1)} %get-tuple-element.50), channel_id=1, source_target_pairs={{0,8},{4,12},{8,0},{12,4},{1,9},{5,13},{9,1},{13,5},{2,10},{6,14},... | collective-permute-start | bytes 196616 | tf_op jit(solution)/shard_map/ppermute | solution.py:330
  44.0 4.9 %collective-permute-start.13 = (bf16[32,1024]{1,0:T(8,128)(2,1)S(1)}, bf16[32,1024]{1,0:T(8,128)(2,1)S(1)}, u32[]{:S(2)}, u32[]{:S(2)}) collective-permute-start(bf16[32,1024]{1,0:T(8,128)(2,1)S(1)} %get-tuple-element.51), channel_id=1, source_target_pairs={{4,8},{8,4},{5,9},{9,5},{6,10},{10,6},{7,11},{11,7},{20,24},{24,20... | collective-permute-start | bytes 196616 | tf_op jit(solution)/shard_map/ppermute | solution.py:330
  44.7 4.3 %collective-permute-start.14 = (bf16[32,1024]{1,0:T(8,128)(2,1)S(1)}, bf16[32,1024]{1,0:T(8,128)(2,1)S(1)}, u32[]{:S(2)}, u32[]{:S(2)}) collective-permute-start(bf16[32,1024]{1,0:T(8,128)(2,1)S(1)} %get-tuple-element.52), channel_id=1, source_target_pairs={{0,4},{4,0},{8,12},{12,8},{1,5},{5,1},{9,13},{13,9},{2,6},{6,2},{1... | collective-permute-start | bytes 196616 | tf_op jit(solution)/shard_map/ppermute | solution.py:330

commit v5 on v4

--- a/solution.py
+++ b/solution.py
@@ -47,17 +47,13 @@
     return jnp.where(keep, full, jnp.zeros_like(full))
 
 
-def precondition(traces_ref, scale_ref, jacobi_ref, z_ref):
-    width = traces_ref.shape[1]
-    block = block_diagonal(jacobi_ref[...].astype(F32), 4).astype(BF16)
-    scales = column_tiles(scale_ref[...])
-    step = block.shape[0]
-    for start in range(0, width, step):
-        product = matmul(traces_ref[:, start : start + step], block)
-        for t, scale in enumerate(scales):
-            part = product[t * LANES : (t + 1) * LANES, :]
-            both = jnp.concatenate([scale, scale], axis=1)
-            z_ref[t * LANES : (t + 1) * LANES, start : start + step] = (part * both).astype(BF16)
+def precondition(field_ref, scale_ref, block_ref, z_ref):
+    step = block_ref.shape[0]
+    scale = scale_ref[...]
+    scale = jnp.concatenate([scale] * (step // LANES), axis=1)
+    for start in range(0, field_ref.shape[1], step):
+        product = matmul(field_ref[:, start : start + step], block_ref[...])
+        z_ref[:, start : start + step] = (product * scale).astype(BF16)
 
 
 def swap_halves(even, odd, low):
@@ -66,12 +62,12 @@
 
 
 def prepare_kernel(
-    rhs_hbm, jacobi_hbm, stiff_hbm, mass_hbm, scale_hbm, z_ref, w_ref, scale_ref,
-    rhs_ref, jacobi_ref, line_ref, sems
+    rhs_hbm, jacobi_hbm, scale_hbm, stiff_hbm, mass_hbm,
+    z_ref, block_ref, scale_ref, face_scale_ref, w_ref, rhs_ref, small_ref, line_ref, sems
 ):
     half = w_ref.shape[1] // 2
     sources = (jacobi_hbm, scale_hbm, rhs_hbm, stiff_hbm, mass_hbm)
-    targets = (jacobi_ref, line_ref, rhs_ref, w_ref.at[:, :half], w_ref.at[:, half:])
+    targets = (small_ref, line_ref, rhs_ref, w_ref.at[:, :half], w_ref.at[:, half:])
     copies = [
         pltpu.make_async_copy(src, dst, sems.at[i])
         for i, (src, dst) in enumerate(zip(sources, targets))
@@ -79,10 +75,13 @@
     for copy in copies:
         copy.start()
     copies[0].wait()
+    block_ref[...] = block_diagonal(small_ref[...].astype(F32), 4).astype(BF16)
     copies[1].wait()
     scale_ref[...] = line_ref[...].reshape(scale_ref.shape)
+    for t, tile in enumerate(column_tiles(scale_ref[...])):
+        face_scale_ref[t * LANES : (t + 1) * LANES, :] = tile
     copies[2].wait()
-    precondition(rhs_ref, scale_ref, jacobi_ref, z_ref)
+    precondition(rhs_ref, face_scale_ref, block_ref, z_ref)
     copies[3].wait()
     copies[4].wait()
 
@@ -102,21 +101,42 @@
     return padded(jnp.concatenate(parts, axis=1))
 
 
-def send_rows(wanted, z_ref, out_refs):
+def wanted_tables(wanted, scale_row):
     (column,) = column_tiles(wanted)
     column = column.astype(I32)
     lane = iota((LANES, LANES), 1)
-    picks = jnp.concatenate(
-        [one_hot(column == lane + t * LANES) for t in range(z_ref.shape[0] // LANES)], axis=1
-    )
-    rows = matmul(picks, z_ref[...]).astype(BF16)
+    picks = []
+    scale = jnp.zeros((LANES, LANES), F32)
+    for t in range(scale_row.shape[1] // LANES):
+        chosen = column == lane + t * LANES
+        picks.append(one_hot(chosen))
+        across = jnp.broadcast_to(scale_row[:, t * LANES : (t + 1) * LANES], (LANES, LANES))
+        scale = scale + jnp.where(chosen, across, 0.0)
+    scale = jnp.broadcast_to(jnp.sum(scale, axis=1, keepdims=True), (LANES, LANES))
+    return jnp.concatenate(picks, axis=1), scale
+
+
+def send_rows(rows, scale, block_ref, out_refs):
+    step = block_ref.shape[0]
+    scale = jnp.concatenate([scale] * (step // LANES), axis=1)
+    slots = out_refs[0].shape[0]
+    for start in range(0, rows.shape[1], step):
+        product = matmul(rows[:, start : start + step], block_ref[...])
+        product = (product * scale).astype(BF16)
+        for c, ref in enumerate(out_refs):
+            ref[:, start : start + step] = product[c * slots : (c + 1) * slots, :]
+
+
+def send_kernel(par_ref, z_ref, ec_ref, eb_ref, ea_ref, *out_refs):
+    (column,) = column_tiles(wanted_row(par_ref[0], [ea_ref, eb_ref, ec_ref]))
+    column = column.astype(I32)
+    lane = iota((LANES, LANES), 1)
+    tiles = range(z_ref.shape[0] // LANES)
+    pick = jnp.concatenate([one_hot(column == lane + t * LANES) for t in tiles], axis=1)
+    rows = matmul(pick, z_ref[...]).astype(BF16)
     slots = out_refs[0].shape[0]
     for c, ref in enumerate(out_refs):
         ref[...] = rows[c * slots : (c + 1) * slots, :]
-
-
-def send_kernel(par_ref, z_ref, la_ref, lb_ref, lc_ref, *out_refs):
-    send_rows(wanted_row(par_ref[0], [la_ref, lb_ref, lc_ref]), z_ref, out_refs)
 
 
 def column_ids(par, faces, slots, tile, axis):
@@ -126,10 +146,10 @@
     return jnp.where(index < faces, index, index + moved)
 
 
-def tables_kernel(slots, faces, count_ref, par_ref, ids_ref, own_ref, halo_ref, spread_ref):
-    par = par_ref[0]
-    ids_all = jnp.where(iota(ids_ref.shape, 1) < count_ref[0], ids_ref[...], -1)
+def element_tables(par, slots, count, ids_ref, own_ref, halo_ref, spread_ref):
+    ids_all = jnp.where(iota(ids_ref.shape, 1) < count, ids_ref[...], -1)
     tiles = spread_ref.shape[0] // LANES
+    faces = own_ref.shape[1]
     owned = faces // LANES
     lanes = [column_ids(par, faces, slots, t, 1) for t in range(tiles)]
     rows = [column_ids(par, faces, slots, t, 0) for t in range(tiles)]
@@ -146,14 +166,7 @@
             spread_ref[span(t), span(k)] = one_hot(across == rows[t])
 
 
-def gather_lift_kernel(pick_ref, z_ref, lift_hbm, x_ref, lift_ref, sem):
-    load = pltpu.make_async_copy(lift_hbm, lift_ref, sem)
-    load.start()
-    gather_kernel(pick_ref, z_ref, x_ref)
-    load.wait()
-
-
-def gather_kernel(pick_ref, z_ref, x_ref):
+def gather_own(pick_ref, z_ref, x_ref):
     width = z_ref.shape[1]
     low = iota((LANES, LANES), 1) < LANES // 2
     for t in range(x_ref.shape[1] // LANES):
@@ -166,8 +179,32 @@
             x_ref[at + LANES : at + 2 * LANES, t * LANES : (t + 1) * LANES] = odd.astype(BF16)
 
 
+def first_gather_kernel(
+    slots, par_ref, count_ref, z_ref, ids_ref, stiff_scale_ref, mass_scale_ref,
+    x_ref, own_ref, halo_ref, spread_ref, element_scale_ref
+):
+    element_tables(par_ref[0], slots, count_ref[0], ids_ref, own_ref, halo_ref, spread_ref)
+    gather_own(own_ref, z_ref, x_ref)
+    (element_scale_ref[0],) = column_tiles(stiff_scale_ref[...])
+    (element_scale_ref[1],) = column_tiles(mass_scale_ref[...])
+
+
+def second_gather_kernel(
+    pick_ref, sums_ref, ba_ref, bb_ref, bc_ref, give_ref, scale_ref, block_ref, lift_hbm,
+    x_ref, lift_ref, gathered_ref, v_ref, z_ref, sem
+):
+    load = pltpu.make_async_copy(lift_hbm, lift_ref, sem)
+    load.start()
+    gather_back([ba_ref, bb_ref, bc_ref], gathered_ref)
+    for t in range(sums_ref.shape[0] // LANES):
+        v_ref[t * LANES : (t + 1) * LANES, :] = collected(sums_ref, give_ref, gathered_ref, t)
+    precondition(v_ref, scale_ref, block_ref, z_ref)
+    gather_own(pick_ref, z_ref, x_ref)
+    load.wait()
+
+
 def operator_kernel(
-    pick_ref, spread_ref, own_x_ref, aa_ref, ab_ref, ac_ref, stiff_scale_ref, mass_scale_ref,
+    pick_ref, spread_ref, own_x_ref, aa_ref, ab_ref, ac_ref, scale_ref,
     w_ref, y_ref, ba_ref, bb_ref, bc_ref, x_ref, halo_ref
 ):
     slots, width = aa_ref.shape
@@ -194,10 +231,8 @@
         for s in range(2 * pairs):
             at = (slice(s * LANES, (s + 1) * LANES), slice(t * LANES, (t + 1) * LANES))
             x_ref[at] = own_x_ref[at] + rows[:, s * LANES : (s + 1) * LANES]
-    (stiff_scale,) = column_tiles(stiff_scale_ref[...])
-    (mass_scale,) = column_tiles(mass_scale_ref[...])
-    stiff = jnp.concatenate([stiff_scale] * 2, axis=0)
-    mass = jnp.concatenate([mass_scale] * 2, axis=0)
+    stiff = jnp.concatenate([scale_ref[0]] * 2, axis=0)
+    mass = jnp.concatenate([scale_ref[1]] * 2, axis=0)
     low = iota((LANES, LANES), 1) < LANES // 2
     half = w_ref.shape[1] // 2
     for p in range(pairs):
@@ -224,8 +259,20 @@
         )
 
 
-def sums_kernel(spread_ref, y_ref, own_ref):
+def sums_kernel(
+    par_ref, spread_ref, y_ref, ec_ref, eb_ref, ea_ref, scale_ref,
+    own_ref, rows_ref, same_ref, give_ref, request_scale_ref, high_ref, low_ref
+):
+    wanted = wanted_row(par_ref[0], [ea_ref, eb_ref, ec_ref])
+    request, request_scale_ref[...] = wanted_tables(wanted, scale_ref[...])
+    target = jnp.broadcast_to(wanted, give_ref.shape)
+    give_ref[...] = one_hot(target == iota(give_ref.shape, 0))
     own_sums(spread_ref, y_ref, own_ref)
+    same_ref[...] = matmul(request, give_ref[...]).astype(BF16)
+    high_ref[...] = own_ref[...].astype(BF16)
+    low_ref[...] = (own_ref[...] - high_ref[...].astype(F32)).astype(BF16)
+    rows_ref[...] = matmul(request, high_ref[...])
+    rows_ref[...] += matmul(request, low_ref[...])
 
 
 def finish_kernel(
@@ -259,35 +306,28 @@
     gathered_ref[3 * slots :, :] = jnp.zeros((LANES - 3 * slots, width), BF16)
 
 
-def collected(own_ref, wanted, gathered_ref, tile):
-    target = jnp.broadcast_to(wanted, (LANES, LANES))
-    picks = one_hot(target == iota((LANES, LANES), 0) + tile * LANES)
-    own = own_ref[tile * LANES : (tile + 1) * LANES, :]
-    return (own + matmul(picks, gathered_ref[...])).astype(BF16)
+def collected(own_ref, give_ref, gathered_ref, tile):
+    rows = slice(tile * LANES, (tile + 1) * LANES)
+    return (own_ref[rows, :] + matmul(give_ref[rows, :], gathered_ref[...])).astype(BF16)
 
 
 def middle_kernel(
-    par_ref, own_ref, ba_ref, bb_ref, bc_ref, la_ref, lb_ref, lc_ref, scale_ref, jacobi_ref, z_ref,
-    oa_ref, ob_ref, oc_ref, gathered_ref, v_ref
-):
-    wanted = wanted_row(par_ref[0], [la_ref, lb_ref, lc_ref])
+    rows_ref, ba_ref, bb_ref, bc_ref, same_ref, request_scale_ref, block_ref,
+    oa_ref, ob_ref, oc_ref, gathered_ref
+):
     gather_back([ba_ref, bb_ref, bc_ref], gathered_ref)
-    for t in range(own_ref.shape[0] // LANES):
-        v_ref[t * LANES : (t + 1) * LANES, :] = collected(own_ref, wanted, gathered_ref, t)
-    precondition(v_ref, scale_ref, jacobi_ref, z_ref)
-    send_rows(wanted, z_ref, [oa_ref, ob_ref, oc_ref])
+    rows = (rows_ref[...] + matmul(same_ref[...], gathered_ref[...])).astype(BF16)
+    send_rows(rows, request_scale_ref[...], block_ref, [oa_ref, ob_ref, oc_ref])
 
 
 def last_kernel(
-    par_ref, own_ref, ba_ref, bb_ref, bc_ref, la_ref, lb_ref, lc_ref, out_hbm, gathered_ref,
-    out_ref, sems
-):
-    wanted = wanted_row(par_ref[0], [la_ref, lb_ref, lc_ref])
+    own_ref, ba_ref, bb_ref, bc_ref, give_ref, out_hbm, gathered_ref, out_ref, sems
+):
     gather_back([ba_ref, bb_ref, bc_ref], gathered_ref)
     copies = []
     for t in range(own_ref.shape[0] // LANES):
         span = pl.ds(t * LANES, LANES)
-        out_ref[span, :] = collected(own_ref, wanted, gathered_ref, t)
+        out_ref[span, :] = collected(own_ref, give_ref, gathered_ref, t)
         copy = pltpu.make_async_copy(out_ref.at[span, :], out_hbm.at[span, :], sems.at[t])
         copy.start()
         copies.append(copy)
@@ -365,13 +405,20 @@
     own_shape = ((faces, width), F32)
     element_flops = 4 * 2 * pairs * elems * eld * eld
 
-    first, weights, scale = call(
+    step = 4 * face_dofs
+    first, block, scale, face_scales, weights = call(
         prepare_kernel,
-        [in_hbm(a) for a in (trace_rhs, jacobi_block, stiffness, mass, face_scale)],
+        [in_hbm(a) for a in (trace_rhs, jacobi_block, face_scale, stiffness, mass)],
         [HBM] * 5,
-        [field, ((eld, 2 * eld), BF16), ((1, faces), F32)],
         [
-            VMEM(trace_rhs.shape, BF16),
+            field,
+            ((step, step), BF16),
+            ((1, faces), F32),
+            ((faces, LANES), F32),
+            ((eld, 2 * eld), BF16),
+        ],
+        [
+            VMEM(*field),
             VMEM(jacobi_block.shape, BF16),
             VMEM(face_scale.shape, F32),
             pltpu.SemaphoreType.DMA((5,)),
@@ -381,7 +428,7 @@
     )
     outgoing = call(
         send_kernel,
-        [par, first, *lists],
+        [par, first, *lists[::-1]],
         [SMEM] + [VMEM] * 4,
         rows,
         [],
@@ -389,63 +436,69 @@
         "send",
     )
     arrived = exchange(outgoing, size)
-    own_pick, halo_pick, spread = call(
-        functools.partial(tables_kernel, slots, faces),
-        [elem_count, par, elem_faces.T],
-        [SMEM, SMEM, VMEM],
+    gather_flops = 2 * slots_all * faces * width
+    tile = (LANES, LANES)
+    own_x, own_pick, halo_pick, spread, element_scales = call(
+        functools.partial(first_gather_kernel, slots),
+        [par, elem_count, first, elem_faces.T, stiff_row, mass_row],
+        [SMEM] * 2 + [VMEM] * 4,
         [
+            x_shape,
             ((slots_all, faces), BF16),
             ((slots_all // 2, 2 * halo_rows), BF16),
             ((ext_rows, slots_all), BF16),
+            ((2, *tile), F32),
         ],
         [],
-        slots_all * ext_rows * 4,
-        "tables",
+        gather_flops,
+        "gather1",
     )
 
     def operator(own_x, arrived, keep_x, name):
         halo = VMEM((2 * halo_rows, 2 * width), BF16)
         return call(
             operator_kernel,
-            [halo_pick, spread, own_x, *arrived, stiff_row, mass_row, weights],
-            [VMEM] * 9,
+            [halo_pick, spread, own_x, *arrived, element_scales, weights],
+            [VMEM] * 8,
             [y_shape, *rows] + ([x_shape] if keep_x else []),
             [halo] if keep_x else [VMEM(*x_shape), halo],
             element_flops,
             name,
         )
 
-    gather_flops = 2 * slots_all * faces * width
-    (own_x,) = call(
-        gather_kernel, [own_pick, first], [VMEM] * 2, [x_shape], [], gather_flops, "gather1"
-    )
     y, *back = operator(own_x, arrived, False, "operator1")
     returned = exchange(back, size)
-    (own,) = call(
+    own, own_rows, same, give, request_scale = call(
         sums_kernel,
-        [spread, y],
-        [VMEM] * 2,
-        [own_shape],
-        [],
+        [par, spread, y, *lists[::-1], scale],
+        [SMEM] + [VMEM] * 6,
+        [
+            own_shape,
+            ((LANES, width), F32),
+            (tile, BF16),
+            ((faces, LANES), BF16),
+            (tile, F32),
+        ],
+        [VMEM(*field)] * 2,
         2 * faces * slots_all * width,
         "sums1",
     )
-    second, *outgoing = call(
+    outgoing = call(
         middle_kernel,
-        [par, own, *returned, *lists, scale, jacobi_block],
-        [SMEM] + [VMEM] * 9,
-        [field, *rows],
-        [VMEM((LANES, width), BF16), VMEM((faces, width), BF16)],
-        2 * faces * width * 256,
+        [own_rows, *returned, same, request_scale, block],
+        [VMEM] * 7,
+        rows,
+        [VMEM((LANES, width), BF16)],
+        2 * LANES * width * 256,
         "middle",
     )
     arrived = exchange(outgoing, size)
     own_x, lift = call(
-        gather_lift_kernel,
-        [own_pick, second, in_hbm(lifting)],
-        [VMEM] * 2 + [HBM],
+        second_gather_kernel,
+        [own_pick, own, *returned, give, face_scales, block, in_hbm(lifting)],
+        [VMEM] * 8 + [HBM],
         [x_shape, (lifting.shape, BF16)],
-        [pltpu.SemaphoreType.DMA],
+        [VMEM((LANES, width), BF16), VMEM(*field), VMEM(*field), pltpu.SemaphoreType.DMA],
         gather_flops,
         "gather2",
     )
@@ -466,8 +519,8 @@
     )
     (applied,) = call(
         last_kernel,
-        [par, own, *returned, *lists],
-        [SMEM] + [VMEM] * 7,
+        [own, *returned, give],
+        [VMEM] * 5,
         [field],
         [
             VMEM((LANES, width), BF16),

time: 50.5 us -> 49.6 us (0.982)
  waiting for transfers between devices: 3.41 us -> 2.32 us
    ppermute x15, waiting for transfers between devices: 3.41 us -> 2.32 us  [exchange(): got = {c: lax.ppermute(arrays[c], 'elem', ways[c]) for c in order}]
    pallas_call x11 -> x10, Pallas kernels: 15.1 us -> 15.1 us  [call(): pl.pallas_call(kernel, out_shape=[jax.ShapeDtypeStruct(s, d) for s, d in...]
  transfers between devices with their start and end apart: 15 -> 15, of which waited for: 5 -> 5; matrix products, arithmetic and copies ran while one was open for 0% -> 0% of each run, Pallas kernels for 14% -> 16%
where the time goes in v5:
time: 49.6 us; the launch traced here: 49.3 us
  starting transfers between devices  30.3 us (61%)
  Pallas kernels  15.1 us (30%)
  waiting for transfers between devices  2.32 us (5%)
  between operations  1.54 us (3%)
    ppermute x15, starting transfers between devices, exchange(): got = {c: lax.ppermute(arrays[c], 'elem', ways[c]) for c in order}  30.3 us
    pallas_call x10, Pallas kernels, call(): pl.pallas_call(kernel, out_shape=[jax.ShapeDtypeStruct(s, d) for s, d in...  15.1 us
    ppermute x15, waiting for transfers between devices, exchange(): got = {c: lax.ppermute(arrays[c], 'elem', ways[c]) for c in order}  2.32 us
  transfers between devices with their start and end apart: 15, of which 5 were waited for; matrix products, arithmetic and copies ran while one was open for 0% of the time, Pallas kernels for 16%

profile of v5, /device:TPU:0, one launch (start us, length us, event | category | flops | bytes accessed | tf_op | source)
XLA Modules:
  0.0 49.3 jit_solution(6186564418721735033)
XLA Ops:
  0.7 4.1 %collective-permute-start.2 = (s32[3,1,32]{2,1,0:T(1,128)}, s32[3,1,32]{2,1,0:T(1,128)S(1)}, u32[]{:S(2)}, u32[]{:S(2)}) collective-permute-start(s32[3,1,32]{2,1,0:T(1,128)} %bitcast.8), channel_id=1, source_target_pairs={{0,8},{4,12},{8,0},{12,4},{1,9},{5,13},{9,1},{13,5},{2,10},{6,14},... | collective-permute-start | bytes 1160 | tf_op jit(solution)/shard_map/ppermute | solution.py:370
  5.4 2.9 %collective-permute-start = (s32[3,1,32]{2,1,0:T(1,128)}, s32[3,1,32]{2,1,0:T(1,128)S(1)}, u32[]{:S(2)}, u32[]{:S(2)}) collective-permute-start(s32[3,1,32]{2,1,0:T(1,128)} %bitcast.10), channel_id=1, source_target_pairs={{0,4},{4,0},{8,12},{12,8},{1,5},{5,1},{9,13},{13,9},{2,6},{6,2},{1... | collective-permute-start | bytes 1160 | tf_op jit(solution)/shard_map/ppermute | solution.py:370
  8.3 1.6 %prepare.1 = (bf16[384,1024]{1,0:T(8,128)(2,1)S(1)}, bf16[256,256]{1,0:T(8,128)(2,1)S(1)}, f32[1,384]{1,0:T(1,128)S(1)}, f32[384,128]{1,0:T(8,128)S(1)}, bf16[384,768]{1,0:T(8,128)(2,1)S(1)}) custom-call(bf16[384,1024]{1,0:T(8,128)(2,1)} %rhs_hbm.1, bf16[64,64]{1,0:T(8,128)(2,1)} %jacobi_hbm.1, f32[384]{0:T(512)} %scale_hbm.1, bf16[384,384]{1,0:T(8,128)(2,1)} %stiff_hbm.1, ...), custom_call_target="tpu_custom_call" | custom-call | flops 201326592 | bytes 1385984 | tf_op jit(solution)/shard_map/prepare/pallas_call | solution.py:341
  10.5 3.5 %collective-permute-start.3 = (bf16[32,1024]{1,0:T(8,128)(2,1)S(1)}, bf16[32,1024]{1,0:T(8,128)(2,1)S(1)}, u32[]{:S(2)}, u32[]{:S(2)}) collective-permute-start(bf16[32,1024]{1,0:T(8,128)(2,1)S(1)} %get-tuple-element.41), channel_id=1, source_target_pairs={{0,8},{4,12},{8,0},{12,4},{1,9},{5,13},{9,1},{13,5},{2,10},{6,14},... | collective-permute-start | bytes 196616 | tf_op jit(solution)/shard_map/ppermute | solution.py:370
  14.0 0.7 %collective-permute-start.4 = (bf16[32,1024]{1,0:T(8,128)(2,1)S(1)}, bf16[32,1024]{1,0:T(8,128)(2,1)S(1)}, u32[]{:S(2)}, u32[]{:S(2)}) collective-permute-start(bf16[32,1024]{1,0:T(8,128)(2,1)S(1)} %get-tuple-element.42), channel_id=1, source_target_pairs={{4,8},{8,4},{5,9},{9,5},{6,10},{10,6},{7,11},{11,7},{20,24},{24,20... | collective-permute-start | bytes 196616 | tf_op jit(solution)/shard_map/ppermute | solution.py:370
  14.7 1.9 %collective-permute-start.5 = (bf16[32,1024]{1,0:T(8,128)(2,1)S(1)}, bf16[32,1024]{1,0:T(8,128)(2,1)S(1)}, u32[]{:S(2)}, u32[]{:S(2)}) collective-permute-start(bf16[32,1024]{1,0:T(8,128)(2,1)S(1)} %get-tuple-element.43), channel_id=1, source_target_pairs={{0,4},{4,0},{8,12},{12,8},{1,5},{5,1},{9,13},{13,9},{2,6},{6,2},{1... | collective-permute-start | bytes 196616 | tf_op jit(solution)/shard_map/ppermute | solution.py:370
  17.3 1.3 %gather1.1 = (bf16[2048,384]{1,0:T(8,128)(2,1)S(1)}, bf16[768,384]{1,0:T(8,128)(2,1)S(1)}, bf16[384,256]{1,0:T(8,128)(2,1)S(1)}, bf16[512,768]{1,0:T(8,128)(2,1)S(1)}, f32[2,128,128]{2,1,0:T(8,128)S(1)}) custom-call(s32[1]{0:T(128)} %bitcast.par_ref, s32[1]{0:T(128)S(6)} %copy.13.count_ref, bf16[384,1024]{1,0:T(8,128)(2,1)S(1)} %get-tuple-element.36.z_ref, ...), custom_call_target="tpu_custom_call" | custom-call | flops 603979776 | bytes 790536 | tf_op jit(solution)/shard_map/gather1/pallas_call | solution.py:341
  19.0 2.7 %operator1.1 = (bf16[768,1024]{1,0:T(8,128)(2,1)S(1)}, bf16[32,1024]{1,0:T(8,128)(2,1)S(1)}, bf16[32,1024]{1,0:T(8,128)(2,1)S(1)}, bf16[32,1024]{1,0:T(8,128)(2,1)S(1)}) custom-call(bf16[384,256]{1,0:T(8,128)(2,1)S(1)} %get-tuple-element.38.pick_ref, bf16[512,768]{1,0:T(8,128)(2,1)S(1)} %get-tuple-element.37.spread_ref, ...), custom_call_target="tpu_custom_call" | custom-call | flops 1207959552 | bytes 3473408 | tf_op jit(solution)/shard_map/operator1/pallas_call | solution.py:341
  21.8 2.8 %collective-permute-start.6 = (bf16[32,1024]{1,0:T(8,128)(2,1)S(1)}, bf16[32,1024]{1,0:T(8,128)(2,1)S(1)}, u32[]{:S(2)}, u32[]{:S(2)}) collective-permute-start(bf16[32,1024]{1,0:T(8,128)(2,1)S(1)} %get-tuple-element.49), channel_id=1, source_target_pairs={{0,8},{4,12},{8,0},{12,4},{1,9},{5,13},{9,1},{13,5},{2,10},{6,14},... | collective-permute-start | bytes 196616 | tf_op jit(solution)/shard_map/ppermute | solution.py:370
  24.5 0.7 %collective-permute-start.7 = (bf16[32,1024]{1,0:T(8,128)(2,1)S(1)}, bf16[32,1024]{1,0:T(8,128)(2,1)S(1)}, u32[]{:S(2)}, u32[]{:S(2)}) collective-permute-start(bf16[32,1024]{1,0:T(8,128)(2,1)S(1)} %get-tuple-element.50), channel_id=1, source_target_pairs={{4,8},{8,4},{5,9},{9,5},{6,10},{10,6},{7,11},{11,7},{20,24},{24,20... | collective-permute-start | bytes 196616 | tf_op jit(solution)/shard_map/ppermute | solution.py:370
  25.2 2.1 %collective-permute-start.8 = (bf16[32,1024]{1,0:T(8,128)(2,1)S(1)}, bf16[32,1024]{1,0:T(8,128)(2,1)S(1)}, u32[]{:S(2)}, u32[]{:S(2)}) collective-permute-start(bf16[32,1024]{1,0:T(8,128)(2,1)S(1)} %get-tuple-element.51), channel_id=1, source_target_pairs={{0,4},{4,0},{8,12},{12,8},{1,5},{5,1},{9,13},{13,9},{2,6},{6,2},{1... | collective-permute-start | bytes 196616 | tf_op jit(solution)/shard_map/ppermute | solution.py:370
  27.3 1.2 %sums1.1 = (f32[384,1024]{1,0:T(8,128)S(1)}, f32[128,1024]{1,0:T(8,128)S(1)}, bf16[128,128]{1,0:T(8,128)(2,1)S(1)}, bf16[384,128]{1,0:T(8,128)(2,1)S(1)}, f32[128,128]{1,0:T(8,128)S(1)}) custom-call(s32[1]{0:T(128)} %bitcast.par_ref, bf16[512,768]{1,0:T(8,128)(2,1)S(1)} %get-tuple-element.37.spread_ref, bf16[768,1024]{1,0:T(8,128)(2,1)S(1)} %get-tuple-element.46.y_ref, ...), custom_call_target="tpu_custom_call" | custom-call | flops 603979776 | bytes 2361988 | tf_op jit(solution)/shard_map/sums1/pallas_call | solution.py:341
  28.6 1.0 %collective-permute-done.8.bc_ref = bf16[32,1024]{1,0:T(8,128)(2,1)S(1)} collective-permute-done((bf16[32,1024]{1,0:T(8,128)(2,1)S(1)}, bf16[32,1024]{1,0:T(8,128)(2,1)S(1)}, u32[]{:S(2)}, u32[]{:S(2)}) %collective-permute-start.8) | collective-permute-done | bytes 65568 | tf_op jit(solution)/shard_map/ppermute | solution.py:370
  29.9 2.8 %collective-permute-start.9 = (bf16[32,1024]{1,0:T(8,128)(2,1)S(1)}, bf16[32,1024]{1,0:T(8,128)(2,1)S(1)}, u32[]{:S(2)}, u32[]{:S(2)}) collective-permute-start(bf16[32,1024]{1,0:T(8,128)(2,1)S(1)} %get-tuple-element.59), channel_id=1, source_target_pairs={{0,8},{4,12},{8,0},{12,4},{1,9},{5,13},{9,1},{13,5},{2,10},{6,14},... | collective-permute-start | bytes 196616 | tf_op jit(solution)/shard_map/ppermute | solution.py:370
  32.7 0.7 %collective-permute-start.10 = (bf16[32,1024]{1,0:T(8,128)(2,1)S(1)}, bf16[32,1024]{1,0:T(8,128)(2,1)S(1)}, u32[]{:S(2)}, u32[]{:S(2)}) collective-permute-start(bf16[32,1024]{1,0:T(8,128)(2,1)S(1)} %get-tuple-element.60), channel_id=1, source_target_pairs={{4,8},{8,4},{5,9},{9,5},{6,10},{10,6},{7,11},{11,7},{20,24},{24,20... | collective-permute-start | bytes 196616 | tf_op jit(solution)/shard_map/ppermute | solution.py:370
  33.3 2.1 %collective-permute-start.11 = (bf16[32,1024]{1,0:T(8,128)(2,1)S(1)}, bf16[32,1024]{1,0:T(8,128)(2,1)S(1)}, u32[]{:S(2)}, u32[]{:S(2)}) collective-permute-start(bf16[32,1024]{1,0:T(8,128)(2,1)S(1)} %get-tuple-element.61), channel_id=1, source_target_pairs={{0,4},{4,0},{8,12},{12,8},{1,5},{5,1},{9,13},{13,9},{2,6},{6,2},{1... | collective-permute-start | bytes 196616 | tf_op jit(solution)/shard_map/ppermute | solution.py:370
  35.4 1.6 %gather2.1 = (bf16[2048,384]{1,0:T(8,128)(2,1)S(1)}, bf16[384,512]{1,0:T(8,128)(2,1)S(1)}) custom-call(bf16[768,384]{1,0:T(8,128)(2,1)S(1)} %get-tuple-element.39.pick_ref, f32[384,1024]{1,0:T(8,128)S(1)} %get-tuple-element.48.sums_ref, bf16[32,1024]{1,0:T(8,128)(2,1)S(1)} %collective-permute-done.6.ba_ref, ...), custom_call_target="tpu_custom_call" | custom-call | flops 603979776 | bytes 3178496 | tf_op jit(solution)/shard_map/gather2/pallas_call | solution.py:341
  37.0 0.7 %collective-permute-done.11.ac_ref = bf16[32,1024]{1,0:T(8,128)(2,1)S(1)} collective-permute-done((bf16[32,1024]{1,0:T(8,128)(2,1)S(1)}, bf16[32,1024]{1,0:T(8,128)(2,1)S(1)}, u32[]{:S(2)}, u32[]{:S(2)}) %collective-permute-start.11) | collective-permute-done | bytes 65568 | tf_op jit(solution)/shard_map/ppermute | solution.py:370
  37.7 2.7 %operator2.1 = (bf16[768,1024]{1,0:T(8,128)(2,1)S(1)}, bf16[32,1024]{1,0:T(8,128)(2,1)S(1)}, bf16[32,1024]{1,0:T(8,128)(2,1)S(1)}, bf16[32,1024]{1,0:T(8,128)(2,1)S(1)}, bf16[2048,384]{1,0:T(8,128)(2,1)S(1)}) custom-call(bf16[384,256]{1,0:T(8,128)(2,1)S(1)} %get-tuple-element.38.pick_ref, bf16[512,768]{1,0:T(8,128)(2,1)S(1)} %get-tuple-element.37.spread_ref, ...), custom_call_target="tpu_custom_call" | custom-call | flops 1207959552 | bytes 3473408 | tf_op jit(solution)/shard_map/operator2/pallas_call | solution.py:341
  40.4 2.8 %collective-permute-start.12 = (bf16[32,1024]{1,0:T(8,128)(2,1)S(1)}, bf16[32,1024]{1,0:T(8,128)(2,1)S(1)}, u32[]{:S(2)}, u32[]{:S(2)}) collective-permute-start(bf16[32,1024]{1,0:T(8,128)(2,1)S(1)} %get-tuple-element.66), channel_id=1, source_target_pairs={{0,8},{4,12},{8,0},{12,4},{1,9},{5,13},{9,1},{13,5},{2,10},{6,14},... | collective-permute-start | bytes 196616 | tf_op jit(solution)/shard_map/ppermute | solution.py:370
  43.2 0.7 %collective-permute-start.13 = (bf16[32,1024]{1,0:T(8,128)(2,1)S(1)}, bf16[32,1024]{1,0:T(8,128)(2,1)S(1)}, u32[]{:S(2)}, u32[]{:S(2)}) collective-permute-start(bf16[32,1024]{1,0:T(8,128)(2,1)S(1)} %get-tuple-element.67), channel_id=1, source_target_pairs={{4,8},{8,4},{5,9},{9,5},{6,10},{10,6},{7,11},{11,7},{20,24},{24,20... | collective-permute-start | bytes 196616 | tf_op jit(solution)/shard_map/ppermute | solution.py:370
  43.8 2.1 %collective-permute-start.14 = (bf16[32,1024]{1,0:T(8,128)(2,1)S(1)}, bf16[32,1024]{1,0:T(8,128)(2,1)S(1)}, u32[]{:S(2)}, u32[]{:S(2)}) collective-permute-start(bf16[32,1024]{1,0:T(8,128)(2,1)S(1)} %get-tuple-element.68), channel_id=1, source_target_pairs={{0,4},{4,0},{8,12},{12,8},{1,5},{5,1},{9,13},{13,9},{2,6},{6,2},{1... | collective-permute-start | bytes 196616 | tf_op jit(solution)/shard_map/ppermute | solution.py:370
  45.9 2.1 %finish.1 = (f32[384,1024]{1,0:T(8,128)S(1)}, bf16[128,8192]{1,0:T(8,128)(2,1)}) custom-call(bf16[512,768]{1,0:T(8,128)(2,1)S(1)} %get-tuple-element.37.spread_ref, bf16[768,1024]{1,0:T(8,128)(2,1)S(1)} %get-tuple-element.62.y_ref, bf16[2048,384]{1,0:T(8,128)(2,1)S(1)} %get-tuple-element.63.x_ref, bf16[384,512]{1,0:T(8,128)(2,1)S(1)} %get-tuple-element.64.lift_ref), custom_call_target="tpu_custom_call" | custom-call | flops 805306368 | bytes 4325376 | tf_op jit(solution)/shard_map/finish/pallas_call | solution.py:341
  48.2 1.1 %last.1 = bf16[384,1024]{1,0:T(8,128)(2,1)} custom-call(f32[384,1024]{1,0:T(8,128)S(1)} %get-tuple-element.65.own_ref, bf16[32,1024]{1,0:T(8,128)(2,1)S(1)} %collective-permute-done.12.ba_ref, bf16[32,1024]{1,0:T(8,128)(2,1)S(1)} %collective-permute-done.13.bb_ref, bf16[32,1024]{1,0:T(8,128)(2,1)S(1)} %collective-permute-done.14.bc_ref, ...), custom_call_target="tpu_custom_call" | custom-call | flops 100663296 | bytes 1867776 | tf_op jit(solution)/shard_map/last/pallas_call | solution.py:341
  (22 shorter events, 2.1 us)
Async XLA Ops:
  0.6 16.6 %copy-start = (s32[128,6]{0,1:T(8,128)S(1)}, s32[128,6]{0,1:T(8,128)}, u32[]{:S(2)}) copy-start(s32[128,6]{0,1:T(8,128)} %param.15) | copy-start | bytes 9220
  0.6 16.6 %copy-start.2 = (f32[128]{0:T(128)S(1)}, f32[128]{0:T(128)}, u32[]{:S(2)}) copy-start(f32[128]{0:T(128)} %param.14) | copy-start | bytes 1540
  0.7 16.6 %copy-start.1 = (f32[128]{0:T(128)S(1)}, f32[128]{0:T(128)}, u32[]{:S(2)}) copy-start(f32[128]{0:T(128)} %param.13) | copy-start | bytes 1540
  0.7 9.3 %collective-permute-start.2 = (s32[3,1,32]{2,1,0:T(1,128)}, s32[3,1,32]{2,1,0:T(1,128)S(1)}, u32[]{:S(2)}, u32[]{:S(2)}) collective-permute-start(s32[3,1,32]{2,1,0:T(1,128)} %bitcast.8), channel_id=1, source_target_pairs={{0,8},{4,12},{8,0},{12,4},{1,9},{5,13},{9,1},{13,5},{2,10},{6,14},... | collective-permute-start | bytes 1160 | tf_op jit(solution)/shard_map/ppermute | solution.py:370
  4.8 5.2 %collective-permute-start.1 = (s32[3,1,32]{2,1,0:T(1,128)}, s32[3,1,32]{2,1,0:T(1,128)S(1)}, u32[]{:S(2)}, u32[]{:S(2)}) collective-permute-start(s32[3,1,32]{2,1,0:T(1,128)} %bitcast.9), channel_id=1, source_target_pairs={{4,8},{8,4},{5,9},{9,5},{6,10},{10,6},{7,11},{11,7},{20,24},{24,20... | collective-permute-start | bytes 1160 | tf_op jit(solution)/shard_map/ppermute | solution.py:370
  5.4 4.7 %collective-permute-start = (s32[3,1,32]{2,1,0:T(1,128)}, s32[3,1,32]{2,1,0:T(1,128)S(1)}, u32[]{:S(2)}, u32[]{:S(2)}) collective-permute-start(s32[3,1,32]{2,1,0:T(1,128)} %bitcast.10), channel_id=1, source_target_pairs={{0,4},{4,0},{8,12},{12,8},{1,5},{5,1},{9,13},{13,9},{2,6},{6,2},{1... | collective-permute-start | bytes 1160 | tf_op jit(solution)/shard_map/ppermute | solution.py:370
  10.5 8.1 %collective-permute-start.3 = (bf16[32,1024]{1,0:T(8,128)(2,1)S(1)}, bf16[32,1024]{1,0:T(8,128)(2,1)S(1)}, u32[]{:S(2)}, u32[]{:S(2)}) collective-permute-start(bf16[32,1024]{1,0:T(8,128)(2,1)S(1)} %get-tuple-element.41), channel_id=1, source_target_pairs={{0,8},{4,12},{8,0},{12,4},{1,9},{5,13},{9,1},{13,5},{2,10},{6,14},... | collective-permute-start | bytes 196616 | tf_op jit(solution)/shard_map/ppermute | solution.py:370
  14.0 4.6 %collective-permute-start.4 = (bf16[32,1024]{1,0:T(8,128)(2,1)S(1)}, bf16[32,1024]{1,0:T(8,128)(2,1)S(1)}, u32[]{:S(2)}, u32[]{:S(2)}) collective-permute-start(bf16[32,1024]{1,0:T(8,128)(2,1)S(1)} %get-tuple-element.42), channel_id=1, source_target_pairs={{4,8},{8,4},{5,9},{9,5},{6,10},{10,6},{7,11},{11,7},{20,24},{24,20... | collective-permute-start | bytes 196616 | tf_op jit(solution)/shard_map/ppermute | solution.py:370
  14.7 4.3 %collective-permute-start.5 = (bf16[32,1024]{1,0:T(8,128)(2,1)S(1)}, bf16[32,1024]{1,0:T(8,128)(2,1)S(1)}, u32[]{:S(2)}, u32[]{:S(2)}) collective-permute-start(bf16[32,1024]{1,0:T(8,128)(2,1)S(1)} %get-tuple-element.43), channel_id=1, source_target_pairs={{0,4},{4,0},{8,12},{12,8},{1,5},{5,1},{9,13},{13,9},{2,6},{6,2},{1... | collective-permute-start | bytes 196616 | tf_op jit(solution)/shard_map/ppermute | solution.py:370
  21.8 6.8 %collective-permute-start.6 = (bf16[32,1024]{1,0:T(8,128)(2,1)S(1)}, bf16[32,1024]{1,0:T(8,128)(2,1)S(1)}, u32[]{:S(2)}, u32[]{:S(2)}) collective-permute-start(bf16[32,1024]{1,0:T(8,128)(2,1)S(1)} %get-tuple-element.49), channel_id=1, source_target_pairs={{0,8},{4,12},{8,0},{12,4},{1,9},{5,13},{9,1},{13,5},{2,10},{6,14},... | collective-permute-start | bytes 196616 | tf_op jit(solution)/shard_map/ppermute | solution.py:370
  24.5 4.0 %collective-permute-start.7 = (bf16[32,1024]{1,0:T(8,128)(2,1)S(1)}, bf16[32,1024]{1,0:T(8,128)(2,1)S(1)}, u32[]{:S(2)}, u32[]{:S(2)}) collective-permute-start(bf16[32,1024]{1,0:T(8,128)(2,1)S(1)} %get-tuple-element.50), channel_id=1, source_target_pairs={{4,8},{8,4},{5,9},{9,5},{6,10},{10,6},{7,11},{11,7},{20,24},{24,20... | collective-permute-start | bytes 196616 | tf_op jit(solution)/shard_map/ppermute | solution.py:370
  25.2 4.3 %collective-permute-start.8 = (bf16[32,1024]{1,0:T(8,128)(2,1)S(1)}, bf16[32,1024]{1,0:T(8,128)(2,1)S(1)}, u32[]{:S(2)}, u32[]{:S(2)}) collective-permute-start(bf16[32,1024]{1,0:T(8,128)(2,1)S(1)} %get-tuple-element.51), channel_id=1, source_target_pairs={{0,4},{4,0},{8,12},{12,8},{1,5},{5,1},{9,13},{13,9},{2,6},{6,2},{1... | collective-permute-start | bytes 196616 | tf_op jit(solution)/shard_map/ppermute | solution.py:370
  29.9 7.1 %collective-permute-start.9 = (bf16[32,1024]{1,0:T(8,128)(2,1)S(1)}, bf16[32,1024]{1,0:T(8,128)(2,1)S(1)}, u32[]{:S(2)}, u32[]{:S(2)}) collective-permute-start(bf16[32,1024]{1,0:T(8,128)(2,1)S(1)} %get-tuple-element.59), channel_id=1, source_target_pairs={{0,8},{4,12},{8,0},{12,4},{1,9},{5,13},{9,1},{13,5},{2,10},{6,14},... | collective-permute-start | bytes 196616 | tf_op jit(solution)/shard_map/ppermute | solution.py:370
  32.7 4.3 %collective-permute-start.10 = (bf16[32,1024]{1,0:T(8,128)(2,1)S(1)}, bf16[32,1024]{1,0:T(8,128)(2,1)S(1)}, u32[]{:S(2)}, u32[]{:S(2)}) collective-permute-start(bf16[32,1024]{1,0:T(8,128)(2,1)S(1)} %get-tuple-element.60), channel_id=1, source_target_pairs={{4,8},{8,4},{5,9},{9,5},{6,10},{10,6},{7,11},{11,7},{20,24},{24,20... | collective-permute-start | bytes 196616 | tf_op jit(solution)/shard_map/ppermute | solution.py:370
  33.3 4.3 %collective-permute-start.11 = (bf16[32,1024]{1,0:T(8,128)(2,1)S(1)}, bf16[32,1024]{1,0:T(8,128)(2,1)S(1)}, u32[]{:S(2)}, u32[]{:S(2)}) collective-permute-start(bf16[32,1024]{1,0:T(8,128)(2,1)S(1)} %get-tuple-element.61), channel_id=1, source_target_pairs={{0,4},{4,0},{8,12},{12,8},{1,5},{5,1},{9,13},{13,9},{2,6},{6,2},{1... | collective-permute-start | bytes 196616 | tf_op jit(solution)/shard_map/ppermute | solution.py:370
  40.4 7.6 %collective-permute-start.12 = (bf16[32,1024]{1,0:T(8,128)(2,1)S(1)}, bf16[32,1024]{1,0:T(8,128)(2,1)S(1)}, u32[]{:S(2)}, u32[]{:S(2)}) collective-permute-start(bf16[32,1024]{1,0:T(8,128)(2,1)S(1)} %get-tuple-element.66), channel_id=1, source_target_pairs={{0,8},{4,12},{8,0},{12,4},{1,9},{5,13},{9,1},{13,5},{2,10},{6,14},... | collective-permute-start | bytes 196616 | tf_op jit(solution)/shard_map/ppermute | solution.py:370
  43.2 4.9 %collective-permute-start.13 = (bf16[32,1024]{1,0:T(8,128)(2,1)S(1)}, bf16[32,1024]{1,0:T(8,128)(2,1)S(1)}, u32[]{:S(2)}, u32[]{:S(2)}) collective-permute-start(bf16[32,1024]{1,0:T(8,128)(2,1)S(1)} %get-tuple-element.67), channel_id=1, source_target_pairs={{4,8},{8,4},{5,9},{9,5},{6,10},{10,6},{7,11},{11,7},{20,24},{24,20... | collective-permute-start | bytes 196616 | tf_op jit(solution)/shard_map/ppermute | solution.py:370
  43.8 4.3 %collective-permute-start.14 = (bf16[32,1024]{1,0:T(8,128)(2,1)S(1)}, bf16[32,1024]{1,0:T(8,128)(2,1)S(1)}, u32[]{:S(2)}, u32[]{:S(2)}) collective-permute-start(bf16[32,1024]{1,0:T(8,128)(2,1)S(1)} %get-tuple-element.68), channel_id=1, source_target_pairs={{0,4},{4,0},{8,12},{12,8},{1,5},{5,1},{9,13},{13,9},{2,6},{6,2},{1... | collective-permute-start | bytes 196616 | tf_op jit(solution)/shard_map/ppermute | solution.py:370

commit v6 on v5

--- a/solution.py
+++ b/solution.py
@@ -354,25 +354,30 @@
     return pltpu.with_memory_space_constraint(array, HBM)
 
 
-def pairings(size):
-    def both(pairs):
-        return [pair for a, b in pairs for pair in ((a, b), (b, a))]
-
-    even = both([(i, i + 1) for i in range(0, size - 1, 2)])
-    odd = both([(i, i + 1) for i in range(1, size - 1, 2)])
-    opposite = [(i, (i + size // 2) % size) for i in range(size)]
-    return (opposite, odd, even)
-
-
-def exchange(arrays, size, reverse=False):
-    ways = pairings(size)
-    order = (2, 1, 0) if reverse else (0, 1, 2)
-    got = {c: lax.ppermute(arrays[c], "elem", ways[c]) for c in order}
-    return [got[c] for c in range(3)]
+def pairings(size, cores):
+    opposite = {i: (i + size // 2) % size for i in range(size)}
+    ways = [opposite]
+    for first in (1, 0):
+        way = {}
+        for i in range(first, size - 1, 2):
+            way[i], way[i + 1] = i + 1, i
+        ways.append(way)
+    return [
+        [
+            (i * cores + k, way[i] * cores + k if i in way else i * cores + (k + 1) % cores)
+            for i in range(size)
+            for k in range(cores)
+        ]
+        for way in ways
+    ]
+
+
+def exchange(arrays, sizes):
+    return [lax.ppermute(a, ("elem", "sub"), p) for a, p in zip(arrays, pairings(*sizes))]
 
 
 def per_device(
-    size,
+    sizes,
     trace_rhs,
     face_scale,
     stiff_scale,
@@ -394,7 +399,7 @@
     halo_rows = LANES
     ext_rows = faces + halo_rows
     slots_all = 6 * elems
-    lists = exchange([halo_faces.transpose(1, 0, 2)] * 3, size, reverse=True)
+    lists = exchange([halo_faces.transpose(1, 0, 2)] * 3, sizes)
     par = (lax.axis_index("elem") % 2).astype(I32).reshape(1)
     stiff_row = stiff_scale.reshape(1, elems)
     mass_row = mass_scale.reshape(1, elems)
@@ -435,7 +440,7 @@
         2 * LANES * faces * width,
         "send",
     )
-    arrived = exchange(outgoing, size)
+    arrived = exchange(outgoing, sizes)
     gather_flops = 2 * slots_all * faces * width
     tile = (LANES, LANES)
     own_x, own_pick, halo_pick, spread, element_scales = call(
@@ -467,7 +472,7 @@
         )
 
     y, *back = operator(own_x, arrived, False, "operator1")
-    returned = exchange(back, size)
+    returned = exchange(back, sizes)
     own, own_rows, same, give, request_scale = call(
         sums_kernel,
         [par, spread, y, *lists[::-1], scale],
@@ -492,7 +497,7 @@
         2 * LANES * width * 256,
         "middle",
     )
-    arrived = exchange(outgoing, size)
+    arrived = exchange(outgoing, sizes)
     own_x, lift = call(
         second_gather_kernel,
         [own_pick, own, *returned, give, face_scales, block, in_hbm(lifting)],
@@ -503,7 +508,7 @@
         "gather2",
     )
     y, *back, x = operator(own_x, arrived, True, "operator2")
-    returned = exchange(back, size)
+    returned = exchange(back, sizes)
     own, interior = call(
         finish_kernel,
         [spread, y, x, lift],
@@ -551,7 +556,7 @@
         P(),
     )
     return jax.shard_map(
-        functools.partial(per_device, mesh.shape["elem"]),
+        functools.partial(per_device, (mesh.shape["elem"], mesh.shape["sub"])),
         mesh=mesh,
         in_specs=in_specs,
         out_specs=(split, split),

time: 49.6 us -> 43.7 us (0.88)
  starting transfers between devices: 30.3 us -> 20.1 us
  waiting for transfers between devices: 2.32 us -> 6.88 us
    ppermute x15, starting transfers between devices: 30.3 us -> 20.1 us  [exchange(): lax.ppermute(a, ('elem', 'sub'), p)]
    ppermute x15, waiting for transfers between devices: 2.32 us -> 6.88 us  [exchange(): lax.ppermute(a, ('elem', 'sub'), p)]
  transfers between devices with their start and end apart: 15 -> 15, of which waited for: 5 -> 7; matrix products, arithmetic and copies ran while one was open for 0% -> 0% of each run, Pallas kernels for 16% -> 18%
where the time goes in v6:
time: 43.7 us; the launch traced here: 43.5 us
  starting transfers between devices  20.1 us (46%)
  Pallas kernels  15.1 us (35%)
  waiting for transfers between devices  6.88 us (16%)
  between operations  1.44 us (3%)
    ppermute x15, starting transfers between devices, exchange(): lax.ppermute(a, ('elem', 'sub'), p)  20.1 us
    pallas_call x10, Pallas kernels, call(): pl.pallas_call(kernel, out_shape=[jax.ShapeDtypeStruct(s, d) for s, d in...  15.1 us
    ppermute x15, waiting for transfers between devices, exchange(): lax.ppermute(a, ('elem', 'sub'), p)  6.88 us
  transfers between devices with their start and end apart: 15, of which 7 were waited for; matrix products, arithmetic and copies ran while one was open for 0% of the time, Pallas kernels for 18%

profile of v6, /device:TPU:0, one launch (start us, length us, event | category | flops | bytes accessed | tf_op | source)
XLA Modules:
  0.0 43.5 jit_solution(14960105893516026358)
XLA Ops:
  0.7 4.1 %collective-permute-start.2 = (s32[3,1,32]{2,1,0:T(1,128)}, s32[3,1,32]{2,1,0:T(1,128)S(1)}, u32[]{:S(2)}, u32[]{:S(2)}) collective-permute-start(s32[3,1,32]{2,1,0:T(1,128)} %bitcast.8), channel_id=1, source_target_pairs={{0,8},{1,9},{4,12},{5,13},{8,0},{9,1},{12,4},{13,5},{2,10},{3,11},... | collective-permute-start | bytes 1160 | tf_op jit(solution)/shard_map/ppermute | solution.py:376
  4.8 1.6 %collective-permute-start = (s32[3,1,32]{2,1,0:T(1,128)}, s32[3,1,32]{2,1,0:T(1,128)S(1)}, u32[]{:S(2)}, u32[]{:S(2)}) collective-permute-start(s32[3,1,32]{2,1,0:T(1,128)} %bitcast.10), channel_id=1, source_target_pairs={{0,4},{1,5},{4,0},{5,1},{8,12},{9,13},{12,8},{13,9},{2,6},{3,7},{6... | collective-permute-start | bytes 1160 | tf_op jit(solution)/shard_map/ppermute | solution.py:376
  6.3 1.6 %prepare.1 = (bf16[384,1024]{1,0:T(8,128)(2,1)S(1)}, bf16[256,256]{1,0:T(8,128)(2,1)S(1)}, f32[1,384]{1,0:T(1,128)S(1)}, f32[384,128]{1,0:T(8,128)S(1)}, bf16[384,768]{1,0:T(8,128)(2,1)S(1)}) custom-call(bf16[384,1024]{1,0:T(8,128)(2,1)} %rhs_hbm.1, bf16[64,64]{1,0:T(8,128)(2,1)} %jacobi_hbm.1, f32[384]{0:T(512)} %scale_hbm.1, bf16[384,384]{1,0:T(8,128)(2,1)} %stiff_hbm.1, ...), custom_call_target="tpu_custom_call" | custom-call | flops 201326592 | bytes 1385984 | tf_op jit(solution)/shard_map/prepare/pallas_call | solution.py:341
  8.0 0.6 %collective-permute-done.ec_ref = s32[3,1,32]{2,1,0:T(1,128)S(1)} collective-permute-done((s32[3,1,32]{2,1,0:T(1,128)}, s32[3,1,32]{2,1,0:T(1,128)S(1)}, u32[]{:S(2)}, u32[]{:S(2)}) %collective-permute-start) | collective-permute-done | bytes 416 | tf_op jit(solution)/shard_map/ppermute | solution.py:376
  8.6 0.4 send.1
  9.0 3.1 %collective-permute-start.3 = (bf16[32,1024]{1,0:T(8,128)(2,1)S(1)}, bf16[32,1024]{1,0:T(8,128)(2,1)S(1)}, u32[]{:S(2)}, u32[]{:S(2)}) collective-permute-start(bf16[32,1024]{1,0:T(8,128)(2,1)S(1)} %get-tuple-element.41), channel_id=1, source_target_pairs={{0,8},{1,9},{4,12},{5,13},{8,0},{9,1},{12,4},{13,5},{2,10},{3,11},... | collective-permute-start | bytes 196616 | tf_op jit(solution)/shard_map/ppermute | solution.py:376
  12.1 0.6 %collective-permute-start.5 = (bf16[32,1024]{1,0:T(8,128)(2,1)S(1)}, bf16[32,1024]{1,0:T(8,128)(2,1)S(1)}, u32[]{:S(2)}, u32[]{:S(2)}) collective-permute-start(bf16[32,1024]{1,0:T(8,128)(2,1)S(1)} %get-tuple-element.43), channel_id=1, source_target_pairs={{0,4},{1,5},{4,0},{5,1},{8,12},{9,13},{12,8},{13,9},{2,6},{3,7},{6... | collective-permute-start | bytes 196616 | tf_op jit(solution)/shard_map/ppermute | solution.py:376
  13.4 1.3 %gather1.1 = (bf16[2048,384]{1,0:T(8,128)(2,1)S(1)}, bf16[768,384]{1,0:T(8,128)(2,1)S(1)}, bf16[384,256]{1,0:T(8,128)(2,1)S(1)}, bf16[512,768]{1,0:T(8,128)(2,1)S(1)}, f32[2,128,128]{2,1,0:T(8,128)S(1)}) custom-call(s32[1]{0:T(128)} %bitcast.par_ref, s32[1]{0:T(128)S(6)} %copy.13.count_ref, bf16[384,1024]{1,0:T(8,128)(2,1)S(1)} %get-tuple-element.36.z_ref, ...), custom_call_target="tpu_custom_call" | custom-call | flops 603979776 | bytes 790536 | tf_op jit(solution)/shard_map/gather1/pallas_call | solution.py:341
  14.9 1.7 %collective-permute-done.5.ac_ref = bf16[32,1024]{1,0:T(8,128)(2,1)S(1)} collective-permute-done((bf16[32,1024]{1,0:T(8,128)(2,1)S(1)}, bf16[32,1024]{1,0:T(8,128)(2,1)S(1)}, u32[]{:S(2)}, u32[]{:S(2)}) %collective-permute-start.5) | collective-permute-done | bytes 65568 | tf_op jit(solution)/shard_map/ppermute | solution.py:376
  16.6 2.7 %operator1.1 = (bf16[768,1024]{1,0:T(8,128)(2,1)S(1)}, bf16[32,1024]{1,0:T(8,128)(2,1)S(1)}, bf16[32,1024]{1,0:T(8,128)(2,1)S(1)}, bf16[32,1024]{1,0:T(8,128)(2,1)S(1)}) custom-call(bf16[384,256]{1,0:T(8,128)(2,1)S(1)} %get-tuple-element.38.pick_ref, bf16[512,768]{1,0:T(8,128)(2,1)S(1)} %get-tuple-element.37.spread_ref, ...), custom_call_target="tpu_custom_call" | custom-call | flops 1207959552 | bytes 3473408 | tf_op jit(solution)/shard_map/operator1/pallas_call | solution.py:341
  19.3 1.3 %collective-permute-start.6 = (bf16[32,1024]{1,0:T(8,128)(2,1)S(1)}, bf16[32,1024]{1,0:T(8,128)(2,1)S(1)}, u32[]{:S(2)}, u32[]{:S(2)}) collective-permute-start(bf16[32,1024]{1,0:T(8,128)(2,1)S(1)} %get-tuple-element.49), channel_id=1, source_target_pairs={{0,8},{1,9},{4,12},{5,13},{8,0},{9,1},{12,4},{13,5},{2,10},{3,11},... | collective-permute-start | bytes 196616 | tf_op jit(solution)/shard_map/ppermute | solution.py:376
  20.6 2.2 %collective-permute-start.8 = (bf16[32,1024]{1,0:T(8,128)(2,1)S(1)}, bf16[32,1024]{1,0:T(8,128)(2,1)S(1)}, u32[]{:S(2)}, u32[]{:S(2)}) collective-permute-start(bf16[32,1024]{1,0:T(8,128)(2,1)S(1)} %get-tuple-element.51), channel_id=1, source_target_pairs={{0,4},{1,5},{4,0},{5,1},{8,12},{9,13},{12,8},{13,9},{2,6},{3,7},{6... | collective-permute-start | bytes 196616 | tf_op jit(solution)/shard_map/ppermute | solution.py:376
  22.9 1.2 %sums1.1 = (f32[384,1024]{1,0:T(8,128)S(1)}, f32[128,1024]{1,0:T(8,128)S(1)}, bf16[128,128]{1,0:T(8,128)(2,1)S(1)}, bf16[384,128]{1,0:T(8,128)(2,1)S(1)}, f32[128,128]{1,0:T(8,128)S(1)}) custom-call(s32[1]{0:T(128)} %bitcast.par_ref, bf16[512,768]{1,0:T(8,128)(2,1)S(1)} %get-tuple-element.37.spread_ref, bf16[768,1024]{1,0:T(8,128)(2,1)S(1)} %get-tuple-element.46.y_ref, ...), custom_call_target="tpu_custom_call" | custom-call | flops 603979776 | bytes 2361988 | tf_op jit(solution)/shard_map/sums1/pallas_call | solution.py:341
  24.1 1.9 %collective-permute-done.6.ba_ref = bf16[32,1024]{1,0:T(8,128)(2,1)S(1)} collective-permute-done((bf16[32,1024]{1,0:T(8,128)(2,1)S(1)}, bf16[32,1024]{1,0:T(8,128)(2,1)S(1)}, u32[]{:S(2)}, u32[]{:S(2)}) %collective-permute-start.6) | collective-permute-done | bytes 65568 | tf_op jit(solution)/shard_map/ppermute | solution.py:376
  26.4 1.2 %collective-permute-start.9 = (bf16[32,1024]{1,0:T(8,128)(2,1)S(1)}, bf16[32,1024]{1,0:T(8,128)(2,1)S(1)}, u32[]{:S(2)}, u32[]{:S(2)}) collective-permute-start(bf16[32,1024]{1,0:T(8,128)(2,1)S(1)} %get-tuple-element.59), channel_id=1, source_target_pairs={{0,8},{1,9},{4,12},{5,13},{8,0},{9,1},{12,4},{13,5},{2,10},{3,11},... | collective-permute-start | bytes 196616 | tf_op jit(solution)/shard_map/ppermute | solution.py:376
  27.6 2.3 %collective-permute-start.11 = (bf16[32,1024]{1,0:T(8,128)(2,1)S(1)}, bf16[32,1024]{1,0:T(8,128)(2,1)S(1)}, u32[]{:S(2)}, u32[]{:S(2)}) collective-permute-start(bf16[32,1024]{1,0:T(8,128)(2,1)S(1)} %get-tuple-element.61), channel_id=1, source_target_pairs={{0,4},{1,5},{4,0},{5,1},{8,12},{9,13},{12,8},{13,9},{2,6},{3,7},{6... | collective-permute-start | bytes 196616 | tf_op jit(solution)/shard_map/ppermute | solution.py:376
  29.9 1.6 %gather2.1 = (bf16[2048,384]{1,0:T(8,128)(2,1)S(1)}, bf16[384,512]{1,0:T(8,128)(2,1)S(1)}) custom-call(bf16[768,384]{1,0:T(8,128)(2,1)S(1)} %get-tuple-element.39.pick_ref, f32[384,1024]{1,0:T(8,128)S(1)} %get-tuple-element.48.sums_ref, bf16[32,1024]{1,0:T(8,128)(2,1)S(1)} %collective-permute-done.6.ba_ref, ...), custom_call_target="tpu_custom_call" | custom-call | flops 603979776 | bytes 3178496 | tf_op jit(solution)/shard_map/gather2/pallas_call | solution.py:341
  31.5 1.5 %collective-permute-done.9.aa_ref = bf16[32,1024]{1,0:T(8,128)(2,1)S(1)} collective-permute-done((bf16[32,1024]{1,0:T(8,128)(2,1)S(1)}, bf16[32,1024]{1,0:T(8,128)(2,1)S(1)}, u32[]{:S(2)}, u32[]{:S(2)}) %collective-permute-start.9) | collective-permute-done | bytes 65568 | tf_op jit(solution)/shard_map/ppermute | solution.py:376
  33.1 2.7 %operator2.1 = (bf16[768,1024]{1,0:T(8,128)(2,1)S(1)}, bf16[32,1024]{1,0:T(8,128)(2,1)S(1)}, bf16[32,1024]{1,0:T(8,128)(2,1)S(1)}, bf16[32,1024]{1,0:T(8,128)(2,1)S(1)}, bf16[2048,384]{1,0:T(8,128)(2,1)S(1)}) custom-call(bf16[384,256]{1,0:T(8,128)(2,1)S(1)} %get-tuple-element.38.pick_ref, bf16[512,768]{1,0:T(8,128)(2,1)S(1)} %get-tuple-element.37.spread_ref, ...), custom_call_target="tpu_custom_call" | custom-call | flops 1207959552 | bytes 3473408 | tf_op jit(solution)/shard_map/operator2/pallas_call | solution.py:341
  35.8 1.4 %collective-permute-start.12 = (bf16[32,1024]{1,0:T(8,128)(2,1)S(1)}, bf16[32,1024]{1,0:T(8,128)(2,1)S(1)}, u32[]{:S(2)}, u32[]{:S(2)}) collective-permute-start(bf16[32,1024]{1,0:T(8,128)(2,1)S(1)} %get-tuple-element.66), channel_id=1, source_target_pairs={{0,8},{1,9},{4,12},{5,13},{8,0},{9,1},{12,4},{13,5},{2,10},{3,11},... | collective-permute-start | bytes 196616 | tf_op jit(solution)/shard_map/ppermute | solution.py:376
  37.2 2.1 %collective-permute-start.14 = (bf16[32,1024]{1,0:T(8,128)(2,1)S(1)}, bf16[32,1024]{1,0:T(8,128)(2,1)S(1)}, u32[]{:S(2)}, u32[]{:S(2)}) collective-permute-start(bf16[32,1024]{1,0:T(8,128)(2,1)S(1)} %get-tuple-element.68), channel_id=1, source_target_pairs={{0,4},{1,5},{4,0},{5,1},{8,12},{9,13},{12,8},{13,9},{2,6},{3,7},{6... | collective-permute-start | bytes 196616 | tf_op jit(solution)/shard_map/ppermute | solution.py:376
  39.4 2.1 %finish.1 = (f32[384,1024]{1,0:T(8,128)S(1)}, bf16[128,8192]{1,0:T(8,128)(2,1)}) custom-call(bf16[512,768]{1,0:T(8,128)(2,1)S(1)} %get-tuple-element.37.spread_ref, bf16[768,1024]{1,0:T(8,128)(2,1)S(1)} %get-tuple-element.62.y_ref, bf16[2048,384]{1,0:T(8,128)(2,1)S(1)} %get-tuple-element.63.x_ref, bf16[384,512]{1,0:T(8,128)(2,1)S(1)} %get-tuple-element.64.lift_ref), custom_call_target="tpu_custom_call" | custom-call | flops 805306368 | bytes 4325376 | tf_op jit(solution)/shard_map/finish/pallas_call | solution.py:341
  41.5 1.0 %collective-permute-done.12.ba_ref = bf16[32,1024]{1,0:T(8,128)(2,1)S(1)} collective-permute-done((bf16[32,1024]{1,0:T(8,128)(2,1)S(1)}, bf16[32,1024]{1,0:T(8,128)(2,1)S(1)}, u32[]{:S(2)}, u32[]{:S(2)}) %collective-permute-start.12) | collective-permute-done | bytes 65568 | tf_op jit(solution)/shard_map/ppermute | solution.py:376
  42.4 1.1 %last.1 = bf16[384,1024]{1,0:T(8,128)(2,1)} custom-call(f32[384,1024]{1,0:T(8,128)S(1)} %get-tuple-element.65.own_ref, bf16[32,1024]{1,0:T(8,128)(2,1)S(1)} %collective-permute-done.12.ba_ref, bf16[32,1024]{1,0:T(8,128)(2,1)S(1)} %collective-permute-done.13.bb_ref, bf16[32,1024]{1,0:T(8,128)(2,1)S(1)} %collective-permute-done.14.bc_ref, ...), custom_call_target="tpu_custom_call" | custom-call | flops 100663296 | bytes 1867776 | tf_op jit(solution)/shard_map/last/pallas_call | solution.py:341
  (22 shorter events, 0.6 us)
Async XLA Ops:
  0.6 12.7 %copy-start = (s32[128,6]{0,1:T(8,128)S(1)}, s32[128,6]{0,1:T(8,128)}, u32[]{:S(2)}) copy-start(s32[128,6]{0,1:T(8,128)} %param.15) | copy-start | bytes 9220
  0.6 12.7 %copy-start.2 = (f32[128]{0:T(128)S(1)}, f32[128]{0:T(128)}, u32[]{:S(2)}) copy-start(f32[128]{0:T(128)} %param.14) | copy-start | bytes 1540
  0.7 12.7 %copy-start.1 = (f32[128]{0:T(128)S(1)}, f32[128]{0:T(128)}, u32[]{:S(2)}) copy-start(f32[128]{0:T(128)} %param.13) | copy-start | bytes 1540
  0.7 7.3 %collective-permute-start.2 = (s32[3,1,32]{2,1,0:T(1,128)}, s32[3,1,32]{2,1,0:T(1,128)S(1)}, u32[]{:S(2)}, u32[]{:S(2)}) collective-permute-start(s32[3,1,32]{2,1,0:T(1,128)} %bitcast.8), channel_id=1, source_target_pairs={{0,8},{1,9},{4,12},{5,13},{8,0},{9,1},{12,4},{13,5},{2,10},{3,11},... | collective-permute-start | bytes 1160 | tf_op jit(solution)/shard_map/ppermute | solution.py:376
  4.8 3.2 %collective-permute-start.1 = (s32[3,1,32]{2,1,0:T(1,128)}, s32[3,1,32]{2,1,0:T(1,128)S(1)}, u32[]{:S(2)}, u32[]{:S(2)}) collective-permute-start(s32[3,1,32]{2,1,0:T(1,128)} %bitcast.9), channel_id=1, source_target_pairs={{0,1},{1,0},{4,8},{5,9},{8,4},{9,5},{12,13},{13,12},{2,3},{3,2},{6... | collective-permute-start | bytes 1160 | tf_op jit(solution)/shard_map/ppermute | solution.py:376
  4.8 3.8 %collective-permute-start = (s32[3,1,32]{2,1,0:T(1,128)}, s32[3,1,32]{2,1,0:T(1,128)S(1)}, u32[]{:S(2)}, u32[]{:S(2)}) collective-permute-start(s32[3,1,32]{2,1,0:T(1,128)} %bitcast.10), channel_id=1, source_target_pairs={{0,4},{1,5},{4,0},{5,1},{8,12},{9,13},{12,8},{13,9},{2,6},{3,7},{6... | collective-permute-start | bytes 1160 | tf_op jit(solution)/shard_map/ppermute | solution.py:376
  9.0 5.9 %collective-permute-start.3 = (bf16[32,1024]{1,0:T(8,128)(2,1)S(1)}, bf16[32,1024]{1,0:T(8,128)(2,1)S(1)}, u32[]{:S(2)}, u32[]{:S(2)}) collective-permute-start(bf16[32,1024]{1,0:T(8,128)(2,1)S(1)} %get-tuple-element.41), channel_id=1, source_target_pairs={{0,8},{1,9},{4,12},{5,13},{8,0},{9,1},{12,4},{13,5},{2,10},{3,11},... | collective-permute-start | bytes 196616 | tf_op jit(solution)/shard_map/ppermute | solution.py:376
  12.1 2.8 %collective-permute-start.4 = (bf16[32,1024]{1,0:T(8,128)(2,1)S(1)}, bf16[32,1024]{1,0:T(8,128)(2,1)S(1)}, u32[]{:S(2)}, u32[]{:S(2)}) collective-permute-start(bf16[32,1024]{1,0:T(8,128)(2,1)S(1)} %get-tuple-element.42), channel_id=1, source_target_pairs={{0,1},{1,0},{4,8},{5,9},{8,4},{9,5},{12,13},{13,12},{2,3},{3,2},{6... | collective-permute-start | bytes 196616 | tf_op jit(solution)/shard_map/ppermute | solution.py:376
  12.1 4.5 %collective-permute-start.5 = (bf16[32,1024]{1,0:T(8,128)(2,1)S(1)}, bf16[32,1024]{1,0:T(8,128)(2,1)S(1)}, u32[]{:S(2)}, u32[]{:S(2)}) collective-permute-start(bf16[32,1024]{1,0:T(8,128)(2,1)S(1)} %get-tuple-element.43), channel_id=1, source_target_pairs={{0,4},{1,5},{4,0},{5,1},{8,12},{9,13},{12,8},{13,9},{2,6},{3,7},{6... | collective-permute-start | bytes 196616 | tf_op jit(solution)/shard_map/ppermute | solution.py:376
  19.3 6.7 %collective-permute-start.6 = (bf16[32,1024]{1,0:T(8,128)(2,1)S(1)}, bf16[32,1024]{1,0:T(8,128)(2,1)S(1)}, u32[]{:S(2)}, u32[]{:S(2)}) collective-permute-start(bf16[32,1024]{1,0:T(8,128)(2,1)S(1)} %get-tuple-element.49), channel_id=1, source_target_pairs={{0,8},{1,9},{4,12},{5,13},{8,0},{9,1},{12,4},{13,5},{2,10},{3,11},... | collective-permute-start | bytes 196616 | tf_op jit(solution)/shard_map/ppermute | solution.py:376
  20.6 5.3 %collective-permute-start.7 = (bf16[32,1024]{1,0:T(8,128)(2,1)S(1)}, bf16[32,1024]{1,0:T(8,128)(2,1)S(1)}, u32[]{:S(2)}, u32[]{:S(2)}) collective-permute-start(bf16[32,1024]{1,0:T(8,128)(2,1)S(1)} %get-tuple-element.50), channel_id=1, source_target_pairs={{0,1},{1,0},{4,8},{5,9},{8,4},{9,5},{12,13},{13,12},{2,3},{3,2},{6... | collective-permute-start | bytes 196616 | tf_op jit(solution)/shard_map/ppermute | solution.py:376
  20.6 5.4 %collective-permute-start.8 = (bf16[32,1024]{1,0:T(8,128)(2,1)S(1)}, bf16[32,1024]{1,0:T(8,128)(2,1)S(1)}, u32[]{:S(2)}, u32[]{:S(2)}) collective-permute-start(bf16[32,1024]{1,0:T(8,128)(2,1)S(1)} %get-tuple-element.51), channel_id=1, source_target_pairs={{0,4},{1,5},{4,0},{5,1},{8,12},{9,13},{12,8},{13,9},{2,6},{3,7},{6... | collective-permute-start | bytes 196616 | tf_op jit(solution)/shard_map/ppermute | solution.py:376
  26.4 6.7 %collective-permute-start.9 = (bf16[32,1024]{1,0:T(8,128)(2,1)S(1)}, bf16[32,1024]{1,0:T(8,128)(2,1)S(1)}, u32[]{:S(2)}, u32[]{:S(2)}) collective-permute-start(bf16[32,1024]{1,0:T(8,128)(2,1)S(1)} %get-tuple-element.59), channel_id=1, source_target_pairs={{0,8},{1,9},{4,12},{5,13},{8,0},{9,1},{12,4},{13,5},{2,10},{3,11},... | collective-permute-start | bytes 196616 | tf_op jit(solution)/shard_map/ppermute | solution.py:376
  27.6 5.4 %collective-permute-start.10 = (bf16[32,1024]{1,0:T(8,128)(2,1)S(1)}, bf16[32,1024]{1,0:T(8,128)(2,1)S(1)}, u32[]{:S(2)}, u32[]{:S(2)}) collective-permute-start(bf16[32,1024]{1,0:T(8,128)(2,1)S(1)} %get-tuple-element.60), channel_id=1, source_target_pairs={{0,1},{1,0},{4,8},{5,9},{8,4},{9,5},{12,13},{13,12},{2,3},{3,2},{6... | collective-permute-start | bytes 196616 | tf_op jit(solution)/shard_map/ppermute | solution.py:376
  27.6 5.4 %collective-permute-start.11 = (bf16[32,1024]{1,0:T(8,128)(2,1)S(1)}, bf16[32,1024]{1,0:T(8,128)(2,1)S(1)}, u32[]{:S(2)}, u32[]{:S(2)}) collective-permute-start(bf16[32,1024]{1,0:T(8,128)(2,1)S(1)} %get-tuple-element.61), channel_id=1, source_target_pairs={{0,4},{1,5},{4,0},{5,1},{8,12},{9,13},{12,8},{13,9},{2,6},{3,7},{6... | collective-permute-start | bytes 196616 | tf_op jit(solution)/shard_map/ppermute | solution.py:376
  35.8 6.6 %collective-permute-start.12 = (bf16[32,1024]{1,0:T(8,128)(2,1)S(1)}, bf16[32,1024]{1,0:T(8,128)(2,1)S(1)}, u32[]{:S(2)}, u32[]{:S(2)}) collective-permute-start(bf16[32,1024]{1,0:T(8,128)(2,1)S(1)} %get-tuple-element.66), channel_id=1, source_target_pairs={{0,8},{1,9},{4,12},{5,13},{8,0},{9,1},{12,4},{13,5},{2,10},{3,11},... | collective-permute-start | bytes 196616 | tf_op jit(solution)/shard_map/ppermute | solution.py:376
  37.2 5.2 %collective-permute-start.13 = (bf16[32,1024]{1,0:T(8,128)(2,1)S(1)}, bf16[32,1024]{1,0:T(8,128)(2,1)S(1)}, u32[]{:S(2)}, u32[]{:S(2)}) collective-permute-start(bf16[32,1024]{1,0:T(8,128)(2,1)S(1)} %get-tuple-element.67), channel_id=1, source_target_pairs={{0,1},{1,0},{4,8},{5,9},{8,4},{9,5},{12,13},{13,12},{2,3},{3,2},{6... | collective-permute-start | bytes 196616 | tf_op jit(solution)/shard_map/ppermute | solution.py:376
  37.2 5.2 %collective-permute-start.14 = (bf16[32,1024]{1,0:T(8,128)(2,1)S(1)}, bf16[32,1024]{1,0:T(8,128)(2,1)S(1)}, u32[]{:S(2)}, u32[]{:S(2)}) collective-permute-start(bf16[32,1024]{1,0:T(8,128)(2,1)S(1)} %get-tuple-element.68), channel_id=1, source_target_pairs={{0,4},{1,5},{4,0},{5,1},{8,12},{9,13},{12,8},{13,9},{2,6},{3,7},{6... | collective-permute-start | bytes 196616 | tf_op jit(solution)/shard_map/ppermute | solution.py:376

commit v7 on v6

--- a/solution.py
+++ b/solution.py
@@ -129,12 +129,12 @@
 
 def send_kernel(par_ref, z_ref, ec_ref, eb_ref, ea_ref, *out_refs):
     (column,) = column_tiles(wanted_row(par_ref[0], [ea_ref, eb_ref, ec_ref]))
-    column = column.astype(I32)
-    lane = iota((LANES, LANES), 1)
+    slots = out_refs[0].shape[0]
+    column = column[: 3 * slots].astype(I32)
+    lane = iota((3 * slots, LANES), 1)
     tiles = range(z_ref.shape[0] // LANES)
     pick = jnp.concatenate([one_hot(column == lane + t * LANES) for t in tiles], axis=1)
     rows = matmul(pick, z_ref[...]).astype(BF16)
-    slots = out_refs[0].shape[0]
     for c, ref in enumerate(out_refs):
         ref[...] = rows[c * slots : (c + 1) * slots, :]
 
@@ -247,7 +247,8 @@
             place = slice(p * LANES, (p + 1) * LANES)
             y_ref[2 * at : 2 * at + LANES, place] = first.astype(BF16)
             y_ref[2 * at + LANES : 2 * at + 2 * LANES, place] = second.astype(BF16)
-    rows = matmul(spread_ref[spread_ref.shape[0] - LANES :, :], y_ref[...]).astype(BF16)
+    faces = spread_ref.shape[0] - LANES
+    rows = matmul(spread_ref[faces : faces + filled, :], y_ref[...]).astype(BF16)
     for c, ref in enumerate((ba_ref, bb_ref, bc_ref)):
         ref[...] = rows[c * slots : (c + 1) * slots, :]
 
@@ -316,8 +317,9 @@
     oa_ref, ob_ref, oc_ref, gathered_ref
 ):
     gather_back([ba_ref, bb_ref, bc_ref], gathered_ref)
-    rows = (rows_ref[...] + matmul(same_ref[...], gathered_ref[...])).astype(BF16)
-    send_rows(rows, request_scale_ref[...], block_ref, [oa_ref, ob_ref, oc_ref])
+    count = 3 * oa_ref.shape[0]
+    rows = rows_ref[:count, :] + matmul(same_ref[:count, :], gathered_ref[...])
+    send_rows(rows.astype(BF16), request_scale_ref[:count, :], block_ref, [oa_ref, ob_ref, oc_ref])
 
 
 def last_kernel(

time: 43.7 us -> 43.7 us (level)
  no operation moved by 1% of the time
where the time goes in v7:
time: 43.7 us; the launch traced here: 43.5 us
  starting transfers between devices  20.1 us (46%)
  Pallas kernels  15.1 us (35%)
  waiting for transfers between devices  6.9 us (16%)
  between operations  1.42 us (3%)
    ppermute x15, starting transfers between devices, exchange(): lax.ppermute(a, ('elem', 'sub'), p)  20.1 us
    pallas_call x10, Pallas kernels, call(): pl.pallas_call(kernel, out_shape=[jax.ShapeDtypeStruct(s, d) for s, d in...  15.1 us
    ppermute x15, waiting for transfers between devices, exchange(): lax.ppermute(a, ('elem', 'sub'), p)  6.9 us
  transfers between devices with their start and end apart: 15, of which 7 were waited for; matrix products, arithmetic and copies ran while one was open for 0% of the time, Pallas kernels for 18%

profile of v7, /device:TPU:0, one launch (start us, length us, event | category | flops | bytes accessed | tf_op | source)
XLA Modules:
  0.0 43.5 jit_solution(15102337053134257841)
XLA Ops:
  0.7 4.1 %collective-permute-start.2 = (s32[3,1,32]{2,1,0:T(1,128)}, s32[3,1,32]{2,1,0:T(1,128)S(1)}, u32[]{:S(2)}, u32[]{:S(2)}) collective-permute-start(s32[3,1,32]{2,1,0:T(1,128)} %bitcast.8), channel_id=1, source_target_pairs={{0,8},{1,9},{4,12},{5,13},{8,0},{9,1},{12,4},{13,5},{2,10},{3,11},... | collective-permute-start | bytes 1160 | tf_op jit(solution)/shard_map/ppermute | solution.py:378
  4.8 1.6 %collective-permute-start = (s32[3,1,32]{2,1,0:T(1,128)}, s32[3,1,32]{2,1,0:T(1,128)S(1)}, u32[]{:S(2)}, u32[]{:S(2)}) collective-permute-start(s32[3,1,32]{2,1,0:T(1,128)} %bitcast.10), channel_id=1, source_target_pairs={{0,4},{1,5},{4,0},{5,1},{8,12},{9,13},{12,8},{13,9},{2,6},{3,7},{6... | collective-permute-start | bytes 1160 | tf_op jit(solution)/shard_map/ppermute | solution.py:378
  6.3 1.6 %prepare.1 = (bf16[384,1024]{1,0:T(8,128)(2,1)S(1)}, bf16[256,256]{1,0:T(8,128)(2,1)S(1)}, f32[1,384]{1,0:T(1,128)S(1)}, f32[384,128]{1,0:T(8,128)S(1)}, bf16[384,768]{1,0:T(8,128)(2,1)S(1)}) custom-call(bf16[384,1024]{1,0:T(8,128)(2,1)} %rhs_hbm.1, bf16[64,64]{1,0:T(8,128)(2,1)} %jacobi_hbm.1, f32[384]{0:T(512)} %scale_hbm.1, bf16[384,384]{1,0:T(8,128)(2,1)} %stiff_hbm.1, ...), custom_call_target="tpu_custom_call" | custom-call | flops 201326592 | bytes 1385984 | tf_op jit(solution)/shard_map/prepare/pallas_call | solution.py:343
  8.0 0.6 %collective-permute-done.ec_ref = s32[3,1,32]{2,1,0:T(1,128)S(1)} collective-permute-done((s32[3,1,32]{2,1,0:T(1,128)}, s32[3,1,32]{2,1,0:T(1,128)S(1)}, u32[]{:S(2)}, u32[]{:S(2)}) %collective-permute-start) | collective-permute-done | bytes 416 | tf_op jit(solution)/shard_map/ppermute | solution.py:378
  8.6 0.4 send.1
  9.0 3.1 %collective-permute-start.3 = (bf16[32,1024]{1,0:T(8,128)(2,1)S(1)}, bf16[32,1024]{1,0:T(8,128)(2,1)S(1)}, u32[]{:S(2)}, u32[]{:S(2)}) collective-permute-start(bf16[32,1024]{1,0:T(8,128)(2,1)S(1)} %get-tuple-element.41), channel_id=1, source_target_pairs={{0,8},{1,9},{4,12},{5,13},{8,0},{9,1},{12,4},{13,5},{2,10},{3,11},... | collective-permute-start | bytes 196616 | tf_op jit(solution)/shard_map/ppermute | solution.py:378
  12.1 0.6 %collective-permute-start.5 = (bf16[32,1024]{1,0:T(8,128)(2,1)S(1)}, bf16[32,1024]{1,0:T(8,128)(2,1)S(1)}, u32[]{:S(2)}, u32[]{:S(2)}) collective-permute-start(bf16[32,1024]{1,0:T(8,128)(2,1)S(1)} %get-tuple-element.43), channel_id=1, source_target_pairs={{0,4},{1,5},{4,0},{5,1},{8,12},{9,13},{12,8},{13,9},{2,6},{3,7},{6... | collective-permute-start | bytes 196616 | tf_op jit(solution)/shard_map/ppermute | solution.py:378
  13.4 1.3 %gather1.1 = (bf16[2048,384]{1,0:T(8,128)(2,1)S(1)}, bf16[768,384]{1,0:T(8,128)(2,1)S(1)}, bf16[384,256]{1,0:T(8,128)(2,1)S(1)}, bf16[512,768]{1,0:T(8,128)(2,1)S(1)}, f32[2,128,128]{2,1,0:T(8,128)S(1)}) custom-call(s32[1]{0:T(128)} %bitcast.par_ref, s32[1]{0:T(128)S(6)} %copy.13.count_ref, bf16[384,1024]{1,0:T(8,128)(2,1)S(1)} %get-tuple-element.36.z_ref, ...), custom_call_target="tpu_custom_call" | custom-call | flops 603979776 | bytes 790536 | tf_op jit(solution)/shard_map/gather1/pallas_call | solution.py:343
  14.9 1.7 %collective-permute-done.5.ac_ref = bf16[32,1024]{1,0:T(8,128)(2,1)S(1)} collective-permute-done((bf16[32,1024]{1,0:T(8,128)(2,1)S(1)}, bf16[32,1024]{1,0:T(8,128)(2,1)S(1)}, u32[]{:S(2)}, u32[]{:S(2)}) %collective-permute-start.5) | collective-permute-done | bytes 65568 | tf_op jit(solution)/shard_map/ppermute | solution.py:378
  16.6 2.7 %operator1.1 = (bf16[768,1024]{1,0:T(8,128)(2,1)S(1)}, bf16[32,1024]{1,0:T(8,128)(2,1)S(1)}, bf16[32,1024]{1,0:T(8,128)(2,1)S(1)}, bf16[32,1024]{1,0:T(8,128)(2,1)S(1)}) custom-call(bf16[384,256]{1,0:T(8,128)(2,1)S(1)} %get-tuple-element.38.pick_ref, bf16[512,768]{1,0:T(8,128)(2,1)S(1)} %get-tuple-element.37.spread_ref, ...), custom_call_target="tpu_custom_call" | custom-call | flops 1207959552 | bytes 3473408 | tf_op jit(solution)/shard_map/operator1/pallas_call | solution.py:343
  19.3 1.3 %collective-permute-start.6 = (bf16[32,1024]{1,0:T(8,128)(2,1)S(1)}, bf16[32,1024]{1,0:T(8,128)(2,1)S(1)}, u32[]{:S(2)}, u32[]{:S(2)}) collective-permute-start(bf16[32,1024]{1,0:T(8,128)(2,1)S(1)} %get-tuple-element.49), channel_id=1, source_target_pairs={{0,8},{1,9},{4,12},{5,13},{8,0},{9,1},{12,4},{13,5},{2,10},{3,11},... | collective-permute-start | bytes 196616 | tf_op jit(solution)/shard_map/ppermute | solution.py:378
  20.6 2.2 %collective-permute-start.8 = (bf16[32,1024]{1,0:T(8,128)(2,1)S(1)}, bf16[32,1024]{1,0:T(8,128)(2,1)S(1)}, u32[]{:S(2)}, u32[]{:S(2)}) collective-permute-start(bf16[32,1024]{1,0:T(8,128)(2,1)S(1)} %get-tuple-element.51), channel_id=1, source_target_pairs={{0,4},{1,5},{4,0},{5,1},{8,12},{9,13},{12,8},{13,9},{2,6},{3,7},{6... | collective-permute-start | bytes 196616 | tf_op jit(solution)/shard_map/ppermute | solution.py:378
  22.8 1.2 %sums1.1 = (f32[384,1024]{1,0:T(8,128)S(1)}, f32[128,1024]{1,0:T(8,128)S(1)}, bf16[128,128]{1,0:T(8,128)(2,1)S(1)}, bf16[384,128]{1,0:T(8,128)(2,1)S(1)}, f32[128,128]{1,0:T(8,128)S(1)}) custom-call(s32[1]{0:T(128)} %bitcast.par_ref, bf16[512,768]{1,0:T(8,128)(2,1)S(1)} %get-tuple-element.37.spread_ref, bf16[768,1024]{1,0:T(8,128)(2,1)S(1)} %get-tuple-element.46.y_ref, ...), custom_call_target="tpu_custom_call" | custom-call | flops 603979776 | bytes 2361988 | tf_op jit(solution)/shard_map/sums1/pallas_call | solution.py:343
  24.1 1.9 %collective-permute-done.6.ba_ref = bf16[32,1024]{1,0:T(8,128)(2,1)S(1)} collective-permute-done((bf16[32,1024]{1,0:T(8,128)(2,1)S(1)}, bf16[32,1024]{1,0:T(8,128)(2,1)S(1)}, u32[]{:S(2)}, u32[]{:S(2)}) %collective-permute-start.6) | collective-permute-done | bytes 65568 | tf_op jit(solution)/shard_map/ppermute | solution.py:378
  26.4 1.2 %collective-permute-start.9 = (bf16[32,1024]{1,0:T(8,128)(2,1)S(1)}, bf16[32,1024]{1,0:T(8,128)(2,1)S(1)}, u32[]{:S(2)}, u32[]{:S(2)}) collective-permute-start(bf16[32,1024]{1,0:T(8,128)(2,1)S(1)} %get-tuple-element.59), channel_id=1, source_target_pairs={{0,8},{1,9},{4,12},{5,13},{8,0},{9,1},{12,4},{13,5},{2,10},{3,11},... | collective-permute-start | bytes 196616 | tf_op jit(solution)/shard_map/ppermute | solution.py:378
  27.6 2.3 %collective-permute-start.11 = (bf16[32,1024]{1,0:T(8,128)(2,1)S(1)}, bf16[32,1024]{1,0:T(8,128)(2,1)S(1)}, u32[]{:S(2)}, u32[]{:S(2)}) collective-permute-start(bf16[32,1024]{1,0:T(8,128)(2,1)S(1)} %get-tuple-element.61), channel_id=1, source_target_pairs={{0,4},{1,5},{4,0},{5,1},{8,12},{9,13},{12,8},{13,9},{2,6},{3,7},{6... | collective-permute-start | bytes 196616 | tf_op jit(solution)/shard_map/ppermute | solution.py:378
  29.9 1.6 %gather2.1 = (bf16[2048,384]{1,0:T(8,128)(2,1)S(1)}, bf16[384,512]{1,0:T(8,128)(2,1)S(1)}) custom-call(bf16[768,384]{1,0:T(8,128)(2,1)S(1)} %get-tuple-element.39.pick_ref, f32[384,1024]{1,0:T(8,128)S(1)} %get-tuple-element.48.sums_ref, bf16[32,1024]{1,0:T(8,128)(2,1)S(1)} %collective-permute-done.6.ba_ref, ...), custom_call_target="tpu_custom_call" | custom-call | flops 603979776 | bytes 3178496 | tf_op jit(solution)/shard_map/gather2/pallas_call | solution.py:343
  31.5 1.5 %collective-permute-done.9.aa_ref = bf16[32,1024]{1,0:T(8,128)(2,1)S(1)} collective-permute-done((bf16[32,1024]{1,0:T(8,128)(2,1)S(1)}, bf16[32,1024]{1,0:T(8,128)(2,1)S(1)}, u32[]{:S(2)}, u32[]{:S(2)}) %collective-permute-start.9) | collective-permute-done | bytes 65568 | tf_op jit(solution)/shard_map/ppermute | solution.py:378
  33.0 2.7 %operator2.1 = (bf16[768,1024]{1,0:T(8,128)(2,1)S(1)}, bf16[32,1024]{1,0:T(8,128)(2,1)S(1)}, bf16[32,1024]{1,0:T(8,128)(2,1)S(1)}, bf16[32,1024]{1,0:T(8,128)(2,1)S(1)}, bf16[2048,384]{1,0:T(8,128)(2,1)S(1)}) custom-call(bf16[384,256]{1,0:T(8,128)(2,1)S(1)} %get-tuple-element.38.pick_ref, bf16[512,768]{1,0:T(8,128)(2,1)S(1)} %get-tuple-element.37.spread_ref, ...), custom_call_target="tpu_custom_call" | custom-call | flops 1207959552 | bytes 3473408 | tf_op jit(solution)/shard_map/operator2/pallas_call | solution.py:343
  35.8 1.4 %collective-permute-start.12 = (bf16[32,1024]{1,0:T(8,128)(2,1)S(1)}, bf16[32,1024]{1,0:T(8,128)(2,1)S(1)}, u32[]{:S(2)}, u32[]{:S(2)}) collective-permute-start(bf16[32,1024]{1,0:T(8,128)(2,1)S(1)} %get-tuple-element.66), channel_id=1, source_target_pairs={{0,8},{1,9},{4,12},{5,13},{8,0},{9,1},{12,4},{13,5},{2,10},{3,11},... | collective-permute-start | bytes 196616 | tf_op jit(solution)/shard_map/ppermute | solution.py:378
  37.2 2.1 %collective-permute-start.14 = (bf16[32,1024]{1,0:T(8,128)(2,1)S(1)}, bf16[32,1024]{1,0:T(8,128)(2,1)S(1)}, u32[]{:S(2)}, u32[]{:S(2)}) collective-permute-start(bf16[32,1024]{1,0:T(8,128)(2,1)S(1)} %get-tuple-element.68), channel_id=1, source_target_pairs={{0,4},{1,5},{4,0},{5,1},{8,12},{9,13},{12,8},{13,9},{2,6},{3,7},{6... | collective-permute-start | bytes 196616 | tf_op jit(solution)/shard_map/ppermute | solution.py:378
  39.3 2.1 %finish.1 = (f32[384,1024]{1,0:T(8,128)S(1)}, bf16[128,8192]{1,0:T(8,128)(2,1)}) custom-call(bf16[512,768]{1,0:T(8,128)(2,1)S(1)} %get-tuple-element.37.spread_ref, bf16[768,1024]{1,0:T(8,128)(2,1)S(1)} %get-tuple-element.62.y_ref, bf16[2048,384]{1,0:T(8,128)(2,1)S(1)} %get-tuple-element.63.x_ref, bf16[384,512]{1,0:T(8,128)(2,1)S(1)} %get-tuple-element.64.lift_ref), custom_call_target="tpu_custom_call" | custom-call | flops 805306368 | bytes 4325376 | tf_op jit(solution)/shard_map/finish/pallas_call | solution.py:343
  41.4 1.0 %collective-permute-done.12.ba_ref = bf16[32,1024]{1,0:T(8,128)(2,1)S(1)} collective-permute-done((bf16[32,1024]{1,0:T(8,128)(2,1)S(1)}, bf16[32,1024]{1,0:T(8,128)(2,1)S(1)}, u32[]{:S(2)}, u32[]{:S(2)}) %collective-permute-start.12) | collective-permute-done | bytes 65568 | tf_op jit(solution)/shard_map/ppermute | solution.py:378
  42.4 1.1 %last.1 = bf16[384,1024]{1,0:T(8,128)(2,1)} custom-call(f32[384,1024]{1,0:T(8,128)S(1)} %get-tuple-element.65.own_ref, bf16[32,1024]{1,0:T(8,128)(2,1)S(1)} %collective-permute-done.12.ba_ref, bf16[32,1024]{1,0:T(8,128)(2,1)S(1)} %collective-permute-done.13.bb_ref, bf16[32,1024]{1,0:T(8,128)(2,1)S(1)} %collective-permute-done.14.bc_ref, ...), custom_call_target="tpu_custom_call" | custom-call | flops 100663296 | bytes 1867776 | tf_op jit(solution)/shard_map/last/pallas_call | solution.py:343
  (22 shorter events, 0.6 us)
Async XLA Ops:
  0.6 12.7 %copy-start = (s32[128,6]{0,1:T(8,128)S(1)}, s32[128,6]{0,1:T(8,128)}, u32[]{:S(2)}) copy-start(s32[128,6]{0,1:T(8,128)} %param.15) | copy-start | bytes 9220
  0.6 12.7 %copy-start.2 = (f32[128]{0:T(128)S(1)}, f32[128]{0:T(128)}, u32[]{:S(2)}) copy-start(f32[128]{0:T(128)} %param.14) | copy-start | bytes 1540
  0.7 12.7 %copy-start.1 = (f32[128]{0:T(128)S(1)}, f32[128]{0:T(128)}, u32[]{:S(2)}) copy-start(f32[128]{0:T(128)} %param.13) | copy-start | bytes 1540
  0.7 7.3 %collective-permute-start.2 = (s32[3,1,32]{2,1,0:T(1,128)}, s32[3,1,32]{2,1,0:T(1,128)S(1)}, u32[]{:S(2)}, u32[]{:S(2)}) collective-permute-start(s32[3,1,32]{2,1,0:T(1,128)} %bitcast.8), channel_id=1, source_target_pairs={{0,8},{1,9},{4,12},{5,13},{8,0},{9,1},{12,4},{13,5},{2,10},{3,11},... | collective-permute-start | bytes 1160 | tf_op jit(solution)/shard_map/ppermute | solution.py:378
  4.8 3.2 %collective-permute-start.1 = (s32[3,1,32]{2,1,0:T(1,128)}, s32[3,1,32]{2,1,0:T(1,128)S(1)}, u32[]{:S(2)}, u32[]{:S(2)}) collective-permute-start(s32[3,1,32]{2,1,0:T(1,128)} %bitcast.9), channel_id=1, source_target_pairs={{0,1},{1,0},{4,8},{5,9},{8,4},{9,5},{12,13},{13,12},{2,3},{3,2},{6... | collective-permute-start | bytes 1160 | tf_op jit(solution)/shard_map/ppermute | solution.py:378
  4.8 3.8 %collective-permute-start = (s32[3,1,32]{2,1,0:T(1,128)}, s32[3,1,32]{2,1,0:T(1,128)S(1)}, u32[]{:S(2)}, u32[]{:S(2)}) collective-permute-start(s32[3,1,32]{2,1,0:T(1,128)} %bitcast.10), channel_id=1, source_target_pairs={{0,4},{1,5},{4,0},{5,1},{8,12},{9,13},{12,8},{13,9},{2,6},{3,7},{6... | collective-permute-start | bytes 1160 | tf_op jit(solution)/shard_map/ppermute | solution.py:378
  9.0 5.9 %collective-permute-start.3 = (bf16[32,1024]{1,0:T(8,128)(2,1)S(1)}, bf16[32,1024]{1,0:T(8,128)(2,1)S(1)}, u32[]{:S(2)}, u32[]{:S(2)}) collective-permute-start(bf16[32,1024]{1,0:T(8,128)(2,1)S(1)} %get-tuple-element.41), channel_id=1, source_target_pairs={{0,8},{1,9},{4,12},{5,13},{8,0},{9,1},{12,4},{13,5},{2,10},{3,11},... | collective-permute-start | bytes 196616 | tf_op jit(solution)/shard_map/ppermute | solution.py:378
  12.1 2.8 %collective-permute-start.4 = (bf16[32,1024]{1,0:T(8,128)(2,1)S(1)}, bf16[32,1024]{1,0:T(8,128)(2,1)S(1)}, u32[]{:S(2)}, u32[]{:S(2)}) collective-permute-start(bf16[32,1024]{1,0:T(8,128)(2,1)S(1)} %get-tuple-element.42), channel_id=1, source_target_pairs={{0,1},{1,0},{4,8},{5,9},{8,4},{9,5},{12,13},{13,12},{2,3},{3,2},{6... | collective-permute-start | bytes 196616 | tf_op jit(solution)/shard_map/ppermute | solution.py:378
  12.1 4.5 %collective-permute-start.5 = (bf16[32,1024]{1,0:T(8,128)(2,1)S(1)}, bf16[32,1024]{1,0:T(8,128)(2,1)S(1)}, u32[]{:S(2)}, u32[]{:S(2)}) collective-permute-start(bf16[32,1024]{1,0:T(8,128)(2,1)S(1)} %get-tuple-element.43), channel_id=1, source_target_pairs={{0,4},{1,5},{4,0},{5,1},{8,12},{9,13},{12,8},{13,9},{2,6},{3,7},{6... | collective-permute-start | bytes 196616 | tf_op jit(solution)/shard_map/ppermute | solution.py:378
  19.3 6.7 %collective-permute-start.6 = (bf16[32,1024]{1,0:T(8,128)(2,1)S(1)}, bf16[32,1024]{1,0:T(8,128)(2,1)S(1)}, u32[]{:S(2)}, u32[]{:S(2)}) collective-permute-start(bf16[32,1024]{1,0:T(8,128)(2,1)S(1)} %get-tuple-element.49), channel_id=1, source_target_pairs={{0,8},{1,9},{4,12},{5,13},{8,0},{9,1},{12,4},{13,5},{2,10},{3,11},... | collective-permute-start | bytes 196616 | tf_op jit(solution)/shard_map/ppermute | solution.py:378
  20.6 5.3 %collective-permute-start.7 = (bf16[32,1024]{1,0:T(8,128)(2,1)S(1)}, bf16[32,1024]{1,0:T(8,128)(2,1)S(1)}, u32[]{:S(2)}, u32[]{:S(2)}) collective-permute-start(bf16[32,1024]{1,0:T(8,128)(2,1)S(1)} %get-tuple-element.50), channel_id=1, source_target_pairs={{0,1},{1,0},{4,8},{5,9},{8,4},{9,5},{12,13},{13,12},{2,3},{3,2},{6... | collective-permute-start | bytes 196616 | tf_op jit(solution)/shard_map/ppermute | solution.py:378
  20.6 5.4 %collective-permute-start.8 = (bf16[32,1024]{1,0:T(8,128)(2,1)S(1)}, bf16[32,1024]{1,0:T(8,128)(2,1)S(1)}, u32[]{:S(2)}, u32[]{:S(2)}) collective-permute-start(bf16[32,1024]{1,0:T(8,128)(2,1)S(1)} %get-tuple-element.51), channel_id=1, source_target_pairs={{0,4},{1,5},{4,0},{5,1},{8,12},{9,13},{12,8},{13,9},{2,6},{3,7},{6... | collective-permute-start | bytes 196616 | tf_op jit(solution)/shard_map/ppermute | solution.py:378
  26.4 6.7 %collective-permute-start.9 = (bf16[32,1024]{1,0:T(8,128)(2,1)S(1)}, bf16[32,1024]{1,0:T(8,128)(2,1)S(1)}, u32[]{:S(2)}, u32[]{:S(2)}) collective-permute-start(bf16[32,1024]{1,0:T(8,128)(2,1)S(1)} %get-tuple-element.59), channel_id=1, source_target_pairs={{0,8},{1,9},{4,12},{5,13},{8,0},{9,1},{12,4},{13,5},{2,10},{3,11},... | collective-permute-start | bytes 196616 | tf_op jit(solution)/shard_map/ppermute | solution.py:378
  27.6 5.4 %collective-permute-start.10 = (bf16[32,1024]{1,0:T(8,128)(2,1)S(1)}, bf16[32,1024]{1,0:T(8,128)(2,1)S(1)}, u32[]{:S(2)}, u32[]{:S(2)}) collective-permute-start(bf16[32,1024]{1,0:T(8,128)(2,1)S(1)} %get-tuple-element.60), channel_id=1, source_target_pairs={{0,1},{1,0},{4,8},{5,9},{8,4},{9,5},{12,13},{13,12},{2,3},{3,2},{6... | collective-permute-start | bytes 196616 | tf_op jit(solution)/shard_map/ppermute | solution.py:378
  27.6 5.4 %collective-permute-start.11 = (bf16[32,1024]{1,0:T(8,128)(2,1)S(1)}, bf16[32,1024]{1,0:T(8,128)(2,1)S(1)}, u32[]{:S(2)}, u32[]{:S(2)}) collective-permute-start(bf16[32,1024]{1,0:T(8,128)(2,1)S(1)} %get-tuple-element.61), channel_id=1, source_target_pairs={{0,4},{1,5},{4,0},{5,1},{8,12},{9,13},{12,8},{13,9},{2,6},{3,7},{6... | collective-permute-start | bytes 196616 | tf_op jit(solution)/shard_map/ppermute | solution.py:378
  35.8 6.6 %collective-permute-start.12 = (bf16[32,1024]{1,0:T(8,128)(2,1)S(1)}, bf16[32,1024]{1,0:T(8,128)(2,1)S(1)}, u32[]{:S(2)}, u32[]{:S(2)}) collective-permute-start(bf16[32,1024]{1,0:T(8,128)(2,1)S(1)} %get-tuple-element.66), channel_id=1, source_target_pairs={{0,8},{1,9},{4,12},{5,13},{8,0},{9,1},{12,4},{13,5},{2,10},{3,11},... | collective-permute-start | bytes 196616 | tf_op jit(solution)/shard_map/ppermute | solution.py:378
  37.2 5.2 %collective-permute-start.13 = (bf16[32,1024]{1,0:T(8,128)(2,1)S(1)}, bf16[32,1024]{1,0:T(8,128)(2,1)S(1)}, u32[]{:S(2)}, u32[]{:S(2)}) collective-permute-start(bf16[32,1024]{1,0:T(8,128)(2,1)S(1)} %get-tuple-element.67), channel_id=1, source_target_pairs={{0,1},{1,0},{4,8},{5,9},{8,4},{9,5},{12,13},{13,12},{2,3},{3,2},{6... | collective-permute-start | bytes 196616 | tf_op jit(solution)/shard_map/ppermute | solution.py:378
  37.2 5.2 %collective-permute-start.14 = (bf16[32,1024]{1,0:T(8,128)(2,1)S(1)}, bf16[32,1024]{1,0:T(8,128)(2,1)S(1)}, u32[]{:S(2)}, u32[]{:S(2)}) collective-permute-start(bf16[32,1024]{1,0:T(8,128)(2,1)S(1)} %get-tuple-element.68), channel_id=1, source_target_pairs={{0,4},{1,5},{4,0},{5,1},{8,12},{9,13},{12,8},{13,9},{2,6},{3,7},{6... | collective-permute-start | bytes 196616 | tf_op jit(solution)/shard_map/ppermute | solution.py:378

commit v8 on v6

--- a/solution.py
+++ b/solution.py
@@ -210,9 +210,9 @@
     slots, width = aa_ref.shape
     pairs = width // LANES
     filled = 3 * slots
-    arrived = jnp.concatenate([aa_ref[...], ab_ref[...], ac_ref[...]], axis=0).astype(F32)
+    arrived = jnp.concatenate([aa_ref[...], ab_ref[...], ac_ref[...]], axis=0)
     low = iota((filled, LANES), 1) < LANES // 2
-    zero = jnp.zeros((filled, LANES), F32)
+    zero = jnp.zeros((filled, LANES), BF16)
     for first in (0, LANES):
         halo_ref[first + filled : first + LANES, :] = jnp.zeros(
             (LANES - filled, halo_ref.shape[1]), BF16
@@ -222,10 +222,10 @@
         turned = pltpu.roll(tile, LANES // 2, 1)
         even = slice(2 * p * LANES, (2 * p + 1) * LANES)
         odd = slice((2 * p + 1) * LANES, (2 * p + 2) * LANES)
-        halo_ref[:filled, even] = jnp.where(low, tile, zero).astype(BF16)
-        halo_ref[LANES : LANES + filled, even] = jnp.where(low, zero, turned).astype(BF16)
-        halo_ref[:filled, odd] = jnp.where(low, turned, zero).astype(BF16)
-        halo_ref[LANES : LANES + filled, odd] = jnp.where(low, zero, tile).astype(BF16)
+        halo_ref[:filled, even] = jnp.where(low, tile, zero)
+        halo_ref[LANES : LANES + filled, even] = jnp.where(low, zero, turned)
+        halo_ref[:filled, odd] = jnp.where(low, turned, zero)
+        halo_ref[LANES : LANES + filled, odd] = jnp.where(low, zero, tile)
     for t in range(x_ref.shape[1] // LANES):
         rows = matmul(pick_ref[t * LANES : (t + 1) * LANES, :], halo_ref[...]).astype(BF16)
         for s in range(2 * pairs):

time: 43.7 us -> 43.7 us (level)
  no operation moved by 1% of the time
where the time goes in v8:
time: 43.7 us; the launch traced here: 43.5 us
  starting transfers between devices  20.1 us (46%)
  Pallas kernels  15.1 us (35%)
  waiting for transfers between devices  6.88 us (16%)
  between operations  1.44 us (3%)
    ppermute x15, starting transfers between devices, exchange(): lax.ppermute(a, ('elem', 'sub'), p)  20.1 us
    pallas_call x10, Pallas kernels, call(): pl.pallas_call(kernel, out_shape=[jax.ShapeDtypeStruct(s, d) for s, d in...  15.1 us
    ppermute x15, waiting for transfers between devices, exchange(): lax.ppermute(a, ('elem', 'sub'), p)  6.88 us
  transfers between devices with their start and end apart: 15, of which 7 were waited for; matrix products, arithmetic and copies ran while one was open for 0% of the time, Pallas kernels for 18%

profile of v8, /device:TPU:0, one launch (start us, length us, event | category | flops | bytes accessed | tf_op | source)
XLA Modules:
  0.0 43.5 jit_solution(16065116951347228165)
XLA Ops:
  0.7 4.1 %collective-permute-start.2 = (s32[3,1,32]{2,1,0:T(1,128)}, s32[3,1,32]{2,1,0:T(1,128)S(1)}, u32[]{:S(2)}, u32[]{:S(2)}) collective-permute-start(s32[3,1,32]{2,1,0:T(1,128)} %bitcast.8), channel_id=1, source_target_pairs={{0,8},{1,9},{4,12},{5,13},{8,0},{9,1},{12,4},{13,5},{2,10},{3,11},... | collective-permute-start | bytes 1160 | tf_op jit(solution)/shard_map/ppermute | solution.py:376
  4.8 1.6 %collective-permute-start = (s32[3,1,32]{2,1,0:T(1,128)}, s32[3,1,32]{2,1,0:T(1,128)S(1)}, u32[]{:S(2)}, u32[]{:S(2)}) collective-permute-start(s32[3,1,32]{2,1,0:T(1,128)} %bitcast.10), channel_id=1, source_target_pairs={{0,4},{1,5},{4,0},{5,1},{8,12},{9,13},{12,8},{13,9},{2,6},{3,7},{6... | collective-permute-start | bytes 1160 | tf_op jit(solution)/shard_map/ppermute | solution.py:376
  6.3 1.6 %prepare.1 = (bf16[384,1024]{1,0:T(8,128)(2,1)S(1)}, bf16[256,256]{1,0:T(8,128)(2,1)S(1)}, f32[1,384]{1,0:T(1,128)S(1)}, f32[384,128]{1,0:T(8,128)S(1)}, bf16[384,768]{1,0:T(8,128)(2,1)S(1)}) custom-call(bf16[384,1024]{1,0:T(8,128)(2,1)} %rhs_hbm.1, bf16[64,64]{1,0:T(8,128)(2,1)} %jacobi_hbm.1, f32[384]{0:T(512)} %scale_hbm.1, bf16[384,384]{1,0:T(8,128)(2,1)} %stiff_hbm.1, ...), custom_call_target="tpu_custom_call" | custom-call | flops 201326592 | bytes 1385984 | tf_op jit(solution)/shard_map/prepare/pallas_call | solution.py:341
  8.0 0.6 %collective-permute-done.ec_ref = s32[3,1,32]{2,1,0:T(1,128)S(1)} collective-permute-done((s32[3,1,32]{2,1,0:T(1,128)}, s32[3,1,32]{2,1,0:T(1,128)S(1)}, u32[]{:S(2)}, u32[]{:S(2)}) %collective-permute-start) | collective-permute-done | bytes 416 | tf_op jit(solution)/shard_map/ppermute | solution.py:376
  8.6 0.4 send.1
  9.0 3.1 %collective-permute-start.3 = (bf16[32,1024]{1,0:T(8,128)(2,1)S(1)}, bf16[32,1024]{1,0:T(8,128)(2,1)S(1)}, u32[]{:S(2)}, u32[]{:S(2)}) collective-permute-start(bf16[32,1024]{1,0:T(8,128)(2,1)S(1)} %get-tuple-element.41), channel_id=1, source_target_pairs={{0,8},{1,9},{4,12},{5,13},{8,0},{9,1},{12,4},{13,5},{2,10},{3,11},... | collective-permute-start | bytes 196616 | tf_op jit(solution)/shard_map/ppermute | solution.py:376
  12.1 0.6 %collective-permute-start.5 = (bf16[32,1024]{1,0:T(8,128)(2,1)S(1)}, bf16[32,1024]{1,0:T(8,128)(2,1)S(1)}, u32[]{:S(2)}, u32[]{:S(2)}) collective-permute-start(bf16[32,1024]{1,0:T(8,128)(2,1)S(1)} %get-tuple-element.43), channel_id=1, source_target_pairs={{0,4},{1,5},{4,0},{5,1},{8,12},{9,13},{12,8},{13,9},{2,6},{3,7},{6... | collective-permute-start | bytes 196616 | tf_op jit(solution)/shard_map/ppermute | solution.py:376
  13.4 1.3 %gather1.1 = (bf16[2048,384]{1,0:T(8,128)(2,1)S(1)}, bf16[768,384]{1,0:T(8,128)(2,1)S(1)}, bf16[384,256]{1,0:T(8,128)(2,1)S(1)}, bf16[512,768]{1,0:T(8,128)(2,1)S(1)}, f32[2,128,128]{2,1,0:T(8,128)S(1)}) custom-call(s32[1]{0:T(128)} %bitcast.par_ref, s32[1]{0:T(128)S(6)} %copy.13.count_ref, bf16[384,1024]{1,0:T(8,128)(2,1)S(1)} %get-tuple-element.36.z_ref, ...), custom_call_target="tpu_custom_call" | custom-call | flops 603979776 | bytes 790536 | tf_op jit(solution)/shard_map/gather1/pallas_call | solution.py:341
  14.9 1.7 %collective-permute-done.5.ac_ref = bf16[32,1024]{1,0:T(8,128)(2,1)S(1)} collective-permute-done((bf16[32,1024]{1,0:T(8,128)(2,1)S(1)}, bf16[32,1024]{1,0:T(8,128)(2,1)S(1)}, u32[]{:S(2)}, u32[]{:S(2)}) %collective-permute-start.5) | collective-permute-done | bytes 65568 | tf_op jit(solution)/shard_map/ppermute | solution.py:376
  16.6 2.7 %operator1.1 = (bf16[768,1024]{1,0:T(8,128)(2,1)S(1)}, bf16[32,1024]{1,0:T(8,128)(2,1)S(1)}, bf16[32,1024]{1,0:T(8,128)(2,1)S(1)}, bf16[32,1024]{1,0:T(8,128)(2,1)S(1)}) custom-call(bf16[384,256]{1,0:T(8,128)(2,1)S(1)} %get-tuple-element.38.pick_ref, bf16[512,768]{1,0:T(8,128)(2,1)S(1)} %get-tuple-element.37.spread_ref, ...), custom_call_target="tpu_custom_call" | custom-call | flops 1207959552 | bytes 3473408 | tf_op jit(solution)/shard_map/operator1/pallas_call | solution.py:341
  19.3 1.3 %collective-permute-start.6 = (bf16[32,1024]{1,0:T(8,128)(2,1)S(1)}, bf16[32,1024]{1,0:T(8,128)(2,1)S(1)}, u32[]{:S(2)}, u32[]{:S(2)}) collective-permute-start(bf16[32,1024]{1,0:T(8,128)(2,1)S(1)} %get-tuple-element.49), channel_id=1, source_target_pairs={{0,8},{1,9},{4,12},{5,13},{8,0},{9,1},{12,4},{13,5},{2,10},{3,11},... | collective-permute-start | bytes 196616 | tf_op jit(solution)/shard_map/ppermute | solution.py:376
  20.6 2.2 %collective-permute-start.8 = (bf16[32,1024]{1,0:T(8,128)(2,1)S(1)}, bf16[32,1024]{1,0:T(8,128)(2,1)S(1)}, u32[]{:S(2)}, u32[]{:S(2)}) collective-permute-start(bf16[32,1024]{1,0:T(8,128)(2,1)S(1)} %get-tuple-element.51), channel_id=1, source_target_pairs={{0,4},{1,5},{4,0},{5,1},{8,12},{9,13},{12,8},{13,9},{2,6},{3,7},{6... | collective-permute-start | bytes 196616 | tf_op jit(solution)/shard_map/ppermute | solution.py:376
  22.9 1.2 %sums1.1 = (f32[384,1024]{1,0:T(8,128)S(1)}, f32[128,1024]{1,0:T(8,128)S(1)}, bf16[128,128]{1,0:T(8,128)(2,1)S(1)}, bf16[384,128]{1,0:T(8,128)(2,1)S(1)}, f32[128,128]{1,0:T(8,128)S(1)}) custom-call(s32[1]{0:T(128)} %bitcast.par_ref, bf16[512,768]{1,0:T(8,128)(2,1)S(1)} %get-tuple-element.37.spread_ref, bf16[768,1024]{1,0:T(8,128)(2,1)S(1)} %get-tuple-element.46.y_ref, ...), custom_call_target="tpu_custom_call" | custom-call | flops 603979776 | bytes 2361988 | tf_op jit(solution)/shard_map/sums1/pallas_call | solution.py:341
  24.1 1.9 %collective-permute-done.6.ba_ref = bf16[32,1024]{1,0:T(8,128)(2,1)S(1)} collective-permute-done((bf16[32,1024]{1,0:T(8,128)(2,1)S(1)}, bf16[32,1024]{1,0:T(8,128)(2,1)S(1)}, u32[]{:S(2)}, u32[]{:S(2)}) %collective-permute-start.6) | collective-permute-done | bytes 65568 | tf_op jit(solution)/shard_map/ppermute | solution.py:376
  26.4 1.2 %collective-permute-start.9 = (bf16[32,1024]{1,0:T(8,128)(2,1)S(1)}, bf16[32,1024]{1,0:T(8,128)(2,1)S(1)}, u32[]{:S(2)}, u32[]{:S(2)}) collective-permute-start(bf16[32,1024]{1,0:T(8,128)(2,1)S(1)} %get-tuple-element.59), channel_id=1, source_target_pairs={{0,8},{1,9},{4,12},{5,13},{8,0},{9,1},{12,4},{13,5},{2,10},{3,11},... | collective-permute-start | bytes 196616 | tf_op jit(solution)/shard_map/ppermute | solution.py:376
  27.6 2.3 %collective-permute-start.11 = (bf16[32,1024]{1,0:T(8,128)(2,1)S(1)}, bf16[32,1024]{1,0:T(8,128)(2,1)S(1)}, u32[]{:S(2)}, u32[]{:S(2)}) collective-permute-start(bf16[32,1024]{1,0:T(8,128)(2,1)S(1)} %get-tuple-element.61), channel_id=1, source_target_pairs={{0,4},{1,5},{4,0},{5,1},{8,12},{9,13},{12,8},{13,9},{2,6},{3,7},{6... | collective-permute-start | bytes 196616 | tf_op jit(solution)/shard_map/ppermute | solution.py:376
  29.9 1.6 %gather2.1 = (bf16[2048,384]{1,0:T(8,128)(2,1)S(1)}, bf16[384,512]{1,0:T(8,128)(2,1)S(1)}) custom-call(bf16[768,384]{1,0:T(8,128)(2,1)S(1)} %get-tuple-element.39.pick_ref, f32[384,1024]{1,0:T(8,128)S(1)} %get-tuple-element.48.sums_ref, bf16[32,1024]{1,0:T(8,128)(2,1)S(1)} %collective-permute-done.6.ba_ref, ...), custom_call_target="tpu_custom_call" | custom-call | flops 603979776 | bytes 3178496 | tf_op jit(solution)/shard_map/gather2/pallas_call | solution.py:341
  31.5 1.5 %collective-permute-done.9.aa_ref = bf16[32,1024]{1,0:T(8,128)(2,1)S(1)} collective-permute-done((bf16[32,1024]{1,0:T(8,128)(2,1)S(1)}, bf16[32,1024]{1,0:T(8,128)(2,1)S(1)}, u32[]{:S(2)}, u32[]{:S(2)}) %collective-permute-start.9) | collective-permute-done | bytes 65568 | tf_op jit(solution)/shard_map/ppermute | solution.py:376
  33.0 2.7 %operator2.1 = (bf16[768,1024]{1,0:T(8,128)(2,1)S(1)}, bf16[32,1024]{1,0:T(8,128)(2,1)S(1)}, bf16[32,1024]{1,0:T(8,128)(2,1)S(1)}, bf16[32,1024]{1,0:T(8,128)(2,1)S(1)}, bf16[2048,384]{1,0:T(8,128)(2,1)S(1)}) custom-call(bf16[384,256]{1,0:T(8,128)(2,1)S(1)} %get-tuple-element.38.pick_ref, bf16[512,768]{1,0:T(8,128)(2,1)S(1)} %get-tuple-element.37.spread_ref, ...), custom_call_target="tpu_custom_call" | custom-call | flops 1207959552 | bytes 3473408 | tf_op jit(solution)/shard_map/operator2/pallas_call | solution.py:341
  35.8 1.4 %collective-permute-start.12 = (bf16[32,1024]{1,0:T(8,128)(2,1)S(1)}, bf16[32,1024]{1,0:T(8,128)(2,1)S(1)}, u32[]{:S(2)}, u32[]{:S(2)}) collective-permute-start(bf16[32,1024]{1,0:T(8,128)(2,1)S(1)} %get-tuple-element.66), channel_id=1, source_target_pairs={{0,8},{1,9},{4,12},{5,13},{8,0},{9,1},{12,4},{13,5},{2,10},{3,11},... | collective-permute-start | bytes 196616 | tf_op jit(solution)/shard_map/ppermute | solution.py:376
  37.2 2.1 %collective-permute-start.14 = (bf16[32,1024]{1,0:T(8,128)(2,1)S(1)}, bf16[32,1024]{1,0:T(8,128)(2,1)S(1)}, u32[]{:S(2)}, u32[]{:S(2)}) collective-permute-start(bf16[32,1024]{1,0:T(8,128)(2,1)S(1)} %get-tuple-element.68), channel_id=1, source_target_pairs={{0,4},{1,5},{4,0},{5,1},{8,12},{9,13},{12,8},{13,9},{2,6},{3,7},{6... | collective-permute-start | bytes 196616 | tf_op jit(solution)/shard_map/ppermute | solution.py:376
  39.3 2.1 %finish.1 = (f32[384,1024]{1,0:T(8,128)S(1)}, bf16[128,8192]{1,0:T(8,128)(2,1)}) custom-call(bf16[512,768]{1,0:T(8,128)(2,1)S(1)} %get-tuple-element.37.spread_ref, bf16[768,1024]{1,0:T(8,128)(2,1)S(1)} %get-tuple-element.62.y_ref, bf16[2048,384]{1,0:T(8,128)(2,1)S(1)} %get-tuple-element.63.x_ref, bf16[384,512]{1,0:T(8,128)(2,1)S(1)} %get-tuple-element.64.lift_ref), custom_call_target="tpu_custom_call" | custom-call | flops 805306368 | bytes 4325376 | tf_op jit(solution)/shard_map/finish/pallas_call | solution.py:341
  41.4 1.0 %collective-permute-done.12.ba_ref = bf16[32,1024]{1,0:T(8,128)(2,1)S(1)} collective-permute-done((bf16[32,1024]{1,0:T(8,128)(2,1)S(1)}, bf16[32,1024]{1,0:T(8,128)(2,1)S(1)}, u32[]{:S(2)}, u32[]{:S(2)}) %collective-permute-start.12) | collective-permute-done | bytes 65568 | tf_op jit(solution)/shard_map/ppermute | solution.py:376
  42.4 1.1 %last.1 = bf16[384,1024]{1,0:T(8,128)(2,1)} custom-call(f32[384,1024]{1,0:T(8,128)S(1)} %get-tuple-element.65.own_ref, bf16[32,1024]{1,0:T(8,128)(2,1)S(1)} %collective-permute-done.12.ba_ref, bf16[32,1024]{1,0:T(8,128)(2,1)S(1)} %collective-permute-done.13.bb_ref, bf16[32,1024]{1,0:T(8,128)(2,1)S(1)} %collective-permute-done.14.bc_ref, ...), custom_call_target="tpu_custom_call" | custom-call | flops 100663296 | bytes 1867776 | tf_op jit(solution)/shard_map/last/pallas_call | solution.py:341
  (22 shorter events, 0.6 us)
Async XLA Ops:
  0.6 12.7 %copy-start = (s32[128,6]{0,1:T(8,128)S(1)}, s32[128,6]{0,1:T(8,128)}, u32[]{:S(2)}) copy-start(s32[128,6]{0,1:T(8,128)} %param.15) | copy-start | bytes 9220
  0.6 12.7 %copy-start.2 = (f32[128]{0:T(128)S(1)}, f32[128]{0:T(128)}, u32[]{:S(2)}) copy-start(f32[128]{0:T(128)} %param.14) | copy-start | bytes 1540
  0.7 12.7 %copy-start.1 = (f32[128]{0:T(128)S(1)}, f32[128]{0:T(128)}, u32[]{:S(2)}) copy-start(f32[128]{0:T(128)} %param.13) | copy-start | bytes 1540
  0.7 7.3 %collective-permute-start.2 = (s32[3,1,32]{2,1,0:T(1,128)}, s32[3,1,32]{2,1,0:T(1,128)S(1)}, u32[]{:S(2)}, u32[]{:S(2)}) collective-permute-start(s32[3,1,32]{2,1,0:T(1,128)} %bitcast.8), channel_id=1, source_target_pairs={{0,8},{1,9},{4,12},{5,13},{8,0},{9,1},{12,4},{13,5},{2,10},{3,11},... | collective-permute-start | bytes 1160 | tf_op jit(solution)/shard_map/ppermute | solution.py:376
  4.8 3.2 %collective-permute-start.1 = (s32[3,1,32]{2,1,0:T(1,128)}, s32[3,1,32]{2,1,0:T(1,128)S(1)}, u32[]{:S(2)}, u32[]{:S(2)}) collective-permute-start(s32[3,1,32]{2,1,0:T(1,128)} %bitcast.9), channel_id=1, source_target_pairs={{0,1},{1,0},{4,8},{5,9},{8,4},{9,5},{12,13},{13,12},{2,3},{3,2},{6... | collective-permute-start | bytes 1160 | tf_op jit(solution)/shard_map/ppermute | solution.py:376
  4.8 3.8 %collective-permute-start = (s32[3,1,32]{2,1,0:T(1,128)}, s32[3,1,32]{2,1,0:T(1,128)S(1)}, u32[]{:S(2)}, u32[]{:S(2)}) collective-permute-start(s32[3,1,32]{2,1,0:T(1,128)} %bitcast.10), channel_id=1, source_target_pairs={{0,4},{1,5},{4,0},{5,1},{8,12},{9,13},{12,8},{13,9},{2,6},{3,7},{6... | collective-permute-start | bytes 1160 | tf_op jit(solution)/shard_map/ppermute | solution.py:376
  9.0 5.9 %collective-permute-start.3 = (bf16[32,1024]{1,0:T(8,128)(2,1)S(1)}, bf16[32,1024]{1,0:T(8,128)(2,1)S(1)}, u32[]{:S(2)}, u32[]{:S(2)}) collective-permute-start(bf16[32,1024]{1,0:T(8,128)(2,1)S(1)} %get-tuple-element.41), channel_id=1, source_target_pairs={{0,8},{1,9},{4,12},{5,13},{8,0},{9,1},{12,4},{13,5},{2,10},{3,11},... | collective-permute-start | bytes 196616 | tf_op jit(solution)/shard_map/ppermute | solution.py:376
  12.1 2.8 %collective-permute-start.4 = (bf16[32,1024]{1,0:T(8,128)(2,1)S(1)}, bf16[32,1024]{1,0:T(8,128)(2,1)S(1)}, u32[]{:S(2)}, u32[]{:S(2)}) collective-permute-start(bf16[32,1024]{1,0:T(8,128)(2,1)S(1)} %get-tuple-element.42), channel_id=1, source_target_pairs={{0,1},{1,0},{4,8},{5,9},{8,4},{9,5},{12,13},{13,12},{2,3},{3,2},{6... | collective-permute-start | bytes 196616 | tf_op jit(solution)/shard_map/ppermute | solution.py:376
  12.1 4.5 %collective-permute-start.5 = (bf16[32,1024]{1,0:T(8,128)(2,1)S(1)}, bf16[32,1024]{1,0:T(8,128)(2,1)S(1)}, u32[]{:S(2)}, u32[]{:S(2)}) collective-permute-start(bf16[32,1024]{1,0:T(8,128)(2,1)S(1)} %get-tuple-element.43), channel_id=1, source_target_pairs={{0,4},{1,5},{4,0},{5,1},{8,12},{9,13},{12,8},{13,9},{2,6},{3,7},{6... | collective-permute-start | bytes 196616 | tf_op jit(solution)/shard_map/ppermute | solution.py:376
  19.3 6.7 %collective-permute-start.6 = (bf16[32,1024]{1,0:T(8,128)(2,1)S(1)}, bf16[32,1024]{1,0:T(8,128)(2,1)S(1)}, u32[]{:S(2)}, u32[]{:S(2)}) collective-permute-start(bf16[32,1024]{1,0:T(8,128)(2,1)S(1)} %get-tuple-element.49), channel_id=1, source_target_pairs={{0,8},{1,9},{4,12},{5,13},{8,0},{9,1},{12,4},{13,5},{2,10},{3,11},... | collective-permute-start | bytes 196616 | tf_op jit(solution)/shard_map/ppermute | solution.py:376
  20.6 5.3 %collective-permute-start.7 = (bf16[32,1024]{1,0:T(8,128)(2,1)S(1)}, bf16[32,1024]{1,0:T(8,128)(2,1)S(1)}, u32[]{:S(2)}, u32[]{:S(2)}) collective-permute-start(bf16[32,1024]{1,0:T(8,128)(2,1)S(1)} %get-tuple-element.50), channel_id=1, source_target_pairs={{0,1},{1,0},{4,8},{5,9},{8,4},{9,5},{12,13},{13,12},{2,3},{3,2},{6... | collective-permute-start | bytes 196616 | tf_op jit(solution)/shard_map/ppermute | solution.py:376
  20.6 5.4 %collective-permute-start.8 = (bf16[32,1024]{1,0:T(8,128)(2,1)S(1)}, bf16[32,1024]{1,0:T(8,128)(2,1)S(1)}, u32[]{:S(2)}, u32[]{:S(2)}) collective-permute-start(bf16[32,1024]{1,0:T(8,128)(2,1)S(1)} %get-tuple-element.51), channel_id=1, source_target_pairs={{0,4},{1,5},{4,0},{5,1},{8,12},{9,13},{12,8},{13,9},{2,6},{3,7},{6... | collective-permute-start | bytes 196616 | tf_op jit(solution)/shard_map/ppermute | solution.py:376
  26.4 6.7 %collective-permute-start.9 = (bf16[32,1024]{1,0:T(8,128)(2,1)S(1)}, bf16[32,1024]{1,0:T(8,128)(2,1)S(1)}, u32[]{:S(2)}, u32[]{:S(2)}) collective-permute-start(bf16[32,1024]{1,0:T(8,128)(2,1)S(1)} %get-tuple-element.59), channel_id=1, source_target_pairs={{0,8},{1,9},{4,12},{5,13},{8,0},{9,1},{12,4},{13,5},{2,10},{3,11},... | collective-permute-start | bytes 196616 | tf_op jit(solution)/shard_map/ppermute | solution.py:376
  27.6 5.4 %collective-permute-start.10 = (bf16[32,1024]{1,0:T(8,128)(2,1)S(1)}, bf16[32,1024]{1,0:T(8,128)(2,1)S(1)}, u32[]{:S(2)}, u32[]{:S(2)}) collective-permute-start(bf16[32,1024]{1,0:T(8,128)(2,1)S(1)} %get-tuple-element.60), channel_id=1, source_target_pairs={{0,1},{1,0},{4,8},{5,9},{8,4},{9,5},{12,13},{13,12},{2,3},{3,2},{6... | collective-permute-start | bytes 196616 | tf_op jit(solution)/shard_map/ppermute | solution.py:376
  27.6 5.4 %collective-permute-start.11 = (bf16[32,1024]{1,0:T(8,128)(2,1)S(1)}, bf16[32,1024]{1,0:T(8,128)(2,1)S(1)}, u32[]{:S(2)}, u32[]{:S(2)}) collective-permute-start(bf16[32,1024]{1,0:T(8,128)(2,1)S(1)} %get-tuple-element.61), channel_id=1, source_target_pairs={{0,4},{1,5},{4,0},{5,1},{8,12},{9,13},{12,8},{13,9},{2,6},{3,7},{6... | collective-permute-start | bytes 196616 | tf_op jit(solution)/shard_map/ppermute | solution.py:376
  35.8 6.6 %collective-permute-start.12 = (bf16[32,1024]{1,0:T(8,128)(2,1)S(1)}, bf16[32,1024]{1,0:T(8,128)(2,1)S(1)}, u32[]{:S(2)}, u32[]{:S(2)}) collective-permute-start(bf16[32,1024]{1,0:T(8,128)(2,1)S(1)} %get-tuple-element.66), channel_id=1, source_target_pairs={{0,8},{1,9},{4,12},{5,13},{8,0},{9,1},{12,4},{13,5},{2,10},{3,11},... | collective-permute-start | bytes 196616 | tf_op jit(solution)/shard_map/ppermute | solution.py:376
  37.2 5.2 %collective-permute-start.13 = (bf16[32,1024]{1,0:T(8,128)(2,1)S(1)}, bf16[32,1024]{1,0:T(8,128)(2,1)S(1)}, u32[]{:S(2)}, u32[]{:S(2)}) collective-permute-start(bf16[32,1024]{1,0:T(8,128)(2,1)S(1)} %get-tuple-element.67), channel_id=1, source_target_pairs={{0,1},{1,0},{4,8},{5,9},{8,4},{9,5},{12,13},{13,12},{2,3},{3,2},{6... | collective-permute-start | bytes 196616 | tf_op jit(solution)/shard_map/ppermute | solution.py:376
  37.2 5.2 %collective-permute-start.14 = (bf16[32,1024]{1,0:T(8,128)(2,1)S(1)}, bf16[32,1024]{1,0:T(8,128)(2,1)S(1)}, u32[]{:S(2)}, u32[]{:S(2)}) collective-permute-start(bf16[32,1024]{1,0:T(8,128)(2,1)S(1)} %get-tuple-element.68), channel_id=1, source_target_pairs={{0,4},{1,5},{4,0},{5,1},{8,12},{9,13},{12,8},{13,9},{2,6},{3,7},{6... | collective-permute-start | bytes 196616 | tf_op jit(solution)/shard_map/ppermute | solution.py:376
